TPU v7x, 512 devices: a whole 4x4x16 slice. The times are simulated.
512 devices in a mesh: tx: 8 (over x, core), ty: 16 (over z), tz: 4 (over y).
Axes of the slice: x: 4, y: 4, z: 16, core: 2. Of those that a mesh axis runs over, the one named last changes fastest.
Arguments:
- start_block: float32 [64, 1048576], P(None, ('tx', 'ty', 'tz'))
- weights: bfloat16 [8192, 6, 128, 128], P(('tx', 'ty', 'tz')), may hold values from 0 to 0.25, as said below
- neighbours: int32 [8192, 6], P(('tx', 'ty', 'tz')), may hold values from 0 to 123, as said below
- boundary: int32 [2048], P(('tx', 'ty', 'tz')), may hold values from 0 to 15, as said below
Outputs:
- basis: float32 [64, 1048576], P(None, ('tx', 'ty', 'tz'))
- rfactor: float32 [64, 64], replicated
Inputs may be any that keep to these rules, and one draw needn't show every extreme that they name: `neighbours`: slot 0 of block row b is b % 16; in the last of each device's 16 rows slot 1 is 123. `boundary`: each device's 4 entries are distinct, the last of them 16 - 1. For each block row b and point p, exactly 16 of the entries weights[b, s, q, p] over all slots s and rows q are nonzero, each positive.
All inputs are finite; a program needn't handle non-finite values.
Results may differ from a plain program's by a relative error of at most 0.00075.
Values may be sent and summed in bfloat16 or wider, within the bound.
No kernel may reach another device: no remote copies, remote signals or barrier semaphores. Data moves between devices by JAX's collectives and lax.ppermute only.
A program may use at most 64 MiB of HBM per device.

v0:
```python
import jax
import jax.numpy as jnp
from jax import lax
from jax.sharding import PartitionSpec as P


def extended(block, sides, width):
    for axis, dim in sides:
        count = lax.axis_size(axis)
        forward = [(i, i + 1) for i in range(count - 1)]
        backward = [(target, source) for source, target in forward]
        low = lax.ppermute(
            lax.slice_in_dim(block, block.shape[dim] - width, None, axis=dim), axis, forward
        )
        high = lax.ppermute(lax.slice_in_dim(block, 0, width, axis=dim), axis, backward)
        block = jnp.concatenate([low, block, high], axis=dim)
    return block


def take_edges(grid, boundary):
    return jnp.take(grid, boundary, axis=1)[:, None, None, None]


def boundary_halo(edge_part):
    return extended(edge_part, (("tx", 1), ("ty", 2), ("tz", 3)), 1)


def as_pool(haloed):
    return haloed.reshape(haloed.shape[0], -1, haloed.shape[-1])


def apply_operator(current, own_grid, far_grid, degree, weights, neighbours):
    pool_grid = jnp.concatenate([own_grid, far_grid], axis=1)
    picked = jnp.take(pool_grid, neighbours, axis=1)
    product = jnp.einsum("kisq,isqp->kip", picked, weights, preferred_element_type=jnp.float32)
    return current * (1.0 - degree * 0.125) + product.reshape(current.shape) * 0.125


def lower_factor(mixed):
    local_gram = jnp.dot(
        mixed, mixed.T, precision=lax.Precision.HIGHEST, preferred_element_type=jnp.float32
    )
    total = lax.psum(local_gram, ("tx", "ty", "tz"))
    return jnp.linalg.cholesky(total)


def solve_lower(lower, values):
    return lax.linalg.triangular_solve(lower, values, left_side=True, lower=True)


def per_device(start_block, weights, neighbours, boundary):
    width, points = start_block.shape
    block_size = weights.shape[-1]
    blocks = points // block_size
    devices = lax.axis_size("tx") * lax.axis_size("ty") * lax.axis_size("tz")
    root_scale = float(points * devices) ** 0.5
    degree = jnp.sum(weights, axis=(1, 2), dtype=jnp.float32).reshape(points)
    own_grid = start_block.astype(jnp.bfloat16).reshape(width, blocks, block_size)
    far_grid = as_pool(boundary_halo(take_edges(own_grid, boundary)))
    mixed = apply_operator(start_block, own_grid, far_grid, degree, weights, neighbours)
    lower = lower_factor(mixed)
    current = solve_lower(lower, mixed) * root_scale
    own_grid = current.astype(jnp.bfloat16).reshape(width, blocks, block_size)
    far_grid = as_pool(boundary_halo(take_edges(own_grid, boundary)))
    mixed = apply_operator(current, own_grid, far_grid, degree, weights, neighbours)
    lower = lower_factor(mixed)
    basis = solve_lower(lower, mixed) * root_scale
    return (basis, lower.T / root_scale)


def solution(mesh):
    placed = (
        P(None, ("tx", "ty", "tz")),
        P(("tx", "ty", "tz"), None, None, None),
        P(("tx", "ty", "tz"), None),
        P(("tx", "ty", "tz")),
    )
    return jax.shard_map(
        per_device,
        mesh=mesh,
        in_specs=placed,
        out_specs=(P(None, ("tx", "ty", "tz")), P()),
        check_vma=False,
    )
```

profile of v0, /device:TPU:1, one launch (start us, length us, event | category | flops | bytes accessed | tf_op | source)
XLA Modules:
  0.0 328.7 jit_solution(997474695390738293)
XLA Ops:
  0.6 0.7 compare_and_fusion.1
  1.3 0.7 compare_select_fusion.1
  2.0 1.1 copy_bitcast_fusion.1
  3.1 0.6 gather_fusion
  3.7 8.8 %collective-permute-start.1 = (bf16[64,1,1,1,4,128]{5,0,4,3,2,1:T(8,128)(2,1)S(1)}, bf16[64,1,1,1,4,128]{5,0,4,3,2,1:T(8,128)(2,1)S(1)}, u32[]{:S(2)}, u32[]{:S(2)}) collective-permute-start(bf16[64,1,1,1,4,128]{5,0,4,3,2,1:T(8,128)(2,1)S(1)} %select_bitcast_fusion.1), channel_id=1, source_target_pairs={{64,0},{128,64},{192,128},{256,192},{320,256},{384,320},{448,384},... | collective-permute-start | bytes 196616 | tf_op jit(solution)/shard_map/ppermute | solution.py:15
  12.5 1.9 collective-permute-start
  14.4 0.7 compare_and_fusion
  15.8 1.3 collective-permute-start.3
  17.1 4.0 %collective-permute-start.2 = (bf16[64,3,1,1,4,128]{5,0,4,3,2,1:T(8,128)(2,1)S(1)}, bf16[64,3,1,1,4,128]{5,0,4,3,2,1:T(8,128)(2,1)S(1)}, u32[]{:S(2)}, u32[]{:S(2)}) collective-permute-start(bf16[64,3,1,1,4,128]{5,0,4,3,2,1:T(8,128)(2,1)S(1)} %pad_maximum_fusion.6), channel_id=1, source_target_pairs={{0,4},{4,8},{8,12},{12,16},{16,20},{20,24},{24,28},{28,32},{32,36}... | collective-permute-start | bytes 589832 | tf_op jit(solution)/shard_map/ppermute | solution.py:12
  21.1 0.7 compare_select_fusion
  21.9 2.2 collective-permute-done.3
  24.1 0.9 collective-permute-done.2
  25.0 1.3 collective-permute-start.5
  26.3 4.0 %collective-permute-start.4 = (bf16[64,3,3,1,4,128]{5,0,4,3,2,1:T(8,128)(2,1)S(1)}, bf16[64,3,3,1,4,128]{5,0,4,3,2,1:T(8,128)(2,1)S(1)}, u32[]{:S(2)}, u32[]{:S(2)}) collective-permute-start(bf16[64,3,3,1,4,128]{5,0,4,3,2,1:T(8,128)(2,1)S(1)} %pad_maximum_fusion.4), channel_id=1, source_target_pairs={{0,1},{1,2},{2,3},{4,5},{5,6},{6,7},{8,9},{9,10},{10,11},{12,13},{... | collective-permute-start | bytes 1769480 | tf_op jit(solution)/shard_map/ppermute | solution.py:12
  30.4 2.4 convert_reduce_fusion
  32.8 7.8 %collective-permute-done.5 = bf16[64,3,3,1,4,128]{5,0,4,3,2,1:T(8,128)(2,1)S(1)} collective-permute-done((bf16[64,3,3,1,4,128]{5,0,4,3,2,1:T(8,128)(2,1)S(1)}, bf16[64,3,3,1,4,128]{5,0,4,3,2,1:T(8,128)(2,1)S(1)}, u32[]{:S(2)}, u32[]{:S(2)}) %collective-permute-start.5) | collective-permute-done | bytes 589856 | tf_op jit(solution)/shard_map/ppermute | solution.py:15
  40.6 0.9 collective-permute-done.4
  41.9 2.0 gather_fusion.1
  43.9 3.2 fusion.23
  47.0 0.6 fusion.30
  47.6 108.8 %psum.14 = f32[64,64]{0,1:T(8,128)S(1)} all-reduce(f32[64,64]{0,1:T(8,128)S(1)} %fusion.30), channel_id=1, replica_groups=mesh['tx'=8,'ty'=16,'tz'=4] {'tx','ty','tz'}, use_global_device_ids=true, to_apply=%region_1.4 | all-reduce | flops 4096 | bytes 32768 | tf_op jit(solution)/shard_map/psum | solution.py:43
  156.5 5.8 %cholesky.44 = f32[64,64]{1,0:T(8,128)S(1)} custom-call(f32[64,64]{1,0:T(8,128)S(1)} %fusion.36), custom_call_target="Cholesky" | custom-call | tf_op jit(solution)/shard_map/jit(cholesky)/cholesky | solution.py:44
  162.4 0.6 compare_reduce_fusion.1
  163.1 0.7 fusion.32
  163.7 4.9 %custom-call.6 = f32[1,64,64]{1,2,0:T(8,128)S(1)} custom-call(f32[1,64,64]{2,1,0:T(8,128)S(1)} %fusion.32), custom_call_target="InvertDiagBlocksLowerTriangular" | custom-call | tf_op jit(solution)/shard_map/triangular_solve/custom-call.0 | solution.py:48
  168.6 0.6 fusion.29
  169.3 0.6 gather_fusion.2
  170.0 2.6 collective-permute-start.7
  172.6 3.0 collective-permute-start.6
  175.6 1.3 collective-permute-done.6
  176.9 1.3 collective-permute-start.9
  178.2 4.3 %collective-permute-start.8 = (bf16[64,3,1,1,4,128]{5,0,4,3,2,1:T(8,128)(2,1)S(1)}, bf16[64,3,1,1,4,128]{5,0,4,3,2,1:T(8,128)(2,1)S(1)}, u32[]{:S(2)}, u32[]{:S(2)}) collective-permute-start(bf16[64,3,1,1,4,128]{5,0,4,3,2,1:T(8,128)(2,1)S(1)} %pad_maximum_fusion.7), channel_id=1, source_target_pairs={{0,4},{4,8},{8,12},{12,16},{16,20},{20,24},{24,28},{28,32},{32,36}... | collective-permute-start | bytes 589832 | tf_op jit(solution)/shard_map/ppermute | solution.py:12
  182.4 2.4 collective-permute-done.9
  184.9 1.8 collective-permute-done.8
  186.7 1.3 collective-permute-start.11
  188.0 4.0 %collective-permute-start.10 = (bf16[64,3,3,1,4,128]{5,0,4,3,2,1:T(8,128)(2,1)S(1)}, bf16[64,3,3,1,4,128]{5,0,4,3,2,1:T(8,128)(2,1)S(1)}, u32[]{:S(2)}, u32[]{:S(2)}) collective-permute-start(bf16[64,3,3,1,4,128]{5,0,4,3,2,1:T(8,128)(2,1)S(1)} %pad_maximum_fusion.5), channel_id=1, source_target_pairs={{0,1},{1,2},{2,3},{4,5},{5,6},{6,7},{8,9},{9,10},{10,11},{12,13},{... | collective-permute-start | bytes 1769480 | tf_op jit(solution)/shard_map/ppermute | solution.py:12
  192.0 11.6 %collective-permute-done.11 = bf16[64,3,3,1,4,128]{5,0,4,3,2,1:T(8,128)(2,1)S(1)} collective-permute-done((bf16[64,3,3,1,4,128]{5,0,4,3,2,1:T(8,128)(2,1)S(1)}, bf16[64,3,3,1,4,128]{5,0,4,3,2,1:T(8,128)(2,1)S(1)}, u32[]{:S(2)}, u32[]{:S(2)}) %collective-permute-start.11) | collective-permute-done | bytes 589856 | tf_op jit(solution)/shard_map/ppermute | solution.py:15
  203.6 0.9 collective-permute-done.10
  204.9 2.0 gather_fusion.3
  206.9 3.1 fusion.17
  210.0 0.6 fusion.31
  210.5 103.8 %psum.15 = f32[64,64]{0,1:T(8,128)S(1)} all-reduce(f32[64,64]{0,1:T(8,128)S(1)} %fusion.31), channel_id=1, replica_groups=mesh['tx'=8,'ty'=16,'tz'=4] {'tx','ty','tz'}, use_global_device_ids=true, to_apply=%region_4.9 | all-reduce | flops 4096 | bytes 32768 | tf_op jit(solution)/shard_map/psum | solution.py:43
  314.5 5.8 %cholesky.55 = f32[64,64]{1,0:T(8,128)S(1)} custom-call(f32[64,64]{1,0:T(8,128)S(1)} %fusion.34), custom_call_target="Cholesky" | custom-call | tf_op jit(solution)/shard_map/jit(cholesky)/cholesky | solution.py:44
  320.4 0.6 compare_reduce_fusion
  321.0 0.7 multiply_bitcast_fusion
  321.7 0.7 copy.42
  322.4 4.9 %custom-call.7 = f32[1,64,64]{1,2,0:T(8,128)S(1)} custom-call(f32[1,64,64]{2,1,0:T(8,128)S(1)} %get-tuple-element.13), custom_call_target="InvertDiagBlocksLowerTriangular" | custom-call | tf_op jit(solution)/shard_map/triangular_solve/custom-call.0 | solution.py:48
  327.3 1.4 convolution_multiply_fusion
  (29 shorter events, 2.3 us)
Async XLA Ops:
  3.7 11.5 %collective-permute-start.1 = (bf16[64,1,1,1,4,128]{5,0,4,3,2,1:T(8,128)(2,1)S(1)}, bf16[64,1,1,1,4,128]{5,0,4,3,2,1:T(8,128)(2,1)S(1)}, u32[]{:S(2)}, u32[]{:S(2)}) collective-permute-start(bf16[64,1,1,1,4,128]{5,0,4,3,2,1:T(8,128)(2,1)S(1)} %select_bitcast_fusion.1), channel_id=1, source_target_pairs={{64,0},{128,64},{192,128},{256,192},{320,256},{384,320},{448,384},... | collective-permute-start | bytes 196616 | tf_op jit(solution)/shard_map/ppermute | solution.py:15
  12.5 3.2 collective-permute-start
  15.8 8.3 %collective-permute-start.3 = (bf16[64,3,1,1,4,128]{5,0,4,3,2,1:T(8,128)(2,1)S(1)}, bf16[64,3,1,1,4,128]{5,0,4,3,2,1:T(8,128)(2,1)S(1)}, u32[]{:S(2)}, u32[]{:S(2)}) collective-permute-start(bf16[64,3,1,1,4,128]{5,0,4,3,2,1:T(8,128)(2,1)S(1)} %pad_maximum_fusion.6), channel_id=1, source_target_pairs={{4,0},{8,4},{12,8},{16,12},{20,16},{24,20},{28,24},{32,28},{36,32}... | collective-permute-start | bytes 589832 | tf_op jit(solution)/shard_map/ppermute | solution.py:15
  17.1 7.9 %collective-permute-start.2 = (bf16[64,3,1,1,4,128]{5,0,4,3,2,1:T(8,128)(2,1)S(1)}, bf16[64,3,1,1,4,128]{5,0,4,3,2,1:T(8,128)(2,1)S(1)}, u32[]{:S(2)}, u32[]{:S(2)}) collective-permute-start(bf16[64,3,1,1,4,128]{5,0,4,3,2,1:T(8,128)(2,1)S(1)} %pad_maximum_fusion.6), channel_id=1, source_target_pairs={{0,4},{4,8},{8,12},{12,16},{16,20},{20,24},{24,28},{28,32},{32,36}... | collective-permute-start | bytes 589832 | tf_op jit(solution)/shard_map/ppermute | solution.py:12
  25.0 15.5 %collective-permute-start.5 = (bf16[64,3,3,1,4,128]{5,0,4,3,2,1:T(8,128)(2,1)S(1)}, bf16[64,3,3,1,4,128]{5,0,4,3,2,1:T(8,128)(2,1)S(1)}, u32[]{:S(2)}, u32[]{:S(2)}) collective-permute-start(bf16[64,3,3,1,4,128]{5,0,4,3,2,1:T(8,128)(2,1)S(1)} %pad_maximum_fusion.4), channel_id=1, source_target_pairs={{1,0},{2,1},{3,2},{5,4},{6,5},{7,6},{9,8},{10,9},{11,10},{13,12},{... | collective-permute-start | bytes 1769480 | tf_op jit(solution)/shard_map/ppermute | solution.py:15
  26.3 15.1 %collective-permute-start.4 = (bf16[64,3,3,1,4,128]{5,0,4,3,2,1:T(8,128)(2,1)S(1)}, bf16[64,3,3,1,4,128]{5,0,4,3,2,1:T(8,128)(2,1)S(1)}, u32[]{:S(2)}, u32[]{:S(2)}) collective-permute-start(bf16[64,3,3,1,4,128]{5,0,4,3,2,1:T(8,128)(2,1)S(1)} %pad_maximum_fusion.4), channel_id=1, source_target_pairs={{0,1},{1,2},{2,3},{4,5},{5,6},{6,7},{8,9},{9,10},{10,11},{12,13},{... | collective-permute-start | bytes 1769480 | tf_op jit(solution)/shard_map/ppermute | solution.py:12
  43.9 3.2 copy-start
  170.0 5.6 %collective-permute-start.7 = (bf16[64,1,1,1,4,128]{5,0,4,3,2,1:T(8,128)(2,1)S(1)}, bf16[64,1,1,1,4,128]{5,0,4,3,2,1:T(8,128)(2,1)S(1)}, u32[]{:S(2)}, u32[]{:S(2)}) collective-permute-start(bf16[64,1,1,1,4,128]{5,0,4,3,2,1:T(8,128)(2,1)S(1)} %select_bitcast_fusion), channel_id=1, source_target_pairs={{64,0},{128,64},{192,128},{256,192},{320,256},{384,320},{448,384},... | collective-permute-start | bytes 196616 | tf_op jit(solution)/shard_map/ppermute | solution.py:15
  172.6 4.3 %collective-permute-start.6 = (bf16[64,1,1,1,4,128]{5,0,4,3,2,1:T(8,128)(2,1)S(1)}, bf16[64,1,1,1,4,128]{5,0,4,3,2,1:T(8,128)(2,1)S(1)}, u32[]{:S(2)}, u32[]{:S(2)}) collective-permute-start(bf16[64,1,1,1,4,128]{5,0,4,3,2,1:T(8,128)(2,1)S(1)} %select_bitcast_fusion), channel_id=1, source_target_pairs={{0,64},{64,128},{128,192},{192,256},{256,320},{320,384},{384,448},... | collective-permute-start | bytes 196616 | tf_op jit(solution)/shard_map/ppermute | solution.py:12
  176.9 8.0 %collective-permute-start.9 = (bf16[64,3,1,1,4,128]{5,0,4,3,2,1:T(8,128)(2,1)S(1)}, bf16[64,3,1,1,4,128]{5,0,4,3,2,1:T(8,128)(2,1)S(1)}, u32[]{:S(2)}, u32[]{:S(2)}) collective-permute-start(bf16[64,3,1,1,4,128]{5,0,4,3,2,1:T(8,128)(2,1)S(1)} %pad_maximum_fusion.7), channel_id=1, source_target_pairs={{4,0},{8,4},{12,8},{16,12},{20,16},{24,20},{28,24},{32,28},{36,32}... | collective-permute-start | bytes 589832 | tf_op jit(solution)/shard_map/ppermute | solution.py:15
  178.2 8.4 %collective-permute-start.8 = (bf16[64,3,1,1,4,128]{5,0,4,3,2,1:T(8,128)(2,1)S(1)}, bf16[64,3,1,1,4,128]{5,0,4,3,2,1:T(8,128)(2,1)S(1)}, u32[]{:S(2)}, u32[]{:S(2)}) collective-permute-start(bf16[64,3,1,1,4,128]{5,0,4,3,2,1:T(8,128)(2,1)S(1)} %pad_maximum_fusion.7), channel_id=1, source_target_pairs={{0,4},{4,8},{8,12},{12,16},{16,20},{20,24},{24,28},{28,32},{32,36}... | collective-permute-start | bytes 589832 | tf_op jit(solution)/shard_map/ppermute | solution.py:12
  186.7 16.9 %collective-permute-start.11 = (bf16[64,3,3,1,4,128]{5,0,4,3,2,1:T(8,128)(2,1)S(1)}, bf16[64,3,3,1,4,128]{5,0,4,3,2,1:T(8,128)(2,1)S(1)}, u32[]{:S(2)}, u32[]{:S(2)}) collective-permute-start(bf16[64,3,3,1,4,128]{5,0,4,3,2,1:T(8,128)(2,1)S(1)} %pad_maximum_fusion.5), channel_id=1, source_target_pairs={{1,0},{2,1},{3,2},{5,4},{6,5},{7,6},{9,8},{10,9},{11,10},{13,12},{... | collective-permute-start | bytes 1769480 | tf_op jit(solution)/shard_map/ppermute | solution.py:15
  188.0 16.5 %collective-permute-start.10 = (bf16[64,3,3,1,4,128]{5,0,4,3,2,1:T(8,128)(2,1)S(1)}, bf16[64,3,3,1,4,128]{5,0,4,3,2,1:T(8,128)(2,1)S(1)}, u32[]{:S(2)}, u32[]{:S(2)}) collective-permute-start(bf16[64,3,3,1,4,128]{5,0,4,3,2,1:T(8,128)(2,1)S(1)} %pad_maximum_fusion.5), channel_id=1, source_target_pairs={{0,1},{1,2},{2,3},{4,5},{5,6},{6,7},{8,9},{9,10},{10,11},{12,13},{... | collective-permute-start | bytes 1769480 | tf_op jit(solution)/shard_map/ppermute | solution.py:12
where the time goes:
time: 330 us; the launch traced here: 329 us
  blocking collectives  213 us (65%)
  starting transfers between devices  37.7 us (11%)
  other arithmetic  31.6 us (10%)
  waiting for transfers between devices  30.1 us (9%)
  matrix products  9.49 us (3%)
  local copies, waits for them, and re-layouts  6.16 us (2%)
    psum x2, blocking collectives, lower_factor(): total = lax.psum(local_gram, ('tx', 'ty', 'tz'))  213 us
    ppermute x6, waiting for transfers between devices, extended(): lax.ppermute(lax.slice_in_dim(block, 0, width, axis=dim), axis, backward)  23.9 us
    ppermute x6, starting transfers between devices, extended(): lax.ppermute(lax.slice_in_dim(block, block.shape[dim] - width, None, axis...  21.2 us
    ppermute x6, starting transfers between devices, extended(): lax.ppermute(lax.slice_in_dim(block, 0, width, axis=dim), axis, backward)  16.5 us
    another operation x6, other arithmetic, lower_factor(): return jnp.linalg.cholesky(total)  13 us
    another operation x3, other arithmetic, solve_lower(): lax.linalg.triangular_solve(lower, values, left_side=True, lower=True)  10.4 us
  transfers between devices with their start and end apart: 12, of which 10 were waited for; matrix products, arithmetic and copies ran while one was open for 1% of the time, Pallas kernels for 0%

commit v1 on v0

v1 whole, which is shorter than its diff:
```python
import functools

import jax
import jax.numpy as jnp
from jax import lax
from jax.experimental import pallas as pl
from jax.experimental.pallas import tpu as pltpu
from jax.sharding import PartitionSpec as P

F32 = jnp.float32
BF16 = jnp.bfloat16
HIGHEST = lax.Precision.HIGHEST
PLANE = ("tx", "tz")
MIB = 1 << 20


def vmem():
    return pl.BlockSpec(memory_space=pltpu.VMEM)


def smem():
    return pl.BlockSpec(memory_space=pltpu.SMEM)


def anywhere():
    return pl.BlockSpec(memory_space=pl.ANY)


def dot_nt(a, b):
    return lax.dot_general(
        a, b, (((1,), (1,)), ((), ())), precision=HIGHEST, preferred_element_type=F32
    )


def edge_kernel(bnd_ref, x_ref, edge_ref, held, sem):
    count = edge_ref.shape[0]
    copies = []
    for j in range(count):
        start = pl.multiple_of(bnd_ref[j] * 128, 128)
        copies.append(
            pltpu.make_async_copy(x_ref.at[:, pl.ds(start, 128)], held.at[j], sem.at[j])
        )
        copies[-1].start()
    for j in range(count):
        copies[j].wait()
        edge_ref[j] = held[j].astype(BF16)


def take_edges(boundary, start_block):
    count = boundary.shape[0]
    width = start_block.shape[0]
    return pl.pallas_call(
        edge_kernel,
        out_shape=jax.ShapeDtypeStruct((count, width, 128), BF16),
        in_specs=[smem(), anywhere()],
        out_specs=vmem(),
        scratch_shapes=[
            pltpu.VMEM((count, width, 128), F32),
            pltpu.SemaphoreType.DMA((count,)),
        ],
        name="edges",
    )(boundary, start_block)


def neighbours_along(block, axis):
    count = lax.axis_size(axis)
    forward = [(i, i + 1) for i in range(count - 1)]
    backward = [(target, source) for source, target in forward]
    return lax.ppermute(block, axis, forward), lax.ppermute(block, axis, backward)


def halo(edge):
    block = edge
    for axis in ("tz", "ty"):
        low, high = neighbours_along(block, axis)
        block = jnp.concatenate([low, block, high], axis=0)
    low, high = neighbours_along(block, "tx")
    return low, block, high


def start_fill(far_refs, pool, base, sem):
    copies = []
    for j, ref in enumerate(far_refs):
        count = ref.shape[0]
        copies.append(
            pltpu.make_async_copy(ref, pool.at[pl.ds(base + j * count, count)], sem.at[j])
        )
        copies[-1].start()
    return copies


def first_kernel(
    nbr_ref, bnd_ref, x_ref, w_ref, low_ref, mid_ref, high_ref,
    mixed_ref, split_ref, edge_ref, keep_ref, pool, sem,
):
    blocks, slots = nbr_ref.shape
    width = x_ref.shape[0]
    fills = start_fill((low_ref, mid_ref, high_ref), pool, blocks, sem)
    for i in range(blocks):
        pool[i] = x_ref[:, i * 128:(i + 1) * 128].astype(BF16)
    for copy in fills:
        copy.wait()
    ones = jnp.ones((16, slots * 128), BF16)
    for i in range(blocks):
        picked = jnp.concatenate([pool[nbr_ref[i, s]] for s in range(slots)], axis=1)
        both = jnp.concatenate([picked, ones], axis=0)
        out = jnp.dot(both, w_ref[i], preferred_element_type=F32)
        keep = 1.0 - out[width:width + 8] * 0.125
        keep_ref[i] = keep
        mixed = x_ref[:, i * 128:(i + 1) * 128] * keep[0:1] + out[:width] * 0.125
        mixed_ref[i] = mixed
        head = mixed.astype(BF16)
        split_ref[i, 0:width] = head
        split_ref[i, width:2 * width] = (mixed - head.astype(F32)).astype(BF16)
    for j in range(edge_ref.shape[0]):
        edge_ref[j] = split_ref[bnd_ref[j]]


def first_step(neighbours, boundary, start_block, weights, far):
    blocks, slots = neighbours.shape
    width = start_block.shape[0]
    total = blocks + 3 * far[0].shape[0]
    return pl.pallas_call(
        first_kernel,
        out_shape=(
            jax.ShapeDtypeStruct((blocks, width, 128), F32),
            jax.ShapeDtypeStruct((blocks, 2 * width, 128), BF16),
            jax.ShapeDtypeStruct((boundary.shape[0], 2 * width, 128), BF16),
            jax.ShapeDtypeStruct((blocks, 8, 128), F32),
        ),
        in_specs=[smem(), smem(), vmem(), vmem(), anywhere(), anywhere(), anywhere()],
        out_specs=(vmem(), vmem(), vmem(), vmem()),
        scratch_shapes=[
            pltpu.VMEM((total, width, 128), BF16),
            pltpu.SemaphoreType.DMA((3,)),
        ],
        compiler_params=pltpu.CompilerParams(vmem_limit_bytes=24 * MIB),
        name="first_step",
    )(neighbours, boundary, start_block, weights, *far)


def gram_kernel(mixed_ref, gram_ref):
    total = None
    for i in range(mixed_ref.shape[0]):
        part = dot_nt(mixed_ref[i], mixed_ref[i])
        total = part if total is None else total + part
    gram_ref[...] = total


def local_gram(mixed):
    blocks, width, _ = mixed.shape
    return pl.pallas_call(
        gram_kernel,
        out_shape=jax.ShapeDtypeStruct((width, width), F32),
        in_specs=[vmem()],
        out_specs=vmem(),
        compiler_params=pltpu.CompilerParams(vmem_limit_bytes=8 * MIB),
        cost_estimate=pl.CostEstimate(
            flops=12 * blocks * 128 * width * width,
            bytes_accessed=4 * blocks * 128 * width,
            transcendentals=0,
        ),
        name="first_gram",
    )(mixed)


def second_kernel(
    nbr_ref, mixed_ref, split_ref, keep_ref, w_ref, gram_ref, low_ref, mid_ref, high_ref,
    out_ref, both_ref, pool, sem,
):
    blocks, slots = nbr_ref.shape
    width = mixed_ref.shape[1]
    fills = start_fill((low_ref, mid_ref, high_ref), pool, blocks, sem)
    for i in range(blocks):
        pool[i] = split_ref[i]
    for copy in fills:
        copy.wait()
    total = None
    for i in range(blocks):
        picked = jnp.concatenate([pool[nbr_ref[i, s]] for s in range(slots)], axis=1)
        out = jnp.dot(picked, w_ref[i], preferred_element_type=F32)
        mixed = mixed_ref[i] * keep_ref[i, 0:1] + (out[:width] + out[width:]) * 0.125
        out_ref[i] = mixed
        part = dot_nt(mixed, mixed)
        total = part if total is None else total + part
    both_ref[...] = jnp.concatenate([gram_ref[...], total], axis=1)


def second_step(neighbours, mixed, split, keep, weights, gram, far):
    blocks, slots = neighbours.shape
    width = mixed.shape[1]
    total = blocks + 3 * far[0].shape[0]
    return pl.pallas_call(
        second_kernel,
        out_shape=(
            jax.ShapeDtypeStruct((blocks, width, 128), F32),
            jax.ShapeDtypeStruct((width, 2 * width), F32),
        ),
        in_specs=[smem()] + [vmem()] * 5 + [anywhere()] * 3,
        out_specs=(vmem(), vmem()),
        scratch_shapes=[
            pltpu.VMEM((total, 2 * width, 128), BF16),
            pltpu.SemaphoreType.DMA((3,)),
        ],
        compiler_params=pltpu.CompilerParams(vmem_limit_bytes=24 * MIB),
        name="second_step",
    )(neighbours, mixed, split, keep, weights, gram, *far)


def sum_over_devices(values):
    rows, lanes = values.shape
    plane = lax.axis_size("tx") * lax.axis_size("tz")
    line = lax.axis_size("ty")
    piece = rows // plane
    parts = lax.all_to_all(values.reshape(plane, piece, lanes), PLANE, 0, 0)
    mine = jnp.sum(parts, axis=0)
    parts = lax.all_to_all(jnp.broadcast_to(mine[None], (line, piece, lanes)), "ty", 0, 0)
    mine = jnp.sum(parts, axis=0)
    parts = lax.all_to_all(jnp.broadcast_to(mine[None], (plane, piece, lanes)), PLANE, 0, 0)
    return parts.reshape(rows, lanes)


def finish_kernel(root_scale, gram_ref, mixed_ref, basis_ref, rfactor_ref):
    width = gram_ref.shape[0]
    shape = (width, 2 * width)
    row_id = lax.broadcasted_iota(jnp.int32, shape, 0)
    lane_id = lax.broadcasted_iota(jnp.int32, shape, 1)
    first = lane_id < width
    upper = gram_ref[...]
    inverse = (jnp.where(first, lane_id, lane_id - width) == row_id).astype(F32)
    pivots = jnp.ones(shape, F32)
    for k in range(width):
        column = jnp.where(first, upper[:, k:k + 1], upper[:, width + k:width + k + 1])
        pivot = column[k:k + 1]
        pivots = jnp.where(row_id == k, pivot, pivots)
        factor = jnp.where(row_id > k, column * (1.0 / pivot), 0.0)
        upper = upper - factor * upper[k:k + 1]
        inverse = inverse - factor * inverse[k:k + 1]
    scale = lax.rsqrt(pivots)
    lower_t = (upper * scale)[:, width:]
    inverse = inverse * scale
    rid = lax.broadcasted_iota(jnp.int32, (width, width), 0)
    cid = lax.broadcasted_iota(jnp.int32, (width, width), 1)
    lower_t = jnp.where(cid >= rid, lower_t, 0.0)
    rfactor = dot_nt(lower_t, inverse[:, :width])
    rfactor_ref[...] = jnp.where(cid >= rid, rfactor, 0.0)
    solve = inverse[:, width:] * root_scale
    for i in range(mixed_ref.shape[0]):
        basis_ref[:, i * 128:(i + 1) * 128] = jnp.dot(
            solve, mixed_ref[i], precision=HIGHEST, preferred_element_type=F32
        )


def finish(gram, mixed, root_scale):
    blocks, width, lanes = mixed.shape
    return pl.pallas_call(
        functools.partial(finish_kernel, root_scale),
        out_shape=(
            jax.ShapeDtypeStruct((width, blocks * lanes), F32),
            jax.ShapeDtypeStruct((width, width), F32),
        ),
        in_specs=[vmem(), vmem()],
        out_specs=(vmem(), vmem()),
        compiler_params=pltpu.CompilerParams(vmem_limit_bytes=16 * MIB),
        name="finish",
    )(gram, mixed)


def per_device(start_block, weights, neighbours, boundary):
    points = start_block.shape[1]
    blocks, slots, size, _ = weights.shape
    devices = lax.axis_size("tx") * lax.axis_size("ty") * lax.axis_size("tz")
    root_scale = float(points * devices) ** 0.5
    tiles = weights.reshape(blocks, slots * size, size)
    far = halo(take_edges(boundary, start_block))
    mixed, split, edge, keep = first_step(neighbours, boundary, start_block, tiles, far)
    far = halo(edge)
    gram = local_gram(mixed)
    mixed, both = second_step(neighbours, mixed, split, keep, tiles, gram, far)
    return finish(sum_over_devices(both), mixed, root_scale)


def solution(mesh):
    placed = (
        P(None, ("tx", "ty", "tz")),
        P(("tx", "ty", "tz"), None, None, None),
        P(("tx", "ty", "tz"), None),
        P(("tx", "ty", "tz")),
    )
    return jax.shard_map(
        per_device,
        mesh=mesh,
        in_specs=placed,
        out_specs=(P(None, ("tx", "ty", "tz")), P()),
        check_vma=False,
    )
```

time: 330 us -> 150 us (0.45)
  blocking collectives: 213 us -> 51.6 us
  other arithmetic: 31.6 us -> 0.93 us
  Pallas kernels: 0 us -> 15.6 us
  matrix products: 9.49 us -> 0 us
  waiting for transfers between devices: 30.1 us -> 37.9 us
    psum x2 -> x0, blocking collectives: 213 us -> none  [lower_factor(): total = lax.psum(local_gram, ('tx', 'ty', 'tz'))]
    all_to_all x0 -> x3, blocking collectives: none -> 51.6 us  [the longest x1 24.2 us: sum_over_devices(): lax.all_to_all(jnp.broadcast_to(mine[None], (line, piece, lanes)), 'ty',...]
    another operation x9 -> x0, other arithmetic: 23.5 us -> none  [the longest x6 13 us: lower_factor(): return jnp.linalg.cholesky(total)]
    pallas_call x0 -> x5, Pallas kernels: none -> 15.6 us  [the longest x1 6.91 us: finish(): pl.pallas_call(functools.partial(finish_kernel, root_scale), out_shape=(j...]
    ppermute x12, waiting for transfers between devices: 30.1 us -> 37.9 us  [the longest x6 26.2 us: neighbours_along(): lax.ppermute(block, axis, backward)]
    dot_general x4 -> x0, matrix products: 7.4 us -> none  [the longest x2 6.25 us: apply_operator(): jnp.einsum('kisq,isqp->kip', picked, weights, preferred_element_type=jnp....]
    gather x4 -> x0, local copies, waits for them, and re-layouts: 5.04 us -> none  [the longest x2 3.91 us: apply_operator(): picked = jnp.take(pool_grid, neighbours, axis=1)]
  transfers between devices with their start and end apart: 12 -> 12, of which waited for: 10 -> 11; matrix products, arithmetic and copies ran while one was open for 1% -> 1% of each run, Pallas kernels for 0% -> 1%
where the time goes in v1:
time: 150 us; the launch traced here: 149 us
  blocking collectives  51.6 us (34%)
  starting transfers between devices  38.8 us (26%)
  waiting for transfers between devices  37.9 us (25%)
  Pallas kernels  15.6 us (10%)
  local copies, waits for them, and re-layouts  3.12 us (2%)
    ppermute x6, waiting for transfers between devices, neighbours_along(): lax.ppermute(block, axis, backward)  26.2 us
    all_to_all x1, blocking collectives, sum_over_devices(): lax.all_to_all(jnp.broadcast_to(mine[None], (line, piece, lanes)), 'ty',...  24.2 us
    ppermute x6, starting transfers between devices, neighbours_along(): lax.ppermute(block, axis, forward)  23.9 us
    all_to_all x1, blocking collectives, sum_over_devices(): parts = lax.all_to_all(values.reshape(plane, piece, lanes), PLANE, 0, 0)  15.2 us
    ppermute x6, starting transfers between devices, neighbours_along(): lax.ppermute(block, axis, backward)  14.9 us
    all_to_all x1, blocking collectives, sum_over_devices(): lax.all_to_all(jnp.broadcast_to(mine[None], (plane, piece, lanes)), PLANE...  12.2 us
    ppermute x6, waiting for transfers between devices, neighbours_along(): lax.ppermute(block, axis, forward)  11.8 us
    pallas_call x1, Pallas kernels, finish(): pl.pallas_call(functools.partial(finish_kernel, root_scale), out_shape=(j...  6.91 us
  transfers between devices with their start and end apart: 12, of which 11 were waited for; matrix products, arithmetic and copies ran while one was open for 1% of the time, Pallas kernels for 1%

profile of v1, /device:TPU:1, one launch (start us, length us, event | category | flops | bytes accessed | tf_op | source)
XLA Modules:
  0.0 148.9 jit_solution(12169284205688964657)
XLA Ops:
  0.6 0.0 copy-start.3
  0.6 0.0 copy-start.2
  0.6 0.0 copy-start.4
  0.7 2.3 %edges.1 = bf16[4,64,128]{2,1,0:T(8,128)(2,1)} custom-call(s32[4]{0:T(128)} %bnd_ref.3, f32[64,2048]{1,0:T(8,128)} %x_ref.3), custom_call_target="tpu_custom_call" | custom-call | tf_op jit(solution)/shard_map/edges/pallas_call | solution.py:52
  2.9 1.3 collective-permute-start.1
  4.2 4.7 %collective-permute-start = (bf16[4,64,128]{2,1,0:T(8,128)(2,1)}, bf16[4,64,128]{2,1,0:T(8,128)(2,1)S(1)}, u32[]{:S(2)}, u32[]{:S(2)}) collective-permute-start(bf16[4,64,128]{2,1,0:T(8,128)(2,1)} %edges.1), channel_id=1, source_target_pairs={{0,1},{1,2},{2,3},{4,5},{5,6},{6,7},{8,9},{9,10},{10,11},{12,13},{... | collective-permute-start | bytes 196616 | tf_op jit(solution)/shard_map/ppermute | solution.py:69
  8.9 0.0 collective-permute-done.1
  8.9 1.6 %collective-permute-done = bf16[4,64,128]{2,1,0:T(8,128)(2,1)S(1)} collective-permute-done((bf16[4,64,128]{2,1,0:T(8,128)(2,1)}, bf16[4,64,128]{2,1,0:T(8,128)(2,1)S(1)}, u32[]{:S(2)}, u32[]{:S(2)}) %collective-permute-start) | collective-permute-done | bytes 65568 | tf_op jit(solution)/shard_map/ppermute | solution.py:69
  10.5 0.9 pad_maximum_fusion
  11.4 3.7 %collective-permute-start.2 = (bf16[12,64,128]{2,1,0:T(8,128)(2,1)S(1)}, bf16[12,64,128]{2,1,0:T(8,128)(2,1)S(1)}, u32[]{:S(2)}, u32[]{:S(2)}) collective-permute-start(bf16[12,64,128]{2,1,0:T(8,128)(2,1)S(1)} %pad_maximum_fusion), channel_id=1, source_target_pairs={{0,4},{4,8},{8,12},{12,16},{16,20},{20,24},{24,28},{28,32},{32,36}... | collective-permute-start | bytes 589832 | tf_op jit(solution)/shard_map/ppermute | solution.py:69
  15.1 1.3 collective-permute-start.3
  16.4 1.3 collective-permute-done.2
  17.8 0.9 constant_dynamic-update-slice_fusion.2
  18.6 3.1 %collective-permute-done.3 = bf16[12,64,128]{2,1,0:T(8,128)(2,1)S(1)} collective-permute-done((bf16[12,64,128]{2,1,0:T(8,128)(2,1)S(1)}, bf16[12,64,128]{2,1,0:T(8,128)(2,1)S(1)}, u32[]{:S(2)}, u32[]{:S(2)}) %collective-permute-start.3) | collective-permute-done | bytes 196640 | tf_op jit(solution)/shard_map/ppermute | solution.py:69
  21.7 7.8 %collective-permute-start.5 = (bf16[36,64,128]{2,1,0:T(8,128)(2,1)S(1)}, bf16[36,64,128]{2,1,0:T(8,128)(2,1)S(1)}, u32[]{:S(2)}, u32[]{:S(2)}) collective-permute-start(bf16[36,64,128]{2,1,0:T(8,128)(2,1)S(1)} %constant_dynamic-update-slice_fusion.mid_ref), channel_id=1, source_target_pairs={{64,0},{128,64},{192,128},{256,192},{320,256},{384,320},{448,384},... | collective-permute-start | bytes 1769480 | tf_op jit(solution)/shard_map/ppermute | solution.py:69
  29.6 1.9 %collective-permute-start.4 = (bf16[36,64,128]{2,1,0:T(8,128)(2,1)S(1)}, bf16[36,64,128]{2,1,0:T(8,128)(2,1)S(1)}, u32[]{:S(2)}, u32[]{:S(2)}) collective-permute-start(bf16[36,64,128]{2,1,0:T(8,128)(2,1)S(1)} %constant_dynamic-update-slice_fusion.mid_ref), channel_id=1, source_target_pairs={{0,64},{64,128},{128,192},{192,256},{256,320},{320,384},{384,448},... | collective-permute-start | bytes 1769480 | tf_op jit(solution)/shard_map/ppermute | solution.py:69
  31.5 0.0 copy-done.4
  31.5 0.1 copy.11.nbr_ref
  31.6 3.8 %collective-permute-done.5.high_ref = bf16[36,64,128]{2,1,0:T(8,128)(2,1)S(1)} collective-permute-done((bf16[36,64,128]{2,1,0:T(8,128)(2,1)S(1)}, bf16[36,64,128]{2,1,0:T(8,128)(2,1)S(1)}, u32[]{:S(2)}, u32[]{:S(2)}) %collective-permute-start.5) | collective-permute-done | bytes 589856 | tf_op jit(solution)/shard_map/ppermute | solution.py:69
  35.4 2.9 %collective-permute-done.4.low_ref = bf16[36,64,128]{2,1,0:T(8,128)(2,1)S(1)} collective-permute-done((bf16[36,64,128]{2,1,0:T(8,128)(2,1)S(1)}, bf16[36,64,128]{2,1,0:T(8,128)(2,1)S(1)}, u32[]{:S(2)}, u32[]{:S(2)}) %collective-permute-start.4) | collective-permute-done | bytes 589856 | tf_op jit(solution)/shard_map/ppermute | solution.py:69
  38.3 0.0 copy-done.3
  38.3 0.0 copy-done.2
  38.3 0.0 copy-start
  38.3 1.9 %copy-done = bf16[16,6,128,128]{3,2,1,0:T(8,128)(2,1)S(1)} copy-done((bf16[16,6,128,128]{3,2,1,0:T(8,128)(2,1)S(1)}, bf16[16,6,128,128]{3,2,1,0:T(8,128)(2,1)}, u32[]{:S(2)}) %copy-start) | copy-done | bytes 3145752
  40.2 1.9 %first_step.1 = (f32[16,64,128]{2,1,0:T(8,128)S(1)}, bf16[16,128,128]{2,1,0:T(8,128)(2,1)S(1)}, bf16[4,128,128]{2,1,0:T(8,128)(2,1)S(1)}, f32[16,8,128]{2,1,0:T(8,128)S(1)}) custom-call(s32[16,6]{1,0:T(8,128)S(1)} %copy.11.nbr_ref, s32[4]{0:T(128)S(1)} %copy-done.3, f32[64,2048]{1,0:T(8,128)S(1)} %copy-done.2, bf16[16,768,128]{2,1,0:T(8,128)(2,1)S(1)} %bitcast.3, ...), custom_call_target="tpu_custom_call" | custom-call | tf_op jit(solution)/shard_map/first_step/pallas_call | solution.py:123
  42.1 3.9 %collective-permute-start.6 = (bf16[4,128,128]{2,1,0:T(8,128)(2,1)S(1)}, bf16[4,128,128]{2,1,0:T(8,128)(2,1)S(1)}, u32[]{:S(2)}, u32[]{:S(2)}) collective-permute-start(bf16[4,128,128]{2,1,0:T(8,128)(2,1)S(1)} %get-tuple-element.11), channel_id=1, source_target_pairs={{0,1},{1,2},{2,3},{4,5},{5,6},{6,7},{8,9},{9,10},{10,11},{12,13},{... | collective-permute-start | bytes 393224 | tf_op jit(solution)/shard_map/ppermute | solution.py:69
  46.0 1.3 collective-permute-start.7
  47.3 0.6 collective-permute-done.6
  48.0 3.7 %collective-permute-done.7 = bf16[4,128,128]{2,1,0:T(8,128)(2,1)S(1)} collective-permute-done((bf16[4,128,128]{2,1,0:T(8,128)(2,1)S(1)}, bf16[4,128,128]{2,1,0:T(8,128)(2,1)S(1)}, u32[]{:S(2)}, u32[]{:S(2)}) %collective-permute-start.7) | collective-permute-done | bytes 131104 | tf_op jit(solution)/shard_map/ppermute | solution.py:69
  51.7 0.0 copy-start.1
  51.7 2.1 %collective-permute-start.8 = (bf16[12,128,128]{2,1,0:T(8,128)(2,1)S(1)}, bf16[12,128,128]{2,1,0:T(8,128)(2,1)S(1)}, u32[]{:S(2)}, u32[]{:S(2)}) collective-permute-start(bf16[12,128,128]{2,1,0:T(8,128)(2,1)S(1)} %constant_dynamic-update-slice_fusion.5), channel_id=1, source_target_pairs={{0,4},{4,8},{8,12},{12,16},{16,20},{20,24},{24,28},{28,32},{32,36}... | collective-permute-start | bytes 1179656 | tf_op jit(solution)/shard_map/ppermute | solution.py:69
  53.8 1.3 collective-permute-start.9
  55.1 4.2 %collective-permute-done.8 = bf16[12,128,128]{2,1,0:T(8,128)(2,1)S(1)} collective-permute-done((bf16[12,128,128]{2,1,0:T(8,128)(2,1)S(1)}, bf16[12,128,128]{2,1,0:T(8,128)(2,1)S(1)}, u32[]{:S(2)}, u32[]{:S(2)}) %collective-permute-start.8) | collective-permute-done | bytes 393248 | tf_op jit(solution)/shard_map/ppermute | solution.py:69
  59.4 4.5 %collective-permute-done.9 = bf16[12,128,128]{2,1,0:T(8,128)(2,1)S(1)} collective-permute-done((bf16[12,128,128]{2,1,0:T(8,128)(2,1)S(1)}, bf16[12,128,128]{2,1,0:T(8,128)(2,1)S(1)}, u32[]{:S(2)}, u32[]{:S(2)}) %collective-permute-start.9) | collective-permute-done | bytes 393248 | tf_op jit(solution)/shard_map/ppermute | solution.py:69
  63.9 0.1 constant_dynamic-update-slice_fusion.8.mid_ref
  64.0 1.9 %collective-permute-start.11 = (bf16[36,128,128]{2,1,0:T(8,128)(2,1)S(1)}, bf16[36,128,128]{2,1,0:T(8,128)(2,1)S(1)}, u32[]{:S(2)}, u32[]{:S(2)}) collective-permute-start(bf16[36,128,128]{2,1,0:T(8,128)(2,1)S(1)} %constant_dynamic-update-slice_fusion.8.mid_ref), channel_id=1, source_target_pairs={{64,0},{128,64},{192,128},{256,192},{320,256},{384,320},{448,384},... | collective-permute-start | bytes 3538952 | tf_op jit(solution)/shard_map/ppermute | solution.py:69
  65.9 7.6 %collective-permute-start.10 = (bf16[36,128,128]{2,1,0:T(8,128)(2,1)S(1)}, bf16[36,128,128]{2,1,0:T(8,128)(2,1)S(1)}, u32[]{:S(2)}, u32[]{:S(2)}) collective-permute-start(bf16[36,128,128]{2,1,0:T(8,128)(2,1)S(1)} %constant_dynamic-update-slice_fusion.8.mid_ref), channel_id=1, source_target_pairs={{0,64},{64,128},{128,192},{192,256},{256,320},{320,384},{384,448},... | collective-permute-start | bytes 3538952 | tf_op jit(solution)/shard_map/ppermute | solution.py:69
  73.5 0.9 first_gram.1.gram_ref
  74.5 11.0 %collective-permute-done.11.high_ref = bf16[36,128,128]{2,1,0:T(8,128)(2,1)S(1)} collective-permute-done((bf16[36,128,128]{2,1,0:T(8,128)(2,1)S(1)}, bf16[36,128,128]{2,1,0:T(8,128)(2,1)S(1)}, u32[]{:S(2)}, u32[]{:S(2)}) %collective-permute-start.11) | collective-permute-done | bytes 1179680 | tf_op jit(solution)/shard_map/ppermute | solution.py:69
  85.5 1.2 collective-permute-done.10.low_ref
  86.7 0.0 copy-done.1
  86.7 3.6 %second_step.1 = (f32[16,64,128]{2,1,0:T(8,128)S(1)}, f32[64,128]{1,0:T(8,128)S(1)}) custom-call(s32[16,6]{1,0:T(8,128)S(1)} %copy.11.nbr_ref, f32[16,64,128]{2,1,0:T(8,128)S(1)} %get-tuple-element.8.mixed_ref, bf16[16,128,128]{2,1,0:T(8,128)(2,1)S(1)} %get-tuple-element.9.split_ref, f32[16,8,128]{2,1,0:T(8,128)S(1)} %get-tuple-element.10.keep_ref, ...), custom_call_target="tpu_custom_call" | custom-call | tf_op jit(solution)/shard_map/second_step/pallas_call | solution.py:193
  90.3 15.2 %all_to_all.15 = f32[32,2,128]{2,1,0:T(2,128)S(1)} all-to-all(f32[32,2,128]{2,1,0:T(2,128)S(1)} %bitcast.6), channel_id=1, replica_groups=mesh['tx'=8,'ty'=16,'tz'=4] {'tx','tz'}, dimensions={0} | all-to-all | bytes 65536 | tf_op jit(solution)/shard_map/all_to_all | solution.py:215
  105.5 24.2 %all_to_all.16 = f32[16,2,128]{2,1,0:T(2,128)S(1)} all-to-all(f32[16,2,128]{2,1,0:T(2,128)S(1)} %broadcast_in_dim.4), channel_id=1, replica_groups=mesh['tx'=8,'ty'=16,'tz'=4] {'ty'}, dimensions={0} | all-to-all | bytes 32768 | tf_op jit(solution)/shard_map/all_to_all | solution.py:217
  129.8 12.2 %all_to_all.17 = f32[32,2,128]{2,1,0:T(2,128)S(1)} all-to-all(f32[32,2,128]{2,1,0:T(2,128)S(1)} %broadcast_in_dim.5), channel_id=1, replica_groups=mesh['tx'=8,'ty'=16,'tz'=4] {'tx','tz'}, dimensions={0} | all-to-all | bytes 65536 | tf_op jit(solution)/shard_map/all_to_all | solution.py:219
  142.0 6.9 %finish.1 = (f32[64,2048]{1,0:T(8,128)}, f32[64,64]{1,0:T(8,128)}) custom-call(f32[64,128]{1,0:T(8,128)S(1)} %bitcast.5, f32[16,64,128]{2,1,0:T(8,128)S(1)} %get-tuple-element.13.mixed_ref), custom_call_target="tpu_custom_call" | custom-call | tf_op jit(solution)/shard_map/finish/pallas_call | solution.py:256
  (15 shorter events, 0.3 us)
Async XLA Ops:
  0.6 37.7 %copy-start.3 = (s32[4]{0:T(128)S(1)}, s32[4]{0:T(128)}, u32[]{:S(2)}) copy-start(s32[4]{0:T(128)} %bnd_ref.3) | copy-start | bytes 52
  0.6 37.7 %copy-start.2 = (f32[64,2048]{1,0:T(8,128)S(1)}, f32[64,2048]{1,0:T(8,128)}, u32[]{:S(2)}) copy-start(f32[64,2048]{1,0:T(8,128)} %x_ref.3) | copy-start | bytes 1572868
  0.6 30.8 %copy-start.4 = (s32[16,6]{0,1:T(8,128)S(1)}, s32[16,6]{0,1:T(8,128)}, u32[]{:S(2)}) copy-start(s32[16,6]{0,1:T(8,128)} %param.6) | copy-start | bytes 1156
  2.9 6.0 %collective-permute-start.1 = (bf16[4,64,128]{2,1,0:T(8,128)(2,1)}, bf16[4,64,128]{2,1,0:T(8,128)(2,1)S(1)}, u32[]{:S(2)}, u32[]{:S(2)}) collective-permute-start(bf16[4,64,128]{2,1,0:T(8,128)(2,1)} %edges.1), channel_id=1, source_target_pairs={{1,0},{2,1},{3,2},{5,4},{6,5},{7,6},{9,8},{10,9},{11,10},{13,12},{... | collective-permute-start | bytes 196616 | tf_op jit(solution)/shard_map/ppermute | solution.py:69
  4.2 6.3 %collective-permute-start = (bf16[4,64,128]{2,1,0:T(8,128)(2,1)}, bf16[4,64,128]{2,1,0:T(8,128)(2,1)S(1)}, u32[]{:S(2)}, u32[]{:S(2)}) collective-permute-start(bf16[4,64,128]{2,1,0:T(8,128)(2,1)} %edges.1), channel_id=1, source_target_pairs={{0,1},{1,2},{2,3},{4,5},{5,6},{6,7},{8,9},{9,10},{10,11},{12,13},{... | collective-permute-start | bytes 196616 | tf_op jit(solution)/shard_map/ppermute | solution.py:69
  11.4 6.3 %collective-permute-start.2 = (bf16[12,64,128]{2,1,0:T(8,128)(2,1)S(1)}, bf16[12,64,128]{2,1,0:T(8,128)(2,1)S(1)}, u32[]{:S(2)}, u32[]{:S(2)}) collective-permute-start(bf16[12,64,128]{2,1,0:T(8,128)(2,1)S(1)} %pad_maximum_fusion), channel_id=1, source_target_pairs={{0,4},{4,8},{8,12},{12,16},{16,20},{20,24},{24,28},{28,32},{32,36}... | collective-permute-start | bytes 589832 | tf_op jit(solution)/shard_map/ppermute | solution.py:69
  15.1 6.6 %collective-permute-start.3 = (bf16[12,64,128]{2,1,0:T(8,128)(2,1)S(1)}, bf16[12,64,128]{2,1,0:T(8,128)(2,1)S(1)}, u32[]{:S(2)}, u32[]{:S(2)}) collective-permute-start(bf16[12,64,128]{2,1,0:T(8,128)(2,1)S(1)} %pad_maximum_fusion), channel_id=1, source_target_pairs={{4,0},{8,4},{12,8},{16,12},{20,16},{24,20},{28,24},{32,28},{36,32}... | collective-permute-start | bytes 589832 | tf_op jit(solution)/shard_map/ppermute | solution.py:69
  21.7 13.6 %collective-permute-start.5 = (bf16[36,64,128]{2,1,0:T(8,128)(2,1)S(1)}, bf16[36,64,128]{2,1,0:T(8,128)(2,1)S(1)}, u32[]{:S(2)}, u32[]{:S(2)}) collective-permute-start(bf16[36,64,128]{2,1,0:T(8,128)(2,1)S(1)} %constant_dynamic-update-slice_fusion.mid_ref), channel_id=1, source_target_pairs={{64,0},{128,64},{192,128},{256,192},{320,256},{384,320},{448,384},... | collective-permute-start | bytes 1769480 | tf_op jit(solution)/shard_map/ppermute | solution.py:69
  29.6 8.7 %collective-permute-start.4 = (bf16[36,64,128]{2,1,0:T(8,128)(2,1)S(1)}, bf16[36,64,128]{2,1,0:T(8,128)(2,1)S(1)}, u32[]{:S(2)}, u32[]{:S(2)}) collective-permute-start(bf16[36,64,128]{2,1,0:T(8,128)(2,1)S(1)} %constant_dynamic-update-slice_fusion.mid_ref), channel_id=1, source_target_pairs={{0,64},{64,128},{128,192},{192,256},{256,320},{320,384},{384,448},... | collective-permute-start | bytes 1769480 | tf_op jit(solution)/shard_map/ppermute | solution.py:69
  38.3 1.9 %copy-start = (bf16[16,6,128,128]{3,2,1,0:T(8,128)(2,1)S(1)}, bf16[16,6,128,128]{3,2,1,0:T(8,128)(2,1)}, u32[]{:S(2)}) copy-start(bf16[16,6,128,128]{3,2,1,0:T(8,128)(2,1)} %param.5) | copy-start | bytes 9437188
  42.1 5.8 %collective-permute-start.6 = (bf16[4,128,128]{2,1,0:T(8,128)(2,1)S(1)}, bf16[4,128,128]{2,1,0:T(8,128)(2,1)S(1)}, u32[]{:S(2)}, u32[]{:S(2)}) collective-permute-start(bf16[4,128,128]{2,1,0:T(8,128)(2,1)S(1)} %get-tuple-element.11), channel_id=1, source_target_pairs={{0,1},{1,2},{2,3},{4,5},{5,6},{6,7},{8,9},{9,10},{10,11},{12,13},{... | collective-permute-start | bytes 393224 | tf_op jit(solution)/shard_map/ppermute | solution.py:69
  46.0 5.7 %collective-permute-start.7 = (bf16[4,128,128]{2,1,0:T(8,128)(2,1)S(1)}, bf16[4,128,128]{2,1,0:T(8,128)(2,1)S(1)}, u32[]{:S(2)}, u32[]{:S(2)}) collective-permute-start(bf16[4,128,128]{2,1,0:T(8,128)(2,1)S(1)} %get-tuple-element.11), channel_id=1, source_target_pairs={{1,0},{2,1},{3,2},{5,4},{6,5},{7,6},{9,8},{10,9},{11,10},{13,12},{... | collective-permute-start | bytes 393224 | tf_op jit(solution)/shard_map/ppermute | solution.py:69
  51.7 34.9 %copy-start.1 = (bf16[16,6,128,128]{3,2,1,0:T(8,128)(2,1)S(1)}, bf16[16,6,128,128]{3,2,1,0:T(8,128)(2,1)}, u32[]{:S(2)}) copy-start(bf16[16,6,128,128]{3,2,1,0:T(8,128)(2,1)} %param.5) | copy-start | bytes 9437188
  51.7 7.5 %collective-permute-start.8 = (bf16[12,128,128]{2,1,0:T(8,128)(2,1)S(1)}, bf16[12,128,128]{2,1,0:T(8,128)(2,1)S(1)}, u32[]{:S(2)}, u32[]{:S(2)}) collective-permute-start(bf16[12,128,128]{2,1,0:T(8,128)(2,1)S(1)} %constant_dynamic-update-slice_fusion.5), channel_id=1, source_target_pairs={{0,4},{4,8},{8,12},{12,16},{16,20},{20,24},{24,28},{28,32},{32,36}... | collective-permute-start | bytes 1179656 | tf_op jit(solution)/shard_map/ppermute | solution.py:69
  53.8 10.1 %collective-permute-start.9 = (bf16[12,128,128]{2,1,0:T(8,128)(2,1)S(1)}, bf16[12,128,128]{2,1,0:T(8,128)(2,1)S(1)}, u32[]{:S(2)}, u32[]{:S(2)}) collective-permute-start(bf16[12,128,128]{2,1,0:T(8,128)(2,1)S(1)} %constant_dynamic-update-slice_fusion.5), channel_id=1, source_target_pairs={{4,0},{8,4},{12,8},{16,12},{20,16},{24,20},{28,24},{32,28},{36,32}... | collective-permute-start | bytes 1179656 | tf_op jit(solution)/shard_map/ppermute | solution.py:69
  64.0 21.5 %collective-permute-start.11 = (bf16[36,128,128]{2,1,0:T(8,128)(2,1)S(1)}, bf16[36,128,128]{2,1,0:T(8,128)(2,1)S(1)}, u32[]{:S(2)}, u32[]{:S(2)}) collective-permute-start(bf16[36,128,128]{2,1,0:T(8,128)(2,1)S(1)} %constant_dynamic-update-slice_fusion.8.mid_ref), channel_id=1, source_target_pairs={{64,0},{128,64},{192,128},{256,192},{320,256},{384,320},{448,384},... | collective-permute-start | bytes 3538952 | tf_op jit(solution)/shard_map/ppermute | solution.py:69
  65.9 20.7 %collective-permute-start.10 = (bf16[36,128,128]{2,1,0:T(8,128)(2,1)S(1)}, bf16[36,128,128]{2,1,0:T(8,128)(2,1)S(1)}, u32[]{:S(2)}, u32[]{:S(2)}) collective-permute-start(bf16[36,128,128]{2,1,0:T(8,128)(2,1)S(1)} %constant_dynamic-update-slice_fusion.8.mid_ref), channel_id=1, source_target_pairs={{0,64},{64,128},{128,192},{192,256},{256,320},{320,384},{384,448},... | collective-permute-start | bytes 3538952 | tf_op jit(solution)/shard_map/ppermute | solution.py:69

commit v2 on v1

--- a/solution.py
+++ b/solution.py
@@ -12,6 +12,7 @@
 HIGHEST = lax.Precision.HIGHEST
 PLANE = ("tx", "tz")
 MIB = 1 << 20
+PANEL = 8
 
 
 def vmem():
@@ -24,6 +25,10 @@
 
 def anywhere():
     return pl.BlockSpec(memory_space=pl.ANY)
+
+
+def in_hbm(array):
+    return pltpu.with_memory_space_constraint(array, pltpu.HBM)
 
 
 def dot_nt(a, b):
@@ -32,8 +37,11 @@
     )
 
 
-def edge_kernel(bnd_ref, x_ref, edge_ref, held, sem):
+def edge_kernel(list_ref, x_ref, edge_ref, bnd_ref, held, list_sem, sem):
     count = edge_ref.shape[0]
+    listing = pltpu.make_async_copy(list_ref, bnd_ref, list_sem)
+    listing.start()
+    listing.wait()
     copies = []
     for j in range(count):
         start = pl.multiple_of(bnd_ref[j] * 128, 128)
@@ -52,14 +60,38 @@
     return pl.pallas_call(
         edge_kernel,
         out_shape=jax.ShapeDtypeStruct((count, width, 128), BF16),
-        in_specs=[smem(), anywhere()],
+        in_specs=[anywhere(), anywhere()],
         out_specs=vmem(),
         scratch_shapes=[
+            pltpu.SMEM((count,), jnp.int32),
             pltpu.VMEM((count, width, 128), F32),
+            pltpu.SemaphoreType.DMA,
             pltpu.SemaphoreType.DMA((count,)),
         ],
+        compiler_params=pltpu.CompilerParams(vmem_limit_bytes=2 * MIB),
         name="edges",
-    )(boundary, start_block)
+    )(in_hbm(boundary), in_hbm(start_block))
+
+
+def hold_kernel(w_ref, held_ref, sem):
+    copy = pltpu.make_async_copy(w_ref, held_ref, sem)
+    copy.start()
+    copy.wait()
+
+
+def hold_weights(tiles):
+    return pl.pallas_call(
+        hold_kernel,
+        out_shape=jax.ShapeDtypeStruct(tiles.shape, tiles.dtype),
+        in_specs=[anywhere()],
+        out_specs=vmem(),
+        scratch_shapes=[pltpu.SemaphoreType.DMA],
+        compiler_params=pltpu.CompilerParams(vmem_limit_bytes=8 * MIB),
+        cost_estimate=pl.CostEstimate(
+            flops=0, bytes_accessed=4 * tiles.size, transcendentals=0
+        ),
+        name="hold_weights",
+    )(in_hbm(tiles))
 
 
 def neighbours_along(block, axis):
@@ -166,7 +198,7 @@
 
 def second_kernel(
     nbr_ref, mixed_ref, split_ref, keep_ref, w_ref, gram_ref, low_ref, mid_ref, high_ref,
-    out_ref, both_ref, pool, sem,
+    out_ref, both_ref, pool, wide, sem,
 ):
     blocks, slots = nbr_ref.shape
     width = mixed_ref.shape[1]
@@ -175,15 +207,13 @@
         pool[i] = split_ref[i]
     for copy in fills:
         copy.wait()
-    total = None
     for i in range(blocks):
         picked = jnp.concatenate([pool[nbr_ref[i, s]] for s in range(slots)], axis=1)
         out = jnp.dot(picked, w_ref[i], preferred_element_type=F32)
         mixed = mixed_ref[i] * keep_ref[i, 0:1] + (out[:width] + out[width:]) * 0.125
         out_ref[i] = mixed
-        part = dot_nt(mixed, mixed)
-        total = part if total is None else total + part
-    both_ref[...] = jnp.concatenate([gram_ref[...], total], axis=1)
+        wide[:, i * 128:(i + 1) * 128] = mixed
+    both_ref[...] = jnp.concatenate([gram_ref[...], dot_nt(wide[...], wide[...])], axis=1)
 
 
 def second_step(neighbours, mixed, split, keep, weights, gram, far):
@@ -200,6 +230,7 @@
         out_specs=(vmem(), vmem()),
         scratch_shapes=[
             pltpu.VMEM((total, 2 * width, 128), BF16),
+            pltpu.VMEM((width, blocks * 128), F32),
             pltpu.SemaphoreType.DMA((3,)),
         ],
         compiler_params=pltpu.CompilerParams(vmem_limit_bytes=24 * MIB),
@@ -221,27 +252,65 @@
 
 
 def finish_kernel(root_scale, gram_ref, mixed_ref, basis_ref, rfactor_ref):
-    width = gram_ref.shape[0]
-    shape = (width, 2 * width)
-    row_id = lax.broadcasted_iota(jnp.int32, shape, 0)
-    lane_id = lax.broadcasted_iota(jnp.int32, shape, 1)
-    first = lane_id < width
-    upper = gram_ref[...]
-    inverse = (jnp.where(first, lane_id, lane_id - width) == row_id).astype(F32)
-    pivots = jnp.ones(shape, F32)
-    for k in range(width):
-        column = jnp.where(first, upper[:, k:k + 1], upper[:, width + k:width + k + 1])
-        pivot = column[k:k + 1]
-        pivots = jnp.where(row_id == k, pivot, pivots)
-        factor = jnp.where(row_id > k, column * (1.0 / pivot), 0.0)
-        upper = upper - factor * upper[k:k + 1]
-        inverse = inverse - factor * inverse[k:k + 1]
-    scale = lax.rsqrt(pivots)
-    lower_t = (upper * scale)[:, width:]
-    inverse = inverse * scale
+    width, lanes = gram_ref.shape
+    tiles = width // PANEL
+    lane = lax.broadcasted_iota(jnp.int32, (PANEL, lanes), 1)
+    row = lax.broadcasted_iota(jnp.int32, (PANEL, lanes), 0)
+    first = lane < width
+    own = jnp.where(first, lane, lane - width)
+    upper = [gram_ref[t * PANEL:(t + 1) * PANEL, :] for t in range(tiles)]
+    inverse = [(own == row + t * PANEL).astype(F32) for t in range(tiles)]
+    pivots = []
+
+    def spread_row(tile, r):
+        return jnp.broadcast_to(tile[r:r + 1], tile.shape)
+
+    for p in range(tiles):
+        columns = []
+        for j in range(PANEL):
+            lane_of = jnp.where(first, 0, width) + (p * PANEL + j)
+            columns.append([
+                jnp.take_along_axis(upper[t], lane_of, axis=1, mode="promise_in_bounds")
+                if t >= p else None
+                for t in range(tiles)
+            ])
+        corner = [[spread_row(columns[j][p], i) for j in range(i + 1)] for i in range(PANEL)]
+        up_rows = [spread_row(upper[p], j) for j in range(PANEL)]
+        inv_rows = [spread_row(inverse[p], j) for j in range(PANEL)]
+        factor = [[None] * PANEL for _ in range(PANEL)]
+        recip = []
+        pivot = corner[0][0]
+        for j in range(PANEL):
+            recip.append(1.0 / corner[j][j])
+            pivot = jnp.where(row == j, corner[j][j], pivot)
+            for i in range(j + 1, PANEL):
+                factor[i][j] = corner[i][j] * recip[j]
+            for i in range(j + 1, PANEL):
+                for m in range(j + 1, i + 1):
+                    corner[i][m] = corner[i][m] - factor[i][j] * corner[m][j]
+        pivots.append(pivot)
+        for j in range(PANEL):
+            for m in range(j + 1, PANEL):
+                up_rows[m] = up_rows[m] - factor[m][j] * up_rows[j]
+                inv_rows[m] = inv_rows[m] - factor[m][j] * inv_rows[j]
+        for t in range(p, tiles):
+            left = []
+            for j in range(PANEL):
+                column = columns[j][t]
+                for m in range(j):
+                    column = column - left[m] * corner[j][m]
+                left.append(column * recip[j])
+            if t == p:
+                left = [jnp.where(row > j, left[j], 0.0) for j in range(PANEL)]
+            for j in range(PANEL):
+                upper[t] = upper[t] - left[j] * up_rows[j]
+                inverse[t] = inverse[t] - left[j] * inv_rows[j]
+    scale = [lax.rsqrt(pivot) for pivot in pivots]
+    upper = jnp.concatenate([a * b for a, b in zip(upper, scale)], axis=0)
+    inverse = jnp.concatenate([a * b for a, b in zip(inverse, scale)], axis=0)
     rid = lax.broadcasted_iota(jnp.int32, (width, width), 0)
     cid = lax.broadcasted_iota(jnp.int32, (width, width), 1)
-    lower_t = jnp.where(cid >= rid, lower_t, 0.0)
+    lower_t = jnp.where(cid >= rid, upper[:, width:], 0.0)
     rfactor = dot_nt(lower_t, inverse[:, :width])
     rfactor_ref[...] = jnp.where(cid >= rid, rfactor, 0.0)
     solve = inverse[:, width:] * root_scale
@@ -271,7 +340,7 @@
     blocks, slots, size, _ = weights.shape
     devices = lax.axis_size("tx") * lax.axis_size("ty") * lax.axis_size("tz")
     root_scale = float(points * devices) ** 0.5
-    tiles = weights.reshape(blocks, slots * size, size)
+    tiles = hold_weights(weights.reshape(blocks, slots * size, size))
     far = halo(take_edges(boundary, start_block))
     mixed, split, edge, keep = first_step(neighbours, boundary, start_block, tiles, far)
     far = halo(edge)

time: 150 us -> 141 us (0.940)
  Pallas kernels: 15.6 us -> 12.6 us
  local copies, waits for them, and re-layouts: 3.12 us -> 0.39 us
    pallas_call x1, Pallas kernels: 6.91 us -> 2.95 us  [finish(): pl.pallas_call(functools.partial(finish_kernel, root_scale), out_shape=(j...]
    unnamed x21 -> x17, local copies, waits for them, and re-layouts: 3 us -> 0.27 us
    pallas_call x0 -> x1, Pallas kernels: none -> 1.96 us  [hold_weights(): pl.pallas_call(hold_kernel, out_shape=jax.ShapeDtypeStruct(tiles.shape, t...]
  transfers between devices with their start and end apart: 12 -> 12, of which waited for: 11 -> 11; matrix products, arithmetic and copies ran while one was open for 1% -> 0% of each run, Pallas kernels for 1% -> 2%
where the time goes in v2:
time: 141 us
  blocking collectives  51.6 us (37%)
  starting transfers between devices  38.1 us (27%)
  waiting for transfers between devices  37 us (26%)
  Pallas kernels  12.6 us (9%)
    ppermute x6, waiting for transfers between devices, neighbours_along(): lax.ppermute(block, axis, backward)  25 us
    all_to_all x1, blocking collectives, sum_over_devices(): lax.all_to_all(jnp.broadcast_to(mine[None], (line, piece, lanes)), 'ty',...  24.2 us
    ppermute x6, starting transfers between devices, neighbours_along(): lax.ppermute(block, axis, forward)  23.2 us
    all_to_all x1, blocking collectives, sum_over_devices(): parts = lax.all_to_all(values.reshape(plane, piece, lanes), PLANE, 0, 0)  15.2 us
    ppermute x6, starting transfers between devices, neighbours_along(): lax.ppermute(block, axis, backward)  14.9 us
    all_to_all x1, blocking collectives, sum_over_devices(): lax.all_to_all(jnp.broadcast_to(mine[None], (plane, piece, lanes)), PLANE...  12.2 us
    ppermute x6, waiting for transfers between devices, neighbours_along(): lax.ppermute(block, axis, forward)  12 us
    pallas_call x1, Pallas kernels, second_step(): pl.pallas_call(second_kernel, out_shape=(jax.ShapeDtypeStruct((blocks, wi...  3.19 us
  transfers between devices with their start and end apart: 12, of which 11 were waited for; matrix products, arithmetic and copies ran while one was open for 0% of the time, Pallas kernels for 2%

profile of v2, /device:TPU:1, one launch (start us, length us, event | category | flops | bytes accessed | tf_op | source)
XLA Modules:
  0.0 140.7 jit_solution(13870710549733800897)
XLA Ops:
  0.6 0.0 copy-start.2
  0.6 1.7 %edges.1 = bf16[4,64,128]{2,1,0:T(8,128)(2,1)S(1)} custom-call(s32[4]{0:T(128)} %bnd_ref.1, f32[64,2048]{1,0:T(8,128)} %x_ref.3), custom_call_target="tpu_custom_call" | custom-call | tf_op jit(solution)/shard_map/edges/pallas_call | solution.py:60
  2.3 1.3 collective-permute-start.1
  3.6 4.7 %collective-permute-start = (bf16[4,64,128]{2,1,0:T(8,128)(2,1)S(1)}, bf16[4,64,128]{2,1,0:T(8,128)(2,1)S(1)}, u32[]{:S(2)}, u32[]{:S(2)}) collective-permute-start(bf16[4,64,128]{2,1,0:T(8,128)(2,1)S(1)} %edges.1), channel_id=1, source_target_pairs={{0,1},{1,2},{2,3},{4,5},{5,6},{6,7},{8,9},{9,10},{10,11},{12,13},{... | collective-permute-start | bytes 196616 | tf_op jit(solution)/shard_map/ppermute | solution.py:101
  8.3 0.0 collective-permute-done.1
  8.3 1.3 collective-permute-done
  9.6 3.7 %collective-permute-start.2 = (bf16[12,64,128]{2,1,0:T(8,128)(2,1)S(1)}, bf16[12,64,128]{2,1,0:T(8,128)(2,1)S(1)}, u32[]{:S(2)}, u32[]{:S(2)}) collective-permute-start(bf16[12,64,128]{2,1,0:T(8,128)(2,1)S(1)} %pad_maximum_fusion), channel_id=1, source_target_pairs={{0,4},{4,8},{8,12},{12,16},{16,20},{20,24},{24,28},{28,32},{32,36}... | collective-permute-start | bytes 589832 | tf_op jit(solution)/shard_map/ppermute | solution.py:101
  13.3 1.3 collective-permute-start.3
  14.6 1.3 collective-permute-done.2
  16.0 3.9 %collective-permute-done.3 = bf16[12,64,128]{2,1,0:T(8,128)(2,1)S(1)} collective-permute-done((bf16[12,64,128]{2,1,0:T(8,128)(2,1)S(1)}, bf16[12,64,128]{2,1,0:T(8,128)(2,1)S(1)}, u32[]{:S(2)}, u32[]{:S(2)}) %collective-permute-start.3) | collective-permute-done | bytes 196640 | tf_op jit(solution)/shard_map/ppermute | solution.py:101
  19.9 7.8 %collective-permute-start.5 = (bf16[36,64,128]{2,1,0:T(8,128)(2,1)S(1)}, bf16[36,64,128]{2,1,0:T(8,128)(2,1)S(1)}, u32[]{:S(2)}, u32[]{:S(2)}) collective-permute-start(bf16[36,64,128]{2,1,0:T(8,128)(2,1)S(1)} %constant_dynamic-update-slice_fusion.mid_ref), channel_id=1, source_target_pairs={{64,0},{128,64},{192,128},{256,192},{320,256},{384,320},{448,384},... | collective-permute-start | bytes 1769480 | tf_op jit(solution)/shard_map/ppermute | solution.py:101
  27.8 1.9 %collective-permute-start.4 = (bf16[36,64,128]{2,1,0:T(8,128)(2,1)S(1)}, bf16[36,64,128]{2,1,0:T(8,128)(2,1)S(1)}, u32[]{:S(2)}, u32[]{:S(2)}) collective-permute-start(bf16[36,64,128]{2,1,0:T(8,128)(2,1)S(1)} %constant_dynamic-update-slice_fusion.mid_ref), channel_id=1, source_target_pairs={{0,64},{64,128},{128,192},{192,256},{256,320},{320,384},{384,448},... | collective-permute-start | bytes 1769480 | tf_op jit(solution)/shard_map/ppermute | solution.py:101
  29.7 0.0 copy-done.2
  29.7 0.1 copy.11.nbr_ref
  29.8 0.0 copy-start
  29.8 0.0 copy-start.1
  29.8 2.0 %hold_weights.1.w_ref = bf16[16,768,128]{2,1,0:T(8,128)(2,1)S(1)} custom-call(bf16[16,768,128]{2,1,0:T(8,128)(2,1)} %bitcast.5), custom_call_target="tpu_custom_call" | custom-call | bytes 6291456 | tf_op jit(solution)/shard_map/hold_weights/pallas_call | solution.py:83
  31.8 1.8 %collective-permute-done.5.high_ref = bf16[36,64,128]{2,1,0:T(8,128)(2,1)S(1)} collective-permute-done((bf16[36,64,128]{2,1,0:T(8,128)(2,1)S(1)}, bf16[36,64,128]{2,1,0:T(8,128)(2,1)S(1)}, u32[]{:S(2)}, u32[]{:S(2)}) %collective-permute-start.5) | collective-permute-done | bytes 589856 | tf_op jit(solution)/shard_map/ppermute | solution.py:101
  33.6 2.9 %collective-permute-done.4.low_ref = bf16[36,64,128]{2,1,0:T(8,128)(2,1)S(1)} collective-permute-done((bf16[36,64,128]{2,1,0:T(8,128)(2,1)S(1)}, bf16[36,64,128]{2,1,0:T(8,128)(2,1)S(1)}, u32[]{:S(2)}, u32[]{:S(2)}) %collective-permute-start.4) | collective-permute-done | bytes 589856 | tf_op jit(solution)/shard_map/ppermute | solution.py:101
  36.5 0.0 copy-done
  36.5 0.0 copy-done.1
  36.5 1.9 %first_step.1 = (f32[16,64,128]{2,1,0:T(8,128)S(1)}, bf16[16,128,128]{2,1,0:T(8,128)(2,1)S(1)}, bf16[4,128,128]{2,1,0:T(8,128)(2,1)S(1)}, f32[16,8,128]{2,1,0:T(8,128)S(1)}) custom-call(s32[16,6]{1,0:T(8,128)S(1)} %copy.11.nbr_ref, s32[4]{0:T(128)S(1)} %copy-done.1, f32[64,2048]{1,0:T(8,128)S(1)} %copy-done, bf16[16,768,128]{2,1,0:T(8,128)(2,1)S(1)} %hold_weights.1.w_ref, ...), custom_call_target="tpu_custom_call" | custom-call | tf_op jit(solution)/shard_map/first_step/pallas_call | solution.py:155
  38.4 4.0 %collective-permute-start.6 = (bf16[4,128,128]{2,1,0:T(8,128)(2,1)S(1)}, bf16[4,128,128]{2,1,0:T(8,128)(2,1)S(1)}, u32[]{:S(2)}, u32[]{:S(2)}) collective-permute-start(bf16[4,128,128]{2,1,0:T(8,128)(2,1)S(1)} %get-tuple-element.11), channel_id=1, source_target_pairs={{0,1},{1,2},{2,3},{4,5},{5,6},{6,7},{8,9},{9,10},{10,11},{12,13},{... | collective-permute-start | bytes 393224 | tf_op jit(solution)/shard_map/ppermute | solution.py:101
  42.4 1.3 collective-permute-start.7
  43.7 0.6 collective-permute-done.6
  44.4 3.7 %collective-permute-done.7 = bf16[4,128,128]{2,1,0:T(8,128)(2,1)S(1)} collective-permute-done((bf16[4,128,128]{2,1,0:T(8,128)(2,1)S(1)}, bf16[4,128,128]{2,1,0:T(8,128)(2,1)S(1)}, u32[]{:S(2)}, u32[]{:S(2)}) %collective-permute-start.7) | collective-permute-done | bytes 131104 | tf_op jit(solution)/shard_map/ppermute | solution.py:101
  48.2 1.8 %collective-permute-start.8 = (bf16[12,128,128]{2,1,0:T(8,128)(2,1)S(1)}, bf16[12,128,128]{2,1,0:T(8,128)(2,1)S(1)}, u32[]{:S(2)}, u32[]{:S(2)}) collective-permute-start(bf16[12,128,128]{2,1,0:T(8,128)(2,1)S(1)} %constant_dynamic-update-slice_fusion.5), channel_id=1, source_target_pairs={{0,4},{4,8},{8,12},{12,16},{16,20},{20,24},{24,28},{28,32},{32,36}... | collective-permute-start | bytes 1179656 | tf_op jit(solution)/shard_map/ppermute | solution.py:101
  50.0 1.3 collective-permute-start.9
  51.3 4.7 %collective-permute-done.8 = bf16[12,128,128]{2,1,0:T(8,128)(2,1)S(1)} collective-permute-done((bf16[12,128,128]{2,1,0:T(8,128)(2,1)S(1)}, bf16[12,128,128]{2,1,0:T(8,128)(2,1)S(1)}, u32[]{:S(2)}, u32[]{:S(2)}) %collective-permute-start.8) | collective-permute-done | bytes 393248 | tf_op jit(solution)/shard_map/ppermute | solution.py:101
  56.1 4.5 %collective-permute-done.9 = bf16[12,128,128]{2,1,0:T(8,128)(2,1)S(1)} collective-permute-done((bf16[12,128,128]{2,1,0:T(8,128)(2,1)S(1)}, bf16[12,128,128]{2,1,0:T(8,128)(2,1)S(1)}, u32[]{:S(2)}, u32[]{:S(2)}) %collective-permute-start.9) | collective-permute-done | bytes 393248 | tf_op jit(solution)/shard_map/ppermute | solution.py:101
  60.6 0.1 constant_dynamic-update-slice_fusion.8.mid_ref
  60.7 1.9 %collective-permute-start.11 = (bf16[36,128,128]{2,1,0:T(8,128)(2,1)S(1)}, bf16[36,128,128]{2,1,0:T(8,128)(2,1)S(1)}, u32[]{:S(2)}, u32[]{:S(2)}) collective-permute-start(bf16[36,128,128]{2,1,0:T(8,128)(2,1)S(1)} %constant_dynamic-update-slice_fusion.8.mid_ref), channel_id=1, source_target_pairs={{64,0},{128,64},{192,128},{256,192},{320,256},{384,320},{448,384},... | collective-permute-start | bytes 3538952 | tf_op jit(solution)/shard_map/ppermute | solution.py:101
  62.6 7.1 %collective-permute-start.10 = (bf16[36,128,128]{2,1,0:T(8,128)(2,1)S(1)}, bf16[36,128,128]{2,1,0:T(8,128)(2,1)S(1)}, u32[]{:S(2)}, u32[]{:S(2)}) collective-permute-start(bf16[36,128,128]{2,1,0:T(8,128)(2,1)S(1)} %constant_dynamic-update-slice_fusion.8.mid_ref), channel_id=1, source_target_pairs={{0,64},{64,128},{128,192},{192,256},{256,320},{320,384},{384,448},... | collective-permute-start | bytes 3538952 | tf_op jit(solution)/shard_map/ppermute | solution.py:101
  69.7 0.9 first_gram.1.gram_ref
  70.6 11.0 %collective-permute-done.11.high_ref = bf16[36,128,128]{2,1,0:T(8,128)(2,1)S(1)} collective-permute-done((bf16[36,128,128]{2,1,0:T(8,128)(2,1)S(1)}, bf16[36,128,128]{2,1,0:T(8,128)(2,1)S(1)}, u32[]{:S(2)}, u32[]{:S(2)}) %collective-permute-start.11) | collective-permute-done | bytes 1179680 | tf_op jit(solution)/shard_map/ppermute | solution.py:101
  81.6 1.2 collective-permute-done.10.low_ref
  82.8 3.2 %second_step.1 = (f32[16,64,128]{2,1,0:T(8,128)S(1)}, f32[64,128]{1,0:T(8,128)S(1)}) custom-call(s32[16,6]{1,0:T(8,128)S(1)} %copy.11.nbr_ref, f32[16,64,128]{2,1,0:T(8,128)S(1)} %get-tuple-element.8.mixed_ref, bf16[16,128,128]{2,1,0:T(8,128)(2,1)S(1)} %get-tuple-element.9.split_ref, f32[16,8,128]{2,1,0:T(8,128)S(1)} %get-tuple-element.10.keep_ref, ...), custom_call_target="tpu_custom_call" | custom-call | tf_op jit(solution)/shard_map/second_step/pallas_call | solution.py:223
  86.0 15.2 %all_to_all.15 = f32[32,2,128]{2,1,0:T(2,128)S(1)} all-to-all(f32[32,2,128]{2,1,0:T(2,128)S(1)} %bitcast.4), channel_id=1, replica_groups=mesh['tx'=8,'ty'=16,'tz'=4] {'tx','tz'}, dimensions={0} | all-to-all | bytes 65536 | tf_op jit(solution)/shard_map/all_to_all | solution.py:246
  101.3 24.2 %all_to_all.16 = f32[16,2,128]{2,1,0:T(2,128)S(1)} all-to-all(f32[16,2,128]{2,1,0:T(2,128)S(1)} %broadcast_in_dim.4), channel_id=1, replica_groups=mesh['tx'=8,'ty'=16,'tz'=4] {'ty'}, dimensions={0} | all-to-all | bytes 32768 | tf_op jit(solution)/shard_map/all_to_all | solution.py:248
  125.6 12.2 %all_to_all.17 = f32[32,2,128]{2,1,0:T(2,128)S(1)} all-to-all(f32[32,2,128]{2,1,0:T(2,128)S(1)} %broadcast_in_dim.5), channel_id=1, replica_groups=mesh['tx'=8,'ty'=16,'tz'=4] {'tx','tz'}, dimensions={0} | all-to-all | bytes 65536 | tf_op jit(solution)/shard_map/all_to_all | solution.py:250
  137.7 2.9 %finish.1 = (f32[64,2048]{1,0:T(8,128)}, f32[64,64]{1,0:T(8,128)}) custom-call(f32[64,128]{1,0:T(8,128)S(1)} %bitcast.3, f32[16,64,128]{2,1,0:T(8,128)S(1)} %get-tuple-element.13.mixed_ref), custom_call_target="tpu_custom_call" | custom-call | tf_op jit(solution)/shard_map/finish/pallas_call | solution.py:325
  (17 shorter events, 0.3 us)
Async XLA Ops:
  0.6 29.1 %copy-start.2 = (s32[16,6]{0,1:T(8,128)S(1)}, s32[16,6]{0,1:T(8,128)}, u32[]{:S(2)}) copy-start(s32[16,6]{0,1:T(8,128)} %param.6) | copy-start | bytes 1156
  2.3 6.0 %collective-permute-start.1 = (bf16[4,64,128]{2,1,0:T(8,128)(2,1)S(1)}, bf16[4,64,128]{2,1,0:T(8,128)(2,1)S(1)}, u32[]{:S(2)}, u32[]{:S(2)}) collective-permute-start(bf16[4,64,128]{2,1,0:T(8,128)(2,1)S(1)} %edges.1), channel_id=1, source_target_pairs={{1,0},{2,1},{3,2},{5,4},{6,5},{7,6},{9,8},{10,9},{11,10},{13,12},{... | collective-permute-start | bytes 196616 | tf_op jit(solution)/shard_map/ppermute | solution.py:101
  3.6 6.0 %collective-permute-start = (bf16[4,64,128]{2,1,0:T(8,128)(2,1)S(1)}, bf16[4,64,128]{2,1,0:T(8,128)(2,1)S(1)}, u32[]{:S(2)}, u32[]{:S(2)}) collective-permute-start(bf16[4,64,128]{2,1,0:T(8,128)(2,1)S(1)} %edges.1), channel_id=1, source_target_pairs={{0,1},{1,2},{2,3},{4,5},{5,6},{6,7},{8,9},{9,10},{10,11},{12,13},{... | collective-permute-start | bytes 196616 | tf_op jit(solution)/shard_map/ppermute | solution.py:101
  9.6 6.3 %collective-permute-start.2 = (bf16[12,64,128]{2,1,0:T(8,128)(2,1)S(1)}, bf16[12,64,128]{2,1,0:T(8,128)(2,1)S(1)}, u32[]{:S(2)}, u32[]{:S(2)}) collective-permute-start(bf16[12,64,128]{2,1,0:T(8,128)(2,1)S(1)} %pad_maximum_fusion), channel_id=1, source_target_pairs={{0,4},{4,8},{8,12},{12,16},{16,20},{20,24},{24,28},{28,32},{32,36}... | collective-permute-start | bytes 589832 | tf_op jit(solution)/shard_map/ppermute | solution.py:101
  13.3 6.6 %collective-permute-start.3 = (bf16[12,64,128]{2,1,0:T(8,128)(2,1)S(1)}, bf16[12,64,128]{2,1,0:T(8,128)(2,1)S(1)}, u32[]{:S(2)}, u32[]{:S(2)}) collective-permute-start(bf16[12,64,128]{2,1,0:T(8,128)(2,1)S(1)} %pad_maximum_fusion), channel_id=1, source_target_pairs={{4,0},{8,4},{12,8},{16,12},{20,16},{24,20},{28,24},{32,28},{36,32}... | collective-permute-start | bytes 589832 | tf_op jit(solution)/shard_map/ppermute | solution.py:101
  19.9 13.6 %collective-permute-start.5 = (bf16[36,64,128]{2,1,0:T(8,128)(2,1)S(1)}, bf16[36,64,128]{2,1,0:T(8,128)(2,1)S(1)}, u32[]{:S(2)}, u32[]{:S(2)}) collective-permute-start(bf16[36,64,128]{2,1,0:T(8,128)(2,1)S(1)} %constant_dynamic-update-slice_fusion.mid_ref), channel_id=1, source_target_pairs={{64,0},{128,64},{192,128},{256,192},{320,256},{384,320},{448,384},... | collective-permute-start | bytes 1769480 | tf_op jit(solution)/shard_map/ppermute | solution.py:101
  27.8 8.7 %collective-permute-start.4 = (bf16[36,64,128]{2,1,0:T(8,128)(2,1)S(1)}, bf16[36,64,128]{2,1,0:T(8,128)(2,1)S(1)}, u32[]{:S(2)}, u32[]{:S(2)}) collective-permute-start(bf16[36,64,128]{2,1,0:T(8,128)(2,1)S(1)} %constant_dynamic-update-slice_fusion.mid_ref), channel_id=1, source_target_pairs={{0,64},{64,128},{128,192},{192,256},{256,320},{320,384},{384,448},... | collective-permute-start | bytes 1769480 | tf_op jit(solution)/shard_map/ppermute | solution.py:101
  29.8 6.7 %copy-start = (f32[64,2048]{1,0:T(8,128)S(1)}, f32[64,2048]{1,0:T(8,128)}, u32[]{:S(2)}) copy-start(f32[64,2048]{1,0:T(8,128)} %x_ref.3) | copy-start | bytes 1572868
  29.8 6.7 %copy-start.1 = (s32[4]{0:T(128)S(1)}, s32[4]{0:T(128)}, u32[]{:S(2)}) copy-start(s32[4]{0:T(128)} %bnd_ref.1) | copy-start | bytes 52
  38.4 5.9 %collective-permute-start.6 = (bf16[4,128,128]{2,1,0:T(8,128)(2,1)S(1)}, bf16[4,128,128]{2,1,0:T(8,128)(2,1)S(1)}, u32[]{:S(2)}, u32[]{:S(2)}) collective-permute-start(bf16[4,128,128]{2,1,0:T(8,128)(2,1)S(1)} %get-tuple-element.11), channel_id=1, source_target_pairs={{0,1},{1,2},{2,3},{4,5},{5,6},{6,7},{8,9},{9,10},{10,11},{12,13},{... | collective-permute-start | bytes 393224 | tf_op jit(solution)/shard_map/ppermute | solution.py:101
  42.4 5.7 %collective-permute-start.7 = (bf16[4,128,128]{2,1,0:T(8,128)(2,1)S(1)}, bf16[4,128,128]{2,1,0:T(8,128)(2,1)S(1)}, u32[]{:S(2)}, u32[]{:S(2)}) collective-permute-start(bf16[4,128,128]{2,1,0:T(8,128)(2,1)S(1)} %get-tuple-element.11), channel_id=1, source_target_pairs={{1,0},{2,1},{3,2},{5,4},{6,5},{7,6},{9,8},{10,9},{11,10},{13,12},{... | collective-permute-start | bytes 393224 | tf_op jit(solution)/shard_map/ppermute | solution.py:101
  48.2 7.8 %collective-permute-start.8 = (bf16[12,128,128]{2,1,0:T(8,128)(2,1)S(1)}, bf16[12,128,128]{2,1,0:T(8,128)(2,1)S(1)}, u32[]{:S(2)}, u32[]{:S(2)}) collective-permute-start(bf16[12,128,128]{2,1,0:T(8,128)(2,1)S(1)} %constant_dynamic-update-slice_fusion.5), channel_id=1, source_target_pairs={{0,4},{4,8},{8,12},{12,16},{16,20},{20,24},{24,28},{28,32},{32,36}... | collective-permute-start | bytes 1179656 | tf_op jit(solution)/shard_map/ppermute | solution.py:101
  50.0 10.6 %collective-permute-start.9 = (bf16[12,128,128]{2,1,0:T(8,128)(2,1)S(1)}, bf16[12,128,128]{2,1,0:T(8,128)(2,1)S(1)}, u32[]{:S(2)}, u32[]{:S(2)}) collective-permute-start(bf16[12,128,128]{2,1,0:T(8,128)(2,1)S(1)} %constant_dynamic-update-slice_fusion.5), channel_id=1, source_target_pairs={{4,0},{8,4},{12,8},{16,12},{20,16},{24,20},{28,24},{32,28},{36,32}... | collective-permute-start | bytes 1179656 | tf_op jit(solution)/shard_map/ppermute | solution.py:101
  60.7 21.0 %collective-permute-start.11 = (bf16[36,128,128]{2,1,0:T(8,128)(2,1)S(1)}, bf16[36,128,128]{2,1,0:T(8,128)(2,1)S(1)}, u32[]{:S(2)}, u32[]{:S(2)}) collective-permute-start(bf16[36,128,128]{2,1,0:T(8,128)(2,1)S(1)} %constant_dynamic-update-slice_fusion.8.mid_ref), channel_id=1, source_target_pairs={{64,0},{128,64},{192,128},{256,192},{320,256},{384,320},{448,384},... | collective-permute-start | bytes 3538952 | tf_op jit(solution)/shard_map/ppermute | solution.py:101
  62.6 20.2 %collective-permute-start.10 = (bf16[36,128,128]{2,1,0:T(8,128)(2,1)S(1)}, bf16[36,128,128]{2,1,0:T(8,128)(2,1)S(1)}, u32[]{:S(2)}, u32[]{:S(2)}) collective-permute-start(bf16[36,128,128]{2,1,0:T(8,128)(2,1)S(1)} %constant_dynamic-update-slice_fusion.8.mid_ref), channel_id=1, source_target_pairs={{0,64},{64,128},{128,192},{192,256},{256,320},{320,384},{384,448},... | collective-permute-start | bytes 3538952 | tf_op jit(solution)/shard_map/ppermute | solution.py:101

commit v3 on v2

--- a/solution.py
+++ b/solution.py
@@ -73,18 +73,25 @@
     )(in_hbm(boundary), in_hbm(start_block))
 
 
-def hold_kernel(w_ref, held_ref, sem):
+def hold_kernel(w_ref, held_ref, keep_ref, sem):
     copy = pltpu.make_async_copy(w_ref, held_ref, sem)
     copy.start()
     copy.wait()
+    ones = jnp.ones((16, w_ref.shape[1]), BF16)
+    for i in range(w_ref.shape[0]):
+        degree = jnp.dot(ones, held_ref[i], preferred_element_type=F32)
+        keep_ref[i] = 1.0 - degree[0:8] * 0.125
 
 
 def hold_weights(tiles):
     return pl.pallas_call(
         hold_kernel,
-        out_shape=jax.ShapeDtypeStruct(tiles.shape, tiles.dtype),
+        out_shape=(
+            jax.ShapeDtypeStruct(tiles.shape, tiles.dtype),
+            jax.ShapeDtypeStruct((tiles.shape[0], 8, tiles.shape[2]), F32),
+        ),
         in_specs=[anywhere()],
-        out_specs=vmem(),
+        out_specs=(vmem(), vmem()),
         scratch_shapes=[pltpu.SemaphoreType.DMA],
         compiler_params=pltpu.CompilerParams(vmem_limit_bytes=8 * MIB),
         cost_estimate=pl.CostEstimate(
@@ -94,52 +101,89 @@
     )(in_hbm(tiles))
 
 
-def neighbours_along(block, axis):
+def partners_along(block, axis):
     count = lax.axis_size(axis)
-    forward = [(i, i + 1) for i in range(count - 1)]
-    backward = [(target, source) for source, target in forward]
-    return lax.ppermute(block, axis, forward), lax.ppermute(block, axis, backward)
-
-
-def halo(edge):
+
+    def pairs(first):
+        lows = range(first, count - 1, 2)
+        return [(i, i + 1) for i in lows] + [(i + 1, i) for i in lows]
+
+    other = lax.ppermute(block, axis, pairs(1))
+    return other, lax.ppermute(block, axis, pairs(0))
+
+
+def near_kernel(own_ref, mid_ref, pool_ref, sem):
+    blocks, listed = own_ref.shape[0], mid_ref.shape[0]
+    copies = [
+        pltpu.make_async_copy(own_ref, pool_ref.at[pl.ds(0, blocks)], sem.at[0]),
+        pltpu.make_async_copy(mid_ref, pool_ref.at[pl.ds(blocks, listed)], sem.at[1]),
+    ]
+    for copy in copies:
+        copy.start()
+    for copy in copies:
+        copy.wait()
+
+
+def near_pool(own, mid):
+    total = own.shape[0] + 3 * mid.shape[0]
+    return pl.pallas_call(
+        near_kernel,
+        out_shape=jax.ShapeDtypeStruct((total, *own.shape[1:]), own.dtype),
+        in_specs=[anywhere(), anywhere()],
+        out_specs=vmem(),
+        scratch_shapes=[pltpu.SemaphoreType.DMA((2,))],
+        compiler_params=pltpu.CompilerParams(vmem_limit_bytes=8 * MIB),
+        cost_estimate=pl.CostEstimate(
+            flops=0, bytes_accessed=4 * (own.size + mid.size), transcendentals=0
+        ),
+        name="near_pool",
+    )(own, mid)
+
+
+def halo(own, edge):
     block = edge
     for axis in ("tz", "ty"):
-        low, high = neighbours_along(block, axis)
-        block = jnp.concatenate([low, block, high], axis=0)
-    low, high = neighbours_along(block, "tx")
-    return low, block, high
-
-
-def start_fill(far_refs, pool, base, sem):
+        block = jnp.concatenate([block, *partners_along(block, axis)], axis=0)
+    other, partner = partners_along(block, "tx")
+    return near_pool(own, block), partner, other
+
+
+def fill_far(pool_ref, far_refs, sem):
+    listed = far_refs[0].shape[0]
+    base = pool_ref.shape[0] - 2 * listed
     copies = []
     for j, ref in enumerate(far_refs):
-        count = ref.shape[0]
         copies.append(
-            pltpu.make_async_copy(ref, pool.at[pl.ds(base + j * count, count)], sem.at[j])
+            pltpu.make_async_copy(ref, pool_ref.at[pl.ds(base + j * listed, listed)], sem.at[j])
         )
         copies[-1].start()
-    return copies
+    for copy in copies:
+        copy.wait()
+
+
+def pool_index(codes, blocks, listed):
+    place = codes - blocks
+    offset = place // listed
+    index = jnp.zeros_like(codes)
+    for axis, step in (("tx", 9), ("ty", 3), ("tz", 1)):
+        way = offset // step % 3
+        even = lax.axis_index(axis) % 2 == 0
+        last = jnp.where(even, 0, 2) if axis == "tx" else jnp.where(even, 2, 0)
+        index = index * 3 + jnp.where(way == 1, 0, jnp.where(way == last, 2, 1))
+    return jnp.where(codes < blocks, codes, blocks + index * listed + place % listed)
 
 
 def first_kernel(
-    nbr_ref, bnd_ref, x_ref, w_ref, low_ref, mid_ref, high_ref,
-    mixed_ref, split_ref, edge_ref, keep_ref, pool, sem,
+    nbr_ref, bnd_ref, x_ref, w_ref, keep_ref, _, partner_ref, other_ref,
+    mixed_ref, split_ref, edge_ref, pool_ref, sem,
 ):
     blocks, slots = nbr_ref.shape
     width = x_ref.shape[0]
-    fills = start_fill((low_ref, mid_ref, high_ref), pool, blocks, sem)
+    fill_far(pool_ref, (partner_ref, other_ref), sem)
     for i in range(blocks):
-        pool[i] = x_ref[:, i * 128:(i + 1) * 128].astype(BF16)
-    for copy in fills:
-        copy.wait()
-    ones = jnp.ones((16, slots * 128), BF16)
-    for i in range(blocks):
-        picked = jnp.concatenate([pool[nbr_ref[i, s]] for s in range(slots)], axis=1)
-        both = jnp.concatenate([picked, ones], axis=0)
-        out = jnp.dot(both, w_ref[i], preferred_element_type=F32)
-        keep = 1.0 - out[width:width + 8] * 0.125
-        keep_ref[i] = keep
-        mixed = x_ref[:, i * 128:(i + 1) * 128] * keep[0:1] + out[:width] * 0.125
+        picked = jnp.concatenate([pool_ref[nbr_ref[i, s]] for s in range(slots)], axis=1)
+        out = jnp.dot(picked, w_ref[i], preferred_element_type=F32)
+        mixed = x_ref[:, i * 128:(i + 1) * 128] * keep_ref[i, 0:1] + out * 0.125
         mixed_ref[i] = mixed
         head = mixed.astype(BF16)
         split_ref[i, 0:width] = head
@@ -148,27 +192,24 @@
         edge_ref[j] = split_ref[bnd_ref[j]]
 
 
-def first_step(neighbours, boundary, start_block, weights, far):
-    blocks, slots = neighbours.shape
+def first_step(index, boundary, start_block, weights, keep, far):
+    blocks = index.shape[0]
     width = start_block.shape[0]
-    total = blocks + 3 * far[0].shape[0]
     return pl.pallas_call(
         first_kernel,
         out_shape=(
             jax.ShapeDtypeStruct((blocks, width, 128), F32),
             jax.ShapeDtypeStruct((blocks, 2 * width, 128), BF16),
             jax.ShapeDtypeStruct((boundary.shape[0], 2 * width, 128), BF16),
-            jax.ShapeDtypeStruct((blocks, 8, 128), F32),
-        ),
-        in_specs=[smem(), smem(), vmem(), vmem(), anywhere(), anywhere(), anywhere()],
-        out_specs=(vmem(), vmem(), vmem(), vmem()),
-        scratch_shapes=[
-            pltpu.VMEM((total, width, 128), BF16),
-            pltpu.SemaphoreType.DMA((3,)),
-        ],
-        compiler_params=pltpu.CompilerParams(vmem_limit_bytes=24 * MIB),
+            jax.ShapeDtypeStruct(far[0].shape, BF16),
+        ),
+        in_specs=[smem(), smem()] + [vmem()] * 4 + [anywhere()] * 2,
+        out_specs=(vmem(),) * 4,
+        scratch_shapes=[pltpu.SemaphoreType.DMA((2,))],
+        input_output_aliases={5: 3},
+        compiler_params=pltpu.CompilerParams(vmem_limit_bytes=16 * MIB),
         name="first_step",
-    )(neighbours, boundary, start_block, weights, *far)
+    )(index, boundary, start_block, weights, keep, *far)[:3]
 
 
 def gram_kernel(mixed_ref, gram_ref):
@@ -197,18 +238,14 @@
 
 
 def second_kernel(
-    nbr_ref, mixed_ref, split_ref, keep_ref, w_ref, gram_ref, low_ref, mid_ref, high_ref,
-    out_ref, both_ref, pool, wide, sem,
+    nbr_ref, mixed_ref, keep_ref, w_ref, gram_ref, _, partner_ref, other_ref,
+    out_ref, both_ref, pool_ref, wide, sem,
 ):
     blocks, slots = nbr_ref.shape
     width = mixed_ref.shape[1]
-    fills = start_fill((low_ref, mid_ref, high_ref), pool, blocks, sem)
+    fill_far(pool_ref, (partner_ref, other_ref), sem)
     for i in range(blocks):
-        pool[i] = split_ref[i]
-    for copy in fills:
-        copy.wait()
-    for i in range(blocks):
-        picked = jnp.concatenate([pool[nbr_ref[i, s]] for s in range(slots)], axis=1)
+        picked = jnp.concatenate([pool_ref[nbr_ref[i, s]] for s in range(slots)], axis=1)
         out = jnp.dot(picked, w_ref[i], preferred_element_type=F32)
         mixed = mixed_ref[i] * keep_ref[i, 0:1] + (out[:width] + out[width:]) * 0.125
         out_ref[i] = mixed
@@ -216,26 +253,26 @@
     both_ref[...] = jnp.concatenate([gram_ref[...], dot_nt(wide[...], wide[...])], axis=1)
 
 
-def second_step(neighbours, mixed, split, keep, weights, gram, far):
-    blocks, slots = neighbours.shape
+def second_step(index, mixed, keep, weights, gram, far):
+    blocks = index.shape[0]
     width = mixed.shape[1]
-    total = blocks + 3 * far[0].shape[0]
     return pl.pallas_call(
         second_kernel,
         out_shape=(
             jax.ShapeDtypeStruct((blocks, width, 128), F32),
             jax.ShapeDtypeStruct((width, 2 * width), F32),
-        ),
-        in_specs=[smem()] + [vmem()] * 5 + [anywhere()] * 3,
-        out_specs=(vmem(), vmem()),
+            jax.ShapeDtypeStruct(far[0].shape, BF16),
+        ),
+        in_specs=[smem()] + [vmem()] * 5 + [anywhere()] * 2,
+        out_specs=(vmem(),) * 3,
         scratch_shapes=[
-            pltpu.VMEM((total, 2 * width, 128), BF16),
             pltpu.VMEM((width, blocks * 128), F32),
-            pltpu.SemaphoreType.DMA((3,)),
+            pltpu.SemaphoreType.DMA((2,)),
         ],
-        compiler_params=pltpu.CompilerParams(vmem_limit_bytes=24 * MIB),
+        input_output_aliases={5: 2},
+        compiler_params=pltpu.CompilerParams(vmem_limit_bytes=16 * MIB),
         name="second_step",
-    )(neighbours, mixed, split, keep, weights, gram, *far)
+    )(index, mixed, keep, weights, gram, *far)[:2]
 
 
 def sum_over_devices(values):
@@ -340,12 +377,14 @@
     blocks, slots, size, _ = weights.shape
     devices = lax.axis_size("tx") * lax.axis_size("ty") * lax.axis_size("tz")
     root_scale = float(points * devices) ** 0.5
-    tiles = hold_weights(weights.reshape(blocks, slots * size, size))
-    far = halo(take_edges(boundary, start_block))
-    mixed, split, edge, keep = first_step(neighbours, boundary, start_block, tiles, far)
-    far = halo(edge)
+    tiles, keep = hold_weights(weights.reshape(blocks, slots * size, size))
+    index = pool_index(neighbours, blocks, boundary.shape[0])
+    own = jnp.swapaxes(start_block.reshape(-1, blocks, size), 0, 1).astype(BF16)
+    far = halo(own, take_edges(boundary, start_block))
+    mixed, split, edge = first_step(index, boundary, start_block, tiles, keep, far)
+    far = halo(split, edge)
     gram = local_gram(mixed)
-    mixed, both = second_step(neighbours, mixed, split, keep, tiles, gram, far)
+    mixed, both = second_step(index, mixed, keep, tiles, gram, far)
     return finish(sum_over_devices(both), mixed, root_scale)
 
 

time: 141 us -> 138 us (0.979)
  waiting for transfers between devices: 37 us -> 25.9 us
  starting transfers between devices: 38.1 us -> 45.8 us
  blocking collectives: 51.6 us -> 50.1 us
    ppermute x12, waiting for transfers between devices: 37 us -> 25.9 us  [the longest x6 15.2 us: partners_along(): return (other, lax.ppermute(block, axis, pairs(0)))]
    ppermute x12, starting transfers between devices: 38.1 us -> 45.8 us  [the longest x6 32.8 us: partners_along(): return (other, lax.ppermute(block, axis, pairs(0)))]
    all_to_all x1, blocking collectives: 15.2 us -> 13.1 us  [sum_over_devices(): parts = lax.all_to_all(values.reshape(plane, piece, lanes), PLANE, 0, 0)]
    pallas_call x1 -> x3, Pallas kernels: 1.96 us -> 2.95 us  [the longest x1 2.49 us: hold_weights(): pl.pallas_call(hold_kernel, out_shape=(jax.ShapeDtypeStruct(tiles.shape,...]
  transfers between devices with their start and end apart: 12 -> 12, of which waited for: 11 -> 5; matrix products, arithmetic and copies ran while one was open for 0% -> 0% of each run, Pallas kernels for 2% -> 3%
where the time goes in v3:
time: 138 us; the launch traced here: 137 us
  blocking collectives  50.1 us (36%)
  starting transfers between devices  45.8 us (33%)
  waiting for transfers between devices  25.9 us (19%)
  Pallas kernels  13.1 us (9%)
    ppermute x6, starting transfers between devices, partners_along(): return (other, lax.ppermute(block, axis, pairs(0)))  32.8 us
    all_to_all x1, blocking collectives, sum_over_devices(): lax.all_to_all(jnp.broadcast_to(mine[None], (line, piece, lanes)), 'ty',...  24.9 us
    ppermute x6, waiting for transfers between devices, partners_along(): return (other, lax.ppermute(block, axis, pairs(0)))  15.2 us
    all_to_all x1, blocking collectives, sum_over_devices(): parts = lax.all_to_all(values.reshape(plane, piece, lanes), PLANE, 0, 0)  13.1 us
    ppermute x6, starting transfers between devices, partners_along(): other = lax.ppermute(block, axis, pairs(1))  13 us
    all_to_all x1, blocking collectives, sum_over_devices(): lax.all_to_all(jnp.broadcast_to(mine[None], (plane, piece, lanes)), PLANE...  12.2 us
    ppermute x6, waiting for transfers between devices, partners_along(): other = lax.ppermute(block, axis, pairs(1))  10.7 us
    pallas_call x1, Pallas kernels, finish(): pl.pallas_call(functools.partial(finish_kernel, root_scale), out_shape=(j...  2.95 us
  transfers between devices with their start and end apart: 12, of which 5 were waited for; matrix products, arithmetic and copies ran while one was open for 0% of the time, Pallas kernels for 3%

profile of v3, /device:TPU:1, one launch (start us, length us, event | category | flops | bytes accessed | tf_op | source)
XLA Modules:
  0.0 137.1 jit_solution(64443755943143455)
XLA Ops:
  0.6 0.0 copy-start.2
  0.6 1.7 %edges.1 = bf16[4,64,128]{2,1,0:T(8,128)(2,1)S(1)} custom-call(s32[4]{0:T(128)} %bnd_ref.1, f32[64,2048]{1,0:T(8,128)} %x_ref.3), custom_call_target="tpu_custom_call" | custom-call | tf_op jit(solution)/shard_map/edges/pallas_call | solution.py:60
  2.3 4.0 %collective-permute-start.1 = (bf16[4,64,128]{2,1,0:T(8,128)(2,1)S(1)}, bf16[4,64,128]{2,1,0:T(8,128)(2,1)S(1)}, u32[]{:S(2)}, u32[]{:S(2)}) collective-permute-start(bf16[4,64,128]{2,1,0:T(8,128)(2,1)S(1)} %edges.1), channel_id=1, source_target_pairs={{0,1},{2,3},{1,0},{3,2},{4,5},{6,7},{5,4},{7,6},{8,9},{10,11},{9,8... | collective-permute-start | bytes 196616 | tf_op jit(solution)/shard_map/ppermute | solution.py:112
  6.3 0.7 collective-permute-start
  7.0 1.0 collective-permute-done.1
  8.0 0.0 collective-permute-done
  8.0 3.7 %collective-permute-start.3 = (bf16[12,64,128]{2,1,0:T(8,128)(2,1)S(1)}, bf16[12,64,128]{2,1,0:T(8,128)(2,1)S(1)}, u32[]{:S(2)}, u32[]{:S(2)}) collective-permute-start(bf16[12,64,128]{2,1,0:T(8,128)(2,1)S(1)} %pad_maximum_fusion), channel_id=1, source_target_pairs={{0,4},{8,12},{16,20},{24,28},{32,36},{40,44},{48,52},{56,60},{4,0}... | collective-permute-start | bytes 589832 | tf_op jit(solution)/shard_map/ppermute | solution.py:112
  11.7 0.7 collective-permute-start.2
  12.4 0.0 collective-permute-done.2
  12.5 2.5 %collective-permute-done.3 = bf16[12,64,128]{2,1,0:T(8,128)(2,1)S(1)} collective-permute-done((bf16[12,64,128]{2,1,0:T(8,128)(2,1)S(1)}, bf16[12,64,128]{2,1,0:T(8,128)(2,1)S(1)}, u32[]{:S(2)}, u32[]{:S(2)}) %collective-permute-start.3) | collective-permute-done | bytes 196640 | tf_op jit(solution)/shard_map/ppermute | solution.py:112
  15.0 5.6 %collective-permute-start.5 = (bf16[36,64,128]{2,1,0:T(8,128)(2,1)S(1)}, bf16[36,64,128]{2,1,0:T(8,128)(2,1)S(1)}, u32[]{:S(2)}, u32[]{:S(2)}) collective-permute-start(bf16[36,64,128]{2,1,0:T(8,128)(2,1)S(1)} %constant_dynamic-update-slice_fusion.mid_ref), channel_id=1, source_target_pairs={{64,128},{192,256},{320,384},{128,64},{256,192},{384,320},{65,129}... | collective-permute-start | bytes 1769480 | tf_op jit(solution)/shard_map/ppermute | solution.py:111
  20.6 5.0 %collective-permute-start.4 = (bf16[36,64,128]{2,1,0:T(8,128)(2,1)S(1)}, bf16[36,64,128]{2,1,0:T(8,128)(2,1)S(1)}, u32[]{:S(2)}, u32[]{:S(2)}) collective-permute-start(bf16[36,64,128]{2,1,0:T(8,128)(2,1)S(1)} %constant_dynamic-update-slice_fusion.mid_ref), channel_id=1, source_target_pairs={{0,64},{128,192},{256,320},{384,448},{64,0},{192,128},{320,256},{4... | collective-permute-start | bytes 1769480 | tf_op jit(solution)/shard_map/ppermute | solution.py:112
  25.6 0.0 copy-done.2
  25.6 0.1 copy.19
  25.7 0.0 copy-start
  25.7 2.5 %hold_weights.1 = (bf16[16,768,128]{2,1,0:T(8,128)(2,1)S(1)}, f32[16,8,128]{2,1,0:T(8,128)S(1)}) custom-call(bf16[16,768,128]{2,1,0:T(8,128)(2,1)} %bitcast.12), custom_call_target="tpu_custom_call" | custom-call | bytes 6291456 | tf_op jit(solution)/shard_map/hold_weights/pallas_call | solution.py:87
  28.2 0.1 compare_select_fusion.nbr_ref
  28.3 0.0 copy-done
  28.3 0.0 copy-start.1
  28.3 0.2 near_pool.2._
  28.5 0.0 collective-permute-done.5.other_ref
  28.5 0.0 collective-permute-done.4.partner_ref
  28.5 0.5 copy-done.1
  29.0 1.7 %first_step.1 = (f32[16,64,128]{2,1,0:T(8,128)S(1)}, bf16[16,128,128]{2,1,0:T(8,128)(2,1)S(1)}, bf16[4,128,128]{2,1,0:T(8,128)(2,1)S(1)}, bf16[124,64,128]{2,1,0:T(8,128)(2,1)S(1)}) custom-call(s32[16,6]{1,0:T(8,128)S(1)} %compare_select_fusion.nbr_ref, s32[4]{0:T(128)S(1)} %copy-done.1, f32[64,2048]{1,0:T(8,128)S(1)} %copy-done, ...), custom_call_target="tpu_custom_call", output_to_operand_aliasing={{3}: (5, {})} | custom-call | tf_op jit(solution)/shard_map/first_step/pallas_call | solution.py:198
  30.7 0.7 collective-permute-start.6
  31.4 8.1 %collective-permute-start.7 = (bf16[4,128,128]{2,1,0:T(8,128)(2,1)S(1)}, bf16[4,128,128]{2,1,0:T(8,128)(2,1)S(1)}, u32[]{:S(2)}, u32[]{:S(2)}) collective-permute-start(bf16[4,128,128]{2,1,0:T(8,128)(2,1)S(1)} %get-tuple-element.13), channel_id=1, source_target_pairs={{0,1},{2,3},{1,0},{3,2},{4,5},{6,7},{5,4},{7,6},{8,9},{10,11},{9,8... | collective-permute-start | bytes 393224 | tf_op jit(solution)/shard_map/ppermute | solution.py:112
  39.5 0.0 collective-permute-done.6
  39.6 0.1 constant_dynamic-update-slice_fusion.6
  39.6 2.5 %collective-permute-done.7 = bf16[4,128,128]{2,1,0:T(8,128)(2,1)S(1)} collective-permute-done((bf16[4,128,128]{2,1,0:T(8,128)(2,1)S(1)}, bf16[4,128,128]{2,1,0:T(8,128)(2,1)S(1)}, u32[]{:S(2)}, u32[]{:S(2)}) %collective-permute-start.7) | collective-permute-done | bytes 131104 | tf_op jit(solution)/shard_map/ppermute | solution.py:112
  42.2 0.1 constant_dynamic-update-slice_fusion.5
  42.2 0.7 collective-permute-start.8
  42.9 10.1 %collective-permute-start.9 = (bf16[12,128,128]{2,1,0:T(8,128)(2,1)S(1)}, bf16[12,128,128]{2,1,0:T(8,128)(2,1)S(1)}, u32[]{:S(2)}, u32[]{:S(2)}) collective-permute-start(bf16[12,128,128]{2,1,0:T(8,128)(2,1)S(1)} %get-tuple-element.16), channel_id=1, source_target_pairs={{0,4},{8,12},{16,20},{24,28},{32,36},{40,44},{48,52},{56,60},{4,0}... | collective-permute-start | bytes 1179656 | tf_op jit(solution)/shard_map/ppermute | solution.py:112
  53.0 0.0 collective-permute-done.8
  53.0 0.1 constant_dynamic-update-slice_fusion.9
  53.1 9.3 %collective-permute-done.9 = bf16[12,128,128]{2,1,0:T(8,128)(2,1)S(1)} collective-permute-done((bf16[12,128,128]{2,1,0:T(8,128)(2,1)S(1)}, bf16[12,128,128]{2,1,0:T(8,128)(2,1)S(1)}, u32[]{:S(2)}, u32[]{:S(2)}) %collective-permute-start.9) | collective-permute-done | bytes 393248 | tf_op jit(solution)/shard_map/ppermute | solution.py:112
  62.4 0.1 constant_dynamic-update-slice_fusion.8.mid_ref
  62.4 4.7 %collective-permute-start.11 = (bf16[36,128,128]{2,1,0:T(8,128)(2,1)S(1)}, bf16[36,128,128]{2,1,0:T(8,128)(2,1)S(1)}, u32[]{:S(2)}, u32[]{:S(2)}) collective-permute-start(bf16[36,128,128]{2,1,0:T(8,128)(2,1)S(1)} %constant_dynamic-update-slice_fusion.8.mid_ref), channel_id=1, source_target_pairs={{64,128},{192,256},{320,384},{128,64},{256,192},{384,320},{65,129}... | collective-permute-start | bytes 3538952 | tf_op jit(solution)/shard_map/ppermute | solution.py:111
  67.1 1.9 %collective-permute-start.10 = (bf16[36,128,128]{2,1,0:T(8,128)(2,1)S(1)}, bf16[36,128,128]{2,1,0:T(8,128)(2,1)S(1)}, u32[]{:S(2)}, u32[]{:S(2)}) collective-permute-start(bf16[36,128,128]{2,1,0:T(8,128)(2,1)S(1)} %constant_dynamic-update-slice_fusion.8.mid_ref), channel_id=1, source_target_pairs={{0,64},{128,192},{256,320},{384,448},{64,0},{192,128},{320,256},{4... | collective-permute-start | bytes 3538952 | tf_op jit(solution)/shard_map/ppermute | solution.py:112
  69.0 0.9 first_gram.1.gram_ref
  70.0 0.3 near_pool.3._
  70.3 10.7 %collective-permute-done.11.other_ref = bf16[36,128,128]{2,1,0:T(8,128)(2,1)S(1)} collective-permute-done((bf16[36,128,128]{2,1,0:T(8,128)(2,1)S(1)}, bf16[36,128,128]{2,1,0:T(8,128)(2,1)S(1)}, u32[]{:S(2)}, u32[]{:S(2)}) %collective-permute-start.11) | collective-permute-done | bytes 1179680 | tf_op jit(solution)/shard_map/ppermute | solution.py:111
  81.0 0.0 collective-permute-done.10.partner_ref
  81.0 2.9 %second_step.1 = (f32[16,64,128]{2,1,0:T(8,128)S(1)}, f32[64,128]{1,0:T(8,128)S(1)}, bf16[124,128,128]{2,1,0:T(8,128)(2,1)S(1)}) custom-call(s32[16,6]{1,0:T(8,128)S(1)} %compare_select_fusion.nbr_ref, f32[16,64,128]{2,1,0:T(8,128)S(1)} %get-tuple-element.11.mixed_ref, ...), custom_call_target="tpu_custom_call", output_to_operand_aliasing={{2}: (5, {})} | custom-call | tf_op jit(solution)/shard_map/second_step/pallas_call | solution.py:259
  83.9 13.1 %all_to_all.15 = f32[32,2,128]{2,1,0:T(2,128)S(1)} all-to-all(f32[32,2,128]{2,1,0:T(2,128)S(1)} %bitcast.11), channel_id=1, replica_groups=mesh['tx'=8,'ty'=16,'tz'=4] {'tx','tz'}, dimensions={0} | all-to-all | bytes 65536 | tf_op jit(solution)/shard_map/all_to_all | solution.py:283
  97.0 24.9 %all_to_all.16 = f32[16,2,128]{2,1,0:T(2,128)S(1)} all-to-all(f32[16,2,128]{2,1,0:T(2,128)S(1)} %broadcast_in_dim.24), channel_id=1, replica_groups=mesh['tx'=8,'ty'=16,'tz'=4] {'ty'}, dimensions={0} | all-to-all | bytes 32768 | tf_op jit(solution)/shard_map/all_to_all | solution.py:285
  122.0 12.2 %all_to_all.17 = f32[32,2,128]{2,1,0:T(2,128)S(1)} all-to-all(f32[32,2,128]{2,1,0:T(2,128)S(1)} %broadcast_in_dim.25), channel_id=1, replica_groups=mesh['tx'=8,'ty'=16,'tz'=4] {'tx','tz'}, dimensions={0} | all-to-all | bytes 65536 | tf_op jit(solution)/shard_map/all_to_all | solution.py:287
  134.1 2.9 %finish.1 = (f32[64,2048]{1,0:T(8,128)}, f32[64,64]{1,0:T(8,128)}) custom-call(f32[64,128]{1,0:T(8,128)S(1)} %bitcast.10, f32[16,64,128]{2,1,0:T(8,128)S(1)} %get-tuple-element.15.mixed_ref), custom_call_target="tpu_custom_call" | custom-call | tf_op jit(solution)/shard_map/finish/pallas_call | solution.py:362
  (12 shorter events, 0.3 us)
Async XLA Ops:
  0.6 25.0 %copy-start.2 = (s32[16,6]{0,1:T(8,128)S(1)}, s32[16,6]{0,1:T(8,128)}, u32[]{:S(2)}) copy-start(s32[16,6]{0,1:T(8,128)} %param.6) | copy-start | bytes 1156
  2.3 5.7 %collective-permute-start.1 = (bf16[4,64,128]{2,1,0:T(8,128)(2,1)S(1)}, bf16[4,64,128]{2,1,0:T(8,128)(2,1)S(1)}, u32[]{:S(2)}, u32[]{:S(2)}) collective-permute-start(bf16[4,64,128]{2,1,0:T(8,128)(2,1)S(1)} %edges.1), channel_id=1, source_target_pairs={{0,1},{2,3},{1,0},{3,2},{4,5},{6,7},{5,4},{7,6},{8,9},{10,11},{9,8... | collective-permute-start | bytes 196616 | tf_op jit(solution)/shard_map/ppermute | solution.py:112
  6.3 1.6 %collective-permute-start = (bf16[4,64,128]{2,1,0:T(8,128)(2,1)S(1)}, bf16[4,64,128]{2,1,0:T(8,128)(2,1)S(1)}, u32[]{:S(2)}, u32[]{:S(2)}) collective-permute-start(bf16[4,64,128]{2,1,0:T(8,128)(2,1)S(1)} %edges.1), channel_id=1, source_target_pairs={{1,2},{2,1},{5,6},{6,5},{9,10},{10,9},{13,14},{14,13},{17,18},{18,... | collective-permute-start | bytes 196616 | tf_op jit(solution)/shard_map/ppermute | solution.py:111
  8.0 6.9 %collective-permute-start.3 = (bf16[12,64,128]{2,1,0:T(8,128)(2,1)S(1)}, bf16[12,64,128]{2,1,0:T(8,128)(2,1)S(1)}, u32[]{:S(2)}, u32[]{:S(2)}) collective-permute-start(bf16[12,64,128]{2,1,0:T(8,128)(2,1)S(1)} %pad_maximum_fusion), channel_id=1, source_target_pairs={{0,4},{8,12},{16,20},{24,28},{32,36},{40,44},{48,52},{56,60},{4,0}... | collective-permute-start | bytes 589832 | tf_op jit(solution)/shard_map/ppermute | solution.py:112
  11.7 0.7 collective-permute-start.2
  15.0 13.5 %collective-permute-start.5 = (bf16[36,64,128]{2,1,0:T(8,128)(2,1)S(1)}, bf16[36,64,128]{2,1,0:T(8,128)(2,1)S(1)}, u32[]{:S(2)}, u32[]{:S(2)}) collective-permute-start(bf16[36,64,128]{2,1,0:T(8,128)(2,1)S(1)} %constant_dynamic-update-slice_fusion.mid_ref), channel_id=1, source_target_pairs={{64,128},{192,256},{320,384},{128,64},{256,192},{384,320},{65,129}... | collective-permute-start | bytes 1769480 | tf_op jit(solution)/shard_map/ppermute | solution.py:111
  20.6 7.9 %collective-permute-start.4 = (bf16[36,64,128]{2,1,0:T(8,128)(2,1)S(1)}, bf16[36,64,128]{2,1,0:T(8,128)(2,1)S(1)}, u32[]{:S(2)}, u32[]{:S(2)}) collective-permute-start(bf16[36,64,128]{2,1,0:T(8,128)(2,1)S(1)} %constant_dynamic-update-slice_fusion.mid_ref), channel_id=1, source_target_pairs={{0,64},{128,192},{256,320},{384,448},{64,0},{192,128},{320,256},{4... | collective-permute-start | bytes 1769480 | tf_op jit(solution)/shard_map/ppermute | solution.py:112
  25.7 2.6 %copy-start = (f32[64,2048]{1,0:T(8,128)S(1)}, f32[64,2048]{1,0:T(8,128)}, u32[]{:S(2)}) copy-start(f32[64,2048]{1,0:T(8,128)} %x_ref.3) | copy-start | bytes 1572868
  28.3 0.7 copy-start.1
  30.7 8.8 %collective-permute-start.6 = (bf16[4,128,128]{2,1,0:T(8,128)(2,1)S(1)}, bf16[4,128,128]{2,1,0:T(8,128)(2,1)S(1)}, u32[]{:S(2)}, u32[]{:S(2)}) collective-permute-start(bf16[4,128,128]{2,1,0:T(8,128)(2,1)S(1)} %get-tuple-element.13), channel_id=1, source_target_pairs={{1,2},{2,1},{5,6},{6,5},{9,10},{10,9},{13,14},{14,13},{17,18},{18,... | collective-permute-start | bytes 393224 | tf_op jit(solution)/shard_map/ppermute | solution.py:111
  31.4 10.8 %collective-permute-start.7 = (bf16[4,128,128]{2,1,0:T(8,128)(2,1)S(1)}, bf16[4,128,128]{2,1,0:T(8,128)(2,1)S(1)}, u32[]{:S(2)}, u32[]{:S(2)}) collective-permute-start(bf16[4,128,128]{2,1,0:T(8,128)(2,1)S(1)} %get-tuple-element.13), channel_id=1, source_target_pairs={{0,1},{2,3},{1,0},{3,2},{4,5},{6,7},{5,4},{7,6},{8,9},{10,11},{9,8... | collective-permute-start | bytes 393224 | tf_op jit(solution)/shard_map/ppermute | solution.py:112
  42.2 10.8 %collective-permute-start.8 = (bf16[12,128,128]{2,1,0:T(8,128)(2,1)S(1)}, bf16[12,128,128]{2,1,0:T(8,128)(2,1)S(1)}, u32[]{:S(2)}, u32[]{:S(2)}) collective-permute-start(bf16[12,128,128]{2,1,0:T(8,128)(2,1)S(1)} %get-tuple-element.16), channel_id=1, source_target_pairs={{4,8},{12,16},{20,24},{28,32},{36,40},{44,48},{52,56},{8,4},{16,12... | collective-permute-start | bytes 1179656 | tf_op jit(solution)/shard_map/ppermute | solution.py:111
  42.9 19.4 %collective-permute-start.9 = (bf16[12,128,128]{2,1,0:T(8,128)(2,1)S(1)}, bf16[12,128,128]{2,1,0:T(8,128)(2,1)S(1)}, u32[]{:S(2)}, u32[]{:S(2)}) collective-permute-start(bf16[12,128,128]{2,1,0:T(8,128)(2,1)S(1)} %get-tuple-element.16), channel_id=1, source_target_pairs={{0,4},{8,12},{16,20},{24,28},{32,36},{40,44},{48,52},{56,60},{4,0}... | collective-permute-start | bytes 1179656 | tf_op jit(solution)/shard_map/ppermute | solution.py:112
  62.4 18.6 %collective-permute-start.11 = (bf16[36,128,128]{2,1,0:T(8,128)(2,1)S(1)}, bf16[36,128,128]{2,1,0:T(8,128)(2,1)S(1)}, u32[]{:S(2)}, u32[]{:S(2)}) collective-permute-start(bf16[36,128,128]{2,1,0:T(8,128)(2,1)S(1)} %constant_dynamic-update-slice_fusion.8.mid_ref), channel_id=1, source_target_pairs={{64,128},{192,256},{320,384},{128,64},{256,192},{384,320},{65,129}... | collective-permute-start | bytes 3538952 | tf_op jit(solution)/shard_map/ppermute | solution.py:111
  67.1 13.9 %collective-permute-start.10 = (bf16[36,128,128]{2,1,0:T(8,128)(2,1)S(1)}, bf16[36,128,128]{2,1,0:T(8,128)(2,1)S(1)}, u32[]{:S(2)}, u32[]{:S(2)}) collective-permute-start(bf16[36,128,128]{2,1,0:T(8,128)(2,1)S(1)} %constant_dynamic-update-slice_fusion.8.mid_ref), channel_id=1, source_target_pairs={{0,64},{128,192},{256,320},{384,448},{64,0},{192,128},{320,256},{4... | collective-permute-start | bytes 3538952 | tf_op jit(solution)/shard_map/ppermute | solution.py:112

commit v4 on v3

--- a/solution.py
+++ b/solution.py
@@ -13,6 +13,7 @@
 PLANE = ("tx", "tz")
 MIB = 1 << 20
 PANEL = 8
+SHARE = 0.875
 
 
 def vmem():
@@ -175,21 +176,20 @@
 
 def first_kernel(
     nbr_ref, bnd_ref, x_ref, w_ref, keep_ref, _, partner_ref, other_ref,
-    mixed_ref, split_ref, edge_ref, pool_ref, sem,
+    mixed_ref, base_ref, step_ref, edge_ref, pool_ref, sem,
 ):
     blocks, slots = nbr_ref.shape
-    width = x_ref.shape[0]
     fill_far(pool_ref, (partner_ref, other_ref), sem)
     for i in range(blocks):
         picked = jnp.concatenate([pool_ref[nbr_ref[i, s]] for s in range(slots)], axis=1)
-        out = jnp.dot(picked, w_ref[i], preferred_element_type=F32)
-        mixed = x_ref[:, i * 128:(i + 1) * 128] * keep_ref[i, 0:1] + out * 0.125
+        out = jnp.dot(picked, w_ref[i], preferred_element_type=F32) * 0.125
+        keep = keep_ref[i, 0:1]
+        mixed = x_ref[:, i * 128:(i + 1) * 128] * keep + out
         mixed_ref[i] = mixed
-        head = mixed.astype(BF16)
-        split_ref[i, 0:width] = head
-        split_ref[i, width:2 * width] = (mixed - head.astype(F32)).astype(BF16)
+        base_ref[i] = mixed * keep + out * SHARE
+        step_ref[i] = (mixed - pool_ref[i].astype(F32) * SHARE).astype(BF16)
     for j in range(edge_ref.shape[0]):
-        edge_ref[j] = split_ref[bnd_ref[j]]
+        edge_ref[j] = step_ref[bnd_ref[j]]
 
 
 def first_step(index, boundary, start_block, weights, keep, far):
@@ -199,17 +199,18 @@
         first_kernel,
         out_shape=(
             jax.ShapeDtypeStruct((blocks, width, 128), F32),
-            jax.ShapeDtypeStruct((blocks, 2 * width, 128), BF16),
-            jax.ShapeDtypeStruct((boundary.shape[0], 2 * width, 128), BF16),
+            jax.ShapeDtypeStruct((blocks, width, 128), F32),
+            jax.ShapeDtypeStruct((blocks, width, 128), BF16),
+            jax.ShapeDtypeStruct((boundary.shape[0], width, 128), BF16),
             jax.ShapeDtypeStruct(far[0].shape, BF16),
         ),
         in_specs=[smem(), smem()] + [vmem()] * 4 + [anywhere()] * 2,
-        out_specs=(vmem(),) * 4,
+        out_specs=(vmem(),) * 5,
         scratch_shapes=[pltpu.SemaphoreType.DMA((2,))],
-        input_output_aliases={5: 3},
+        input_output_aliases={5: 4},
         compiler_params=pltpu.CompilerParams(vmem_limit_bytes=16 * MIB),
         name="first_step",
-    )(index, boundary, start_block, weights, keep, *far)[:3]
+    )(index, boundary, start_block, weights, keep, *far)[:4]
 
 
 def gram_kernel(mixed_ref, gram_ref):
@@ -238,24 +239,22 @@
 
 
 def second_kernel(
-    nbr_ref, mixed_ref, keep_ref, w_ref, gram_ref, _, partner_ref, other_ref,
+    nbr_ref, base_ref, w_ref, gram_ref, _, partner_ref, other_ref,
     out_ref, both_ref, pool_ref, wide, sem,
 ):
     blocks, slots = nbr_ref.shape
-    width = mixed_ref.shape[1]
     fill_far(pool_ref, (partner_ref, other_ref), sem)
     for i in range(blocks):
         picked = jnp.concatenate([pool_ref[nbr_ref[i, s]] for s in range(slots)], axis=1)
         out = jnp.dot(picked, w_ref[i], preferred_element_type=F32)
-        mixed = mixed_ref[i] * keep_ref[i, 0:1] + (out[:width] + out[width:]) * 0.125
+        mixed = base_ref[i] + out * 0.125
         out_ref[i] = mixed
         wide[:, i * 128:(i + 1) * 128] = mixed
     both_ref[...] = jnp.concatenate([gram_ref[...], dot_nt(wide[...], wide[...])], axis=1)
 
 
-def second_step(index, mixed, keep, weights, gram, far):
-    blocks = index.shape[0]
-    width = mixed.shape[1]
+def second_step(index, base, weights, gram, far):
+    blocks, width, _ = base.shape
     return pl.pallas_call(
         second_kernel,
         out_shape=(
@@ -263,16 +262,16 @@
             jax.ShapeDtypeStruct((width, 2 * width), F32),
             jax.ShapeDtypeStruct(far[0].shape, BF16),
         ),
-        in_specs=[smem()] + [vmem()] * 5 + [anywhere()] * 2,
+        in_specs=[smem()] + [vmem()] * 4 + [anywhere()] * 2,
         out_specs=(vmem(),) * 3,
         scratch_shapes=[
             pltpu.VMEM((width, blocks * 128), F32),
             pltpu.SemaphoreType.DMA((2,)),
         ],
-        input_output_aliases={5: 2},
+        input_output_aliases={4: 2},
         compiler_params=pltpu.CompilerParams(vmem_limit_bytes=16 * MIB),
         name="second_step",
-    )(index, mixed, keep, weights, gram, *far)[:2]
+    )(index, base, weights, gram, *far)[:2]
 
 
 def sum_over_devices(values):
@@ -381,10 +380,10 @@
     index = pool_index(neighbours, blocks, boundary.shape[0])
     own = jnp.swapaxes(start_block.reshape(-1, blocks, size), 0, 1).astype(BF16)
     far = halo(own, take_edges(boundary, start_block))
-    mixed, split, edge = first_step(index, boundary, start_block, tiles, keep, far)
-    far = halo(split, edge)
+    mixed, base, step, edge = first_step(index, boundary, start_block, tiles, keep, far)
+    far = halo(step, edge)
     gram = local_gram(mixed)
-    mixed, both = second_step(index, mixed, keep, tiles, gram, far)
+    mixed, both = second_step(index, base, tiles, gram, far)
     return finish(sum_over_devices(both), mixed, root_scale)
 
 

time: 138 us -> 126 us (0.913)
  waiting for transfers between devices: 25.9 us -> 14.1 us
  blocking collectives: 50.1 us -> 54.1 us
  starting transfers between devices: 45.8 us -> 42.7 us
    ppermute x6, waiting for transfers between devices: 10.7 us -> 4.53 us  [partners_along(): other = lax.ppermute(block, axis, pairs(1))]
    ppermute x6, waiting for transfers between devices: 15.2 us -> 9.62 us  [partners_along(): return (other, lax.ppermute(block, axis, pairs(0)))]
    all_to_all x1, blocking collectives: 13.1 us -> 16.7 us  [sum_over_devices(): parts = lax.all_to_all(values.reshape(plane, piece, lanes), PLANE, 0, 0)]
    ppermute x6, starting transfers between devices: 32.8 us -> 29.4 us  [partners_along(): return (other, lax.ppermute(block, axis, pairs(0)))]
where the time goes in v4:
time: 126 us; the launch traced here: 125 us
  blocking collectives  54.1 us (43%)
  starting transfers between devices  42.7 us (34%)
  waiting for transfers between devices  14.1 us (11%)
  Pallas kernels  12.2 us (10%)
    ppermute x6, starting transfers between devices, partners_along(): return (other, lax.ppermute(block, axis, pairs(0)))  29.4 us
    all_to_all x1, blocking collectives, sum_over_devices(): lax.all_to_all(jnp.broadcast_to(mine[None], (line, piece, lanes)), 'ty',...  25.2 us
    all_to_all x1, blocking collectives, sum_over_devices(): parts = lax.all_to_all(values.reshape(plane, piece, lanes), PLANE, 0, 0)  16.7 us
    ppermute x6, starting transfers between devices, partners_along(): other = lax.ppermute(block, axis, pairs(1))  13.3 us
    all_to_all x1, blocking collectives, sum_over_devices(): lax.all_to_all(jnp.broadcast_to(mine[None], (plane, piece, lanes)), PLANE...  12.2 us
    ppermute x6, waiting for transfers between devices, partners_along(): return (other, lax.ppermute(block, axis, pairs(0)))  9.62 us
    ppermute x6, waiting for transfers between devices, partners_along(): other = lax.ppermute(block, axis, pairs(1))  4.53 us
    pallas_call x1, Pallas kernels, finish(): pl.pallas_call(functools.partial(finish_kernel, root_scale), out_shape=(j...  2.95 us
  transfers between devices with their start and end apart: 12, of which 5 were waited for; matrix products, arithmetic and copies ran while one was open for 0% of the time, Pallas kernels for 3%

profile of v4, /device:TPU:1, one launch (start us, length us, event | category | flops | bytes accessed | tf_op | source)
XLA Modules:
  0.0 125.0 jit_solution(11370110252003836240)
XLA Ops:
  0.6 0.0 copy-start.2
  0.6 1.7 %edges.1 = bf16[4,64,128]{2,1,0:T(8,128)(2,1)S(1)} custom-call(s32[4]{0:T(128)} %bnd_ref.1, f32[64,2048]{1,0:T(8,128)} %x_ref.3), custom_call_target="tpu_custom_call" | custom-call | tf_op jit(solution)/shard_map/edges/pallas_call | solution.py:61
  2.3 4.0 %collective-permute-start.1 = (bf16[4,64,128]{2,1,0:T(8,128)(2,1)S(1)}, bf16[4,64,128]{2,1,0:T(8,128)(2,1)S(1)}, u32[]{:S(2)}, u32[]{:S(2)}) collective-permute-start(bf16[4,64,128]{2,1,0:T(8,128)(2,1)S(1)} %edges.1), channel_id=1, source_target_pairs={{0,1},{2,3},{1,0},{3,2},{4,5},{6,7},{5,4},{7,6},{8,9},{10,11},{9,8... | collective-permute-start | bytes 196616 | tf_op jit(solution)/shard_map/ppermute | solution.py:113
  6.3 0.7 collective-permute-start
  7.0 1.0 collective-permute-done.1
  8.0 0.0 collective-permute-done
  8.0 3.7 %collective-permute-start.3 = (bf16[12,64,128]{2,1,0:T(8,128)(2,1)S(1)}, bf16[12,64,128]{2,1,0:T(8,128)(2,1)S(1)}, u32[]{:S(2)}, u32[]{:S(2)}) collective-permute-start(bf16[12,64,128]{2,1,0:T(8,128)(2,1)S(1)} %pad_maximum_fusion), channel_id=1, source_target_pairs={{0,4},{8,12},{16,20},{24,28},{32,36},{40,44},{48,52},{56,60},{4,0}... | collective-permute-start | bytes 589832 | tf_op jit(solution)/shard_map/ppermute | solution.py:113
  11.7 0.7 collective-permute-start.2
  12.4 0.0 copy-start
  12.5 0.0 collective-permute-done.2
  12.5 2.4 %collective-permute-done.3 = bf16[12,64,128]{2,1,0:T(8,128)(2,1)S(1)} collective-permute-done((bf16[12,64,128]{2,1,0:T(8,128)(2,1)S(1)}, bf16[12,64,128]{2,1,0:T(8,128)(2,1)S(1)}, u32[]{:S(2)}, u32[]{:S(2)}) %collective-permute-start.3) | collective-permute-done | bytes 196640 | tf_op jit(solution)/shard_map/ppermute | solution.py:113
  15.0 5.6 %collective-permute-start.5 = (bf16[36,64,128]{2,1,0:T(8,128)(2,1)S(1)}, bf16[36,64,128]{2,1,0:T(8,128)(2,1)S(1)}, u32[]{:S(2)}, u32[]{:S(2)}) collective-permute-start(bf16[36,64,128]{2,1,0:T(8,128)(2,1)S(1)} %constant_dynamic-update-slice_fusion.mid_ref), channel_id=1, source_target_pairs={{64,128},{192,256},{320,384},{128,64},{256,192},{384,320},{65,129}... | collective-permute-start | bytes 1769480 | tf_op jit(solution)/shard_map/ppermute | solution.py:112
  20.6 5.0 %collective-permute-start.4 = (bf16[36,64,128]{2,1,0:T(8,128)(2,1)S(1)}, bf16[36,64,128]{2,1,0:T(8,128)(2,1)S(1)}, u32[]{:S(2)}, u32[]{:S(2)}) collective-permute-start(bf16[36,64,128]{2,1,0:T(8,128)(2,1)S(1)} %constant_dynamic-update-slice_fusion.mid_ref), channel_id=1, source_target_pairs={{0,64},{128,192},{256,320},{384,448},{64,0},{192,128},{320,256},{4... | collective-permute-start | bytes 1769480 | tf_op jit(solution)/shard_map/ppermute | solution.py:113
  25.6 0.0 copy-done.2
  25.6 0.1 copy.19
  25.7 2.4 %hold_weights.1 = (bf16[16,768,128]{2,1,0:T(8,128)(2,1)S(1)}, f32[16,8,128]{2,1,0:T(8,128)S(1)}) custom-call(bf16[16,768,128]{2,1,0:T(8,128)(2,1)} %bitcast.12), custom_call_target="tpu_custom_call" | custom-call | bytes 6291456 | tf_op jit(solution)/shard_map/hold_weights/pallas_call | solution.py:88
  28.2 0.0 copy-start.1
  28.2 0.1 compare_select_fusion.nbr_ref
  28.2 0.0 copy-done
  28.3 0.2 near_pool.2._
  28.5 0.0 collective-permute-done.5.other_ref
  28.5 0.0 collective-permute-done.4.partner_ref
  28.5 0.3 copy-done.1
  28.8 1.7 %first_step.1 = (f32[16,64,128]{2,1,0:T(8,128)S(1)}, f32[16,64,128]{2,1,0:T(8,128)S(1)}, bf16[16,64,128]{2,1,0:T(8,128)(2,1)S(1)}, bf16[4,64,128]{2,1,0:T(8,128)(2,1)S(1)}, bf16[124,64,128]{2,1,0:T(8,128)(2,1)S(1)}) custom-call(s32[16,6]{1,0:T(8,128)S(1)} %compare_select_fusion.nbr_ref, s32[4]{0:T(128)S(1)} %copy-done.1, ...), custom_call_target="tpu_custom_call", output_to_operand_aliasing={{4}: (5, {})} | custom-call | tf_op jit(solution)/shard_map/first_step/pallas_call | solution.py:198
  30.5 5.6 %collective-permute-start.7 = (bf16[4,64,128]{2,1,0:T(8,128)(2,1)S(1)}, bf16[4,64,128]{2,1,0:T(8,128)(2,1)S(1)}, u32[]{:S(2)}, u32[]{:S(2)}) collective-permute-start(bf16[4,64,128]{2,1,0:T(8,128)(2,1)S(1)} %get-tuple-element.15), channel_id=1, source_target_pairs={{0,1},{2,3},{1,0},{3,2},{4,5},{6,7},{5,4},{7,6},{8,9},{10,11},{9,8... | collective-permute-start | bytes 196616 | tf_op jit(solution)/shard_map/ppermute | solution.py:113
  36.1 0.7 collective-permute-start.6
  36.8 0.0 collective-permute-done.6
  36.8 1.7 %collective-permute-done.7 = bf16[4,64,128]{2,1,0:T(8,128)(2,1)S(1)} collective-permute-done((bf16[4,64,128]{2,1,0:T(8,128)(2,1)S(1)}, bf16[4,64,128]{2,1,0:T(8,128)(2,1)S(1)}, u32[]{:S(2)}, u32[]{:S(2)}) %collective-permute-start.7) | collective-permute-done | bytes 65568 | tf_op jit(solution)/shard_map/ppermute | solution.py:113
  38.6 0.7 collective-permute-start.8
  39.3 9.2 %collective-permute-start.9 = (bf16[12,64,128]{2,1,0:T(8,128)(2,1)S(1)}, bf16[12,64,128]{2,1,0:T(8,128)(2,1)S(1)}, u32[]{:S(2)}, u32[]{:S(2)}) collective-permute-start(bf16[12,64,128]{2,1,0:T(8,128)(2,1)S(1)} %get-tuple-element.18), channel_id=1, source_target_pairs={{0,4},{8,12},{16,20},{24,28},{32,36},{40,44},{48,52},{56,60},{4,0}... | collective-permute-start | bytes 589832 | tf_op jit(solution)/shard_map/ppermute | solution.py:113
  48.5 0.0 collective-permute-done.8
  48.6 4.5 %collective-permute-done.9 = bf16[12,64,128]{2,1,0:T(8,128)(2,1)S(1)} collective-permute-done((bf16[12,64,128]{2,1,0:T(8,128)(2,1)S(1)}, bf16[12,64,128]{2,1,0:T(8,128)(2,1)S(1)}, u32[]{:S(2)}, u32[]{:S(2)}) %collective-permute-start.9) | collective-permute-done | bytes 196640 | tf_op jit(solution)/shard_map/ppermute | solution.py:113
  53.1 5.0 %collective-permute-start.11 = (bf16[36,64,128]{2,1,0:T(8,128)(2,1)S(1)}, bf16[36,64,128]{2,1,0:T(8,128)(2,1)S(1)}, u32[]{:S(2)}, u32[]{:S(2)}) collective-permute-start(bf16[36,64,128]{2,1,0:T(8,128)(2,1)S(1)} %constant_dynamic-update-slice_fusion.8.mid_ref), channel_id=1, source_target_pairs={{64,128},{192,256},{320,384},{128,64},{256,192},{384,320},{65,129}... | collective-permute-start | bytes 1769480 | tf_op jit(solution)/shard_map/ppermute | solution.py:112
  58.1 1.9 %collective-permute-start.10 = (bf16[36,64,128]{2,1,0:T(8,128)(2,1)S(1)}, bf16[36,64,128]{2,1,0:T(8,128)(2,1)S(1)}, u32[]{:S(2)}, u32[]{:S(2)}) collective-permute-start(bf16[36,64,128]{2,1,0:T(8,128)(2,1)S(1)} %constant_dynamic-update-slice_fusion.8.mid_ref), channel_id=1, source_target_pairs={{0,64},{128,192},{256,320},{384,448},{64,0},{192,128},{320,256},{4... | collective-permute-start | bytes 1769480 | tf_op jit(solution)/shard_map/ppermute | solution.py:113
  60.0 0.9 first_gram.1.gram_ref
  61.0 0.2 near_pool.3._
  61.1 4.5 %collective-permute-done.11.other_ref = bf16[36,64,128]{2,1,0:T(8,128)(2,1)S(1)} collective-permute-done((bf16[36,64,128]{2,1,0:T(8,128)(2,1)S(1)}, bf16[36,64,128]{2,1,0:T(8,128)(2,1)S(1)}, u32[]{:S(2)}, u32[]{:S(2)}) %collective-permute-start.11) | collective-permute-done | bytes 589856 | tf_op jit(solution)/shard_map/ppermute | solution.py:112
  65.7 0.0 collective-permute-done.10.partner_ref
  65.7 2.2 %second_step.1 = (f32[16,64,128]{2,1,0:T(8,128)S(1)}, f32[64,128]{1,0:T(8,128)S(1)}, bf16[124,64,128]{2,1,0:T(8,128)(2,1)S(1)}) custom-call(s32[16,6]{1,0:T(8,128)S(1)} %compare_select_fusion.nbr_ref, f32[16,64,128]{2,1,0:T(8,128)S(1)} %get-tuple-element.12.base_ref, ...), custom_call_target="tpu_custom_call", output_to_operand_aliasing={{2}: (4, {})} | custom-call | tf_op jit(solution)/shard_map/second_step/pallas_call | solution.py:258
  67.9 16.7 %all_to_all.15 = f32[32,2,128]{2,1,0:T(2,128)S(1)} all-to-all(f32[32,2,128]{2,1,0:T(2,128)S(1)} %bitcast.11), channel_id=1, replica_groups=mesh['tx'=8,'ty'=16,'tz'=4] {'tx','tz'}, dimensions={0} | all-to-all | bytes 65536 | tf_op jit(solution)/shard_map/all_to_all | solution.py:282
  84.7 25.2 %all_to_all.16 = f32[16,2,128]{2,1,0:T(2,128)S(1)} all-to-all(f32[16,2,128]{2,1,0:T(2,128)S(1)} %broadcast_in_dim.24), channel_id=1, replica_groups=mesh['tx'=8,'ty'=16,'tz'=4] {'ty'}, dimensions={0} | all-to-all | bytes 32768 | tf_op jit(solution)/shard_map/all_to_all | solution.py:284
  109.9 12.2 %all_to_all.17 = f32[32,2,128]{2,1,0:T(2,128)S(1)} all-to-all(f32[32,2,128]{2,1,0:T(2,128)S(1)} %broadcast_in_dim.25), channel_id=1, replica_groups=mesh['tx'=8,'ty'=16,'tz'=4] {'tx','tz'}, dimensions={0} | all-to-all | bytes 65536 | tf_op jit(solution)/shard_map/all_to_all | solution.py:286
  122.0 2.9 %finish.1 = (f32[64,2048]{1,0:T(8,128)}, f32[64,64]{1,0:T(8,128)}) custom-call(f32[64,128]{1,0:T(8,128)S(1)} %bitcast.10, f32[16,64,128]{2,1,0:T(8,128)S(1)} %get-tuple-element.17.mixed_ref), custom_call_target="tpu_custom_call" | custom-call | tf_op jit(solution)/shard_map/finish/pallas_call | solution.py:361
  (16 shorter events, 0.4 us)
Async XLA Ops:
  0.6 25.0 %copy-start.2 = (s32[16,6]{0,1:T(8,128)S(1)}, s32[16,6]{0,1:T(8,128)}, u32[]{:S(2)}) copy-start(s32[16,6]{0,1:T(8,128)} %param.6) | copy-start | bytes 1156
  2.3 5.7 %collective-permute-start.1 = (bf16[4,64,128]{2,1,0:T(8,128)(2,1)S(1)}, bf16[4,64,128]{2,1,0:T(8,128)(2,1)S(1)}, u32[]{:S(2)}, u32[]{:S(2)}) collective-permute-start(bf16[4,64,128]{2,1,0:T(8,128)(2,1)S(1)} %edges.1), channel_id=1, source_target_pairs={{0,1},{2,3},{1,0},{3,2},{4,5},{6,7},{5,4},{7,6},{8,9},{10,11},{9,8... | collective-permute-start | bytes 196616 | tf_op jit(solution)/shard_map/ppermute | solution.py:113
  6.3 1.6 %collective-permute-start = (bf16[4,64,128]{2,1,0:T(8,128)(2,1)S(1)}, bf16[4,64,128]{2,1,0:T(8,128)(2,1)S(1)}, u32[]{:S(2)}, u32[]{:S(2)}) collective-permute-start(bf16[4,64,128]{2,1,0:T(8,128)(2,1)S(1)} %edges.1), channel_id=1, source_target_pairs={{1,2},{2,1},{5,6},{6,5},{9,10},{10,9},{13,14},{14,13},{17,18},{18,... | collective-permute-start | bytes 196616 | tf_op jit(solution)/shard_map/ppermute | solution.py:112
  8.0 6.9 %collective-permute-start.3 = (bf16[12,64,128]{2,1,0:T(8,128)(2,1)S(1)}, bf16[12,64,128]{2,1,0:T(8,128)(2,1)S(1)}, u32[]{:S(2)}, u32[]{:S(2)}) collective-permute-start(bf16[12,64,128]{2,1,0:T(8,128)(2,1)S(1)} %pad_maximum_fusion), channel_id=1, source_target_pairs={{0,4},{8,12},{16,20},{24,28},{32,36},{40,44},{48,52},{56,60},{4,0}... | collective-permute-start | bytes 589832 | tf_op jit(solution)/shard_map/ppermute | solution.py:113
  11.7 0.7 collective-permute-start.2
  12.4 15.8 %copy-start = (f32[64,2048]{1,0:T(8,128)S(1)}, f32[64,2048]{1,0:T(8,128)}, u32[]{:S(2)}) copy-start(f32[64,2048]{1,0:T(8,128)} %x_ref.3) | copy-start | bytes 1572868
  15.0 13.5 %collective-permute-start.5 = (bf16[36,64,128]{2,1,0:T(8,128)(2,1)S(1)}, bf16[36,64,128]{2,1,0:T(8,128)(2,1)S(1)}, u32[]{:S(2)}, u32[]{:S(2)}) collective-permute-start(bf16[36,64,128]{2,1,0:T(8,128)(2,1)S(1)} %constant_dynamic-update-slice_fusion.mid_ref), channel_id=1, source_target_pairs={{64,128},{192,256},{320,384},{128,64},{256,192},{384,320},{65,129}... | collective-permute-start | bytes 1769480 | tf_op jit(solution)/shard_map/ppermute | solution.py:112
  20.6 7.9 %collective-permute-start.4 = (bf16[36,64,128]{2,1,0:T(8,128)(2,1)S(1)}, bf16[36,64,128]{2,1,0:T(8,128)(2,1)S(1)}, u32[]{:S(2)}, u32[]{:S(2)}) collective-permute-start(bf16[36,64,128]{2,1,0:T(8,128)(2,1)S(1)} %constant_dynamic-update-slice_fusion.mid_ref), channel_id=1, source_target_pairs={{0,64},{128,192},{256,320},{384,448},{64,0},{192,128},{320,256},{4... | collective-permute-start | bytes 1769480 | tf_op jit(solution)/shard_map/ppermute | solution.py:113
  28.2 0.7 copy-start.1
  30.5 8.0 %collective-permute-start.7 = (bf16[4,64,128]{2,1,0:T(8,128)(2,1)S(1)}, bf16[4,64,128]{2,1,0:T(8,128)(2,1)S(1)}, u32[]{:S(2)}, u32[]{:S(2)}) collective-permute-start(bf16[4,64,128]{2,1,0:T(8,128)(2,1)S(1)} %get-tuple-element.15), channel_id=1, source_target_pairs={{0,1},{2,3},{1,0},{3,2},{4,5},{6,7},{5,4},{7,6},{8,9},{10,11},{9,8... | collective-permute-start | bytes 196616 | tf_op jit(solution)/shard_map/ppermute | solution.py:113
  36.1 0.7 collective-permute-start.6
  38.6 9.9 %collective-permute-start.8 = (bf16[12,64,128]{2,1,0:T(8,128)(2,1)S(1)}, bf16[12,64,128]{2,1,0:T(8,128)(2,1)S(1)}, u32[]{:S(2)}, u32[]{:S(2)}) collective-permute-start(bf16[12,64,128]{2,1,0:T(8,128)(2,1)S(1)} %get-tuple-element.18), channel_id=1, source_target_pairs={{4,8},{12,16},{20,24},{28,32},{36,40},{44,48},{52,56},{8,4},{16,12... | collective-permute-start | bytes 589832 | tf_op jit(solution)/shard_map/ppermute | solution.py:112
  39.3 13.8 %collective-permute-start.9 = (bf16[12,64,128]{2,1,0:T(8,128)(2,1)S(1)}, bf16[12,64,128]{2,1,0:T(8,128)(2,1)S(1)}, u32[]{:S(2)}, u32[]{:S(2)}) collective-permute-start(bf16[12,64,128]{2,1,0:T(8,128)(2,1)S(1)} %get-tuple-element.18), channel_id=1, source_target_pairs={{0,4},{8,12},{16,20},{24,28},{32,36},{40,44},{48,52},{56,60},{4,0}... | collective-permute-start | bytes 589832 | tf_op jit(solution)/shard_map/ppermute | solution.py:113
  53.1 12.6 %collective-permute-start.11 = (bf16[36,64,128]{2,1,0:T(8,128)(2,1)S(1)}, bf16[36,64,128]{2,1,0:T(8,128)(2,1)S(1)}, u32[]{:S(2)}, u32[]{:S(2)}) collective-permute-start(bf16[36,64,128]{2,1,0:T(8,128)(2,1)S(1)} %constant_dynamic-update-slice_fusion.8.mid_ref), channel_id=1, source_target_pairs={{64,128},{192,256},{320,384},{128,64},{256,192},{384,320},{65,129}... | collective-permute-start | bytes 1769480 | tf_op jit(solution)/shard_map/ppermute | solution.py:112
  58.1 7.6 %collective-permute-start.10 = (bf16[36,64,128]{2,1,0:T(8,128)(2,1)S(1)}, bf16[36,64,128]{2,1,0:T(8,128)(2,1)S(1)}, u32[]{:S(2)}, u32[]{:S(2)}) collective-permute-start(bf16[36,64,128]{2,1,0:T(8,128)(2,1)S(1)} %constant_dynamic-update-slice_fusion.8.mid_ref), channel_id=1, source_target_pairs={{0,64},{128,192},{256,320},{384,448},{64,0},{192,128},{320,256},{4... | collective-permute-start | bytes 1769480 | tf_op jit(solution)/shard_map/ppermute | solution.py:113

commit v5 on v4

--- a/solution.py
+++ b/solution.py
@@ -38,21 +38,18 @@
     )
 
 
-def edge_kernel(list_ref, x_ref, edge_ref, bnd_ref, held, list_sem, sem):
-    count = edge_ref.shape[0]
-    listing = pltpu.make_async_copy(list_ref, bnd_ref, list_sem)
-    listing.start()
-    listing.wait()
-    copies = []
-    for j in range(count):
+def edge_kernel(list_ref, x_ref, edge_ref, bnd_ref, held, sem):
+    copies = [
+        pltpu.make_async_copy(list_ref, bnd_ref, sem.at[0]),
+        pltpu.make_async_copy(x_ref, held, sem.at[1]),
+    ]
+    for copy in copies:
+        copy.start()
+    for copy in copies:
+        copy.wait()
+    for j in range(edge_ref.shape[0]):
         start = pl.multiple_of(bnd_ref[j] * 128, 128)
-        copies.append(
-            pltpu.make_async_copy(x_ref.at[:, pl.ds(start, 128)], held.at[j], sem.at[j])
-        )
-        copies[-1].start()
-    for j in range(count):
-        copies[j].wait()
-        edge_ref[j] = held[j].astype(BF16)
+        edge_ref[j] = held[:, pl.ds(start, 128)].astype(BF16)
 
 
 def take_edges(boundary, start_block):
@@ -65,9 +62,8 @@
         out_specs=vmem(),
         scratch_shapes=[
             pltpu.SMEM((count,), jnp.int32),
-            pltpu.VMEM((count, width, 128), F32),
-            pltpu.SemaphoreType.DMA,
-            pltpu.SemaphoreType.DMA((count,)),
+            pltpu.VMEM(start_block.shape, F32),
+            pltpu.SemaphoreType.DMA((2,)),
         ],
         compiler_params=pltpu.CompilerParams(vmem_limit_bytes=2 * MIB),
         name="edges",
@@ -174,43 +170,80 @@
     return jnp.where(codes < blocks, codes, blocks + index * listed + place % listed)
 
 
+def gather_sum(table_ref, pool_ref, w_ref, slots, i):
+    picked = [pool_ref[table_ref[i * slots + s]] for s in range(slots)]
+    return jnp.dot(jnp.concatenate(picked, axis=1), w_ref[i], preferred_element_type=F32)
+
+
+def first_row(slots, table_ref, x_ref, w_ref, keep_ref, pool_ref, i, lanes):
+    out = gather_sum(table_ref, pool_ref, w_ref, slots, i) * 0.125
+    keep = keep_ref[i, 0:1]
+    mixed = x_ref[:, lanes] * keep + out
+    step = (mixed - pool_ref[i].astype(F32) * SHARE).astype(BF16)
+    return mixed, mixed * keep + out * SHARE, step
+
+
+def listed_kernel(
+    slots, table_ref, x_ref, w_ref, keep_ref, _, partner_ref, other_ref,
+    edge_ref, pool_ref, sem,
+):
+    fill_far(pool_ref, (partner_ref, other_ref), sem)
+    first = w_ref.shape[0] * slots
+    for j in range(edge_ref.shape[0]):
+        i = table_ref[first + j]
+        lanes = pl.ds(pl.multiple_of(i * 128, 128), 128)
+        edge_ref[j] = first_row(slots, table_ref, x_ref, w_ref, keep_ref, pool_ref, i, lanes)[2]
+
+
+def listed_rows(table, count, start_block, weights, keep, far):
+    blocks, depth, size = weights.shape
+    width = start_block.shape[0]
+    return pl.pallas_call(
+        functools.partial(listed_kernel, depth // size),
+        out_shape=(
+            jax.ShapeDtypeStruct((count, width, size), BF16),
+            jax.ShapeDtypeStruct(far[0].shape, BF16),
+        ),
+        in_specs=[smem()] + [vmem()] * 4 + [anywhere()] * 2,
+        out_specs=(vmem(),) * 2,
+        scratch_shapes=[pltpu.SemaphoreType.DMA((2,))],
+        input_output_aliases={4: 1},
+        compiler_params=pltpu.CompilerParams(vmem_limit_bytes=16 * MIB),
+        name="listed_rows",
+    )(table, start_block, weights, keep, *far)
+
+
 def first_kernel(
-    nbr_ref, bnd_ref, x_ref, w_ref, keep_ref, _, partner_ref, other_ref,
-    mixed_ref, base_ref, step_ref, edge_ref, pool_ref, sem,
+    slots, table_ref, x_ref, w_ref, keep_ref, pool_ref, mixed_ref, base_ref, step_ref
 ):
-    blocks, slots = nbr_ref.shape
-    fill_far(pool_ref, (partner_ref, other_ref), sem)
-    for i in range(blocks):
-        picked = jnp.concatenate([pool_ref[nbr_ref[i, s]] for s in range(slots)], axis=1)
-        out = jnp.dot(picked, w_ref[i], preferred_element_type=F32) * 0.125
-        keep = keep_ref[i, 0:1]
-        mixed = x_ref[:, i * 128:(i + 1) * 128] * keep + out
-        mixed_ref[i] = mixed
-        base_ref[i] = mixed * keep + out * SHARE
-        step_ref[i] = (mixed - pool_ref[i].astype(F32) * SHARE).astype(BF16)
-    for j in range(edge_ref.shape[0]):
-        edge_ref[j] = step_ref[bnd_ref[j]]
-
-
-def first_step(index, boundary, start_block, weights, keep, far):
-    blocks = index.shape[0]
+    for i in range(w_ref.shape[0]):
+        lanes = slice(i * 128, (i + 1) * 128)
+        mixed_ref[i], base_ref[i], step_ref[i] = first_row(
+            slots, table_ref, x_ref, w_ref, keep_ref, pool_ref, i, lanes
+        )
+
+
+def first_step(table, start_block, weights, keep, pool):
+    blocks, depth, size = weights.shape
     width = start_block.shape[0]
-    return pl.pallas_call(
-        first_kernel,
+    shape = (blocks, width, size)
+    return pl.pallas_call(
+        functools.partial(first_kernel, depth // size),
         out_shape=(
-            jax.ShapeDtypeStruct((blocks, width, 128), F32),
-            jax.ShapeDtypeStruct((blocks, width, 128), F32),
-            jax.ShapeDtypeStruct((blocks, width, 128), BF16),
-            jax.ShapeDtypeStruct((boundary.shape[0], width, 128), BF16),
-            jax.ShapeDtypeStruct(far[0].shape, BF16),
-        ),
-        in_specs=[smem(), smem()] + [vmem()] * 4 + [anywhere()] * 2,
-        out_specs=(vmem(),) * 5,
-        scratch_shapes=[pltpu.SemaphoreType.DMA((2,))],
-        input_output_aliases={5: 4},
+            jax.ShapeDtypeStruct(shape, F32),
+            jax.ShapeDtypeStruct(shape, F32),
+            jax.ShapeDtypeStruct(shape, BF16),
+        ),
+        in_specs=[smem()] + [vmem()] * 4,
+        out_specs=(vmem(),) * 3,
         compiler_params=pltpu.CompilerParams(vmem_limit_bytes=16 * MIB),
+        cost_estimate=pl.CostEstimate(
+            flops=2 * width * blocks * depth * size,
+            bytes_accessed=2 * weights.size,
+            transcendentals=0,
+        ),
         name="first_step",
-    )(index, boundary, start_block, weights, keep, *far)[:4]
+    )(table, start_block, weights, keep, pool)
 
 
 def gram_kernel(mixed_ref, gram_ref):
@@ -239,24 +272,21 @@
 
 
 def second_kernel(
-    nbr_ref, base_ref, w_ref, gram_ref, _, partner_ref, other_ref,
+    slots, table_ref, base_ref, w_ref, gram_ref, _, partner_ref, other_ref,
     out_ref, both_ref, pool_ref, wide, sem,
 ):
-    blocks, slots = nbr_ref.shape
     fill_far(pool_ref, (partner_ref, other_ref), sem)
-    for i in range(blocks):
-        picked = jnp.concatenate([pool_ref[nbr_ref[i, s]] for s in range(slots)], axis=1)
-        out = jnp.dot(picked, w_ref[i], preferred_element_type=F32)
-        mixed = base_ref[i] + out * 0.125
+    for i in range(w_ref.shape[0]):
+        mixed = base_ref[i] + gather_sum(table_ref, pool_ref, w_ref, slots, i) * 0.125
         out_ref[i] = mixed
         wide[:, i * 128:(i + 1) * 128] = mixed
     both_ref[...] = jnp.concatenate([gram_ref[...], dot_nt(wide[...], wide[...])], axis=1)
 
 
-def second_step(index, base, weights, gram, far):
+def second_step(table, base, weights, gram, far):
     blocks, width, _ = base.shape
     return pl.pallas_call(
-        second_kernel,
+        functools.partial(second_kernel, weights.shape[1] // weights.shape[2]),
         out_shape=(
             jax.ShapeDtypeStruct((blocks, width, 128), F32),
             jax.ShapeDtypeStruct((width, 2 * width), F32),
@@ -271,7 +301,7 @@
         input_output_aliases={4: 2},
         compiler_params=pltpu.CompilerParams(vmem_limit_bytes=16 * MIB),
         name="second_step",
-    )(index, base, weights, gram, *far)[:2]
+    )(table, base, weights, gram, *far)[:2]
 
 
 def sum_over_devices(values):
@@ -377,13 +407,16 @@
     devices = lax.axis_size("tx") * lax.axis_size("ty") * lax.axis_size("tz")
     root_scale = float(points * devices) ** 0.5
     tiles, keep = hold_weights(weights.reshape(blocks, slots * size, size))
-    index = pool_index(neighbours, blocks, boundary.shape[0])
+    listed = boundary.shape[0]
+    index = pool_index(neighbours, blocks, listed)
+    table = jnp.concatenate([index.reshape(-1), boundary])
     own = jnp.swapaxes(start_block.reshape(-1, blocks, size), 0, 1).astype(BF16)
     far = halo(own, take_edges(boundary, start_block))
-    mixed, base, step, edge = first_step(index, boundary, start_block, tiles, keep, far)
+    edge, pool = listed_rows(table, listed, start_block, tiles, keep, far)
+    mixed, base, step = first_step(table, start_block, tiles, keep, pool)
     far = halo(step, edge)
     gram = local_gram(mixed)
-    mixed, both = second_step(index, base, tiles, gram, far)
+    mixed, both = second_step(table, base, tiles, gram, far)
     return finish(sum_over_devices(both), mixed, root_scale)
 
 

time: 126 us -> 124 us (0.984)
  waiting for transfers between devices: 14.1 us -> 12.6 us
    ppermute x6, waiting for transfers between devices: 4.53 us -> 3.22 us  [partners_along(): other = lax.ppermute(block, axis, pairs(1))]
    pallas_call x2 -> x3, Pallas kernels: 3.92 us -> 4.45 us  [the longest x1 2.05 us: second_step(): pl.pallas_call(functools.partial(second_kernel, weights.shape[1] // weigh...]
  transfers between devices with their start and end apart: 12 -> 12, of which waited for: 5 -> 5; matrix products, arithmetic and copies ran while one was open for 0% -> 0% of each run, Pallas kernels for 3% -> 4%
where the time goes in v5:
time: 124 us
  blocking collectives  54 us (44%)
  starting transfers between devices  43.1 us (35%)
  waiting for transfers between devices  12.6 us (10%)
  Pallas kernels  12.2 us (10%)
    ppermute x6, starting transfers between devices, partners_along(): return (other, lax.ppermute(block, axis, pairs(0)))  29.6 us
    all_to_all x1, blocking collectives, sum_over_devices(): lax.all_to_all(jnp.broadcast_to(mine[None], (line, piece, lanes)), 'ty',...  25.2 us
    all_to_all x1, blocking collectives, sum_over_devices(): parts = lax.all_to_all(values.reshape(plane, piece, lanes), PLANE, 0, 0)  16.7 us
    ppermute x6, starting transfers between devices, partners_along(): other = lax.ppermute(block, axis, pairs(1))  13.5 us
    all_to_all x1, blocking collectives, sum_over_devices(): lax.all_to_all(jnp.broadcast_to(mine[None], (plane, piece, lanes)), PLANE...  12.2 us
    ppermute x6, waiting for transfers between devices, partners_along(): return (other, lax.ppermute(block, axis, pairs(0)))  9.43 us
    ppermute x6, waiting for transfers between devices, partners_along(): other = lax.ppermute(block, axis, pairs(1))  3.22 us
    pallas_call x1, Pallas kernels, finish(): pl.pallas_call(functools.partial(finish_kernel, root_scale), out_shape=(j...  2.95 us
  transfers between devices with their start and end apart: 12, of which 5 were waited for; matrix products, arithmetic and copies ran while one was open for 0% of the time, Pallas kernels for 4%

profile of v5, /device:TPU:1, one launch (start us, length us, event | category | flops | bytes accessed | tf_op | source)
XLA Modules:
  0.0 123.6 jit_solution(2485854604896832631)
XLA Ops:
  0.6 0.0 copy-start.1
  0.6 1.1 edges.1
  1.7 4.0 %collective-permute-start.1 = (bf16[4,64,128]{2,1,0:T(8,128)(2,1)S(1)}, bf16[4,64,128]{2,1,0:T(8,128)(2,1)S(1)}, u32[]{:S(2)}, u32[]{:S(2)}) collective-permute-start(bf16[4,64,128]{2,1,0:T(8,128)(2,1)S(1)} %edges.1), channel_id=1, source_target_pairs={{0,1},{2,3},{1,0},{3,2},{4,5},{6,7},{5,4},{7,6},{8,9},{10,11},{9,8... | collective-permute-start | bytes 196616 | tf_op jit(solution)/shard_map/ppermute | solution.py:109
  5.8 0.7 collective-permute-start
  6.5 1.0 collective-permute-done.1
  7.4 0.0 collective-permute-done
  7.4 3.7 %collective-permute-start.3 = (bf16[12,64,128]{2,1,0:T(8,128)(2,1)S(1)}, bf16[12,64,128]{2,1,0:T(8,128)(2,1)S(1)}, u32[]{:S(2)}, u32[]{:S(2)}) collective-permute-start(bf16[12,64,128]{2,1,0:T(8,128)(2,1)S(1)} %pad_maximum_fusion), channel_id=1, source_target_pairs={{0,4},{8,12},{16,20},{24,28},{32,36},{40,44},{48,52},{56,60},{4,0}... | collective-permute-start | bytes 589832 | tf_op jit(solution)/shard_map/ppermute | solution.py:109
  11.2 0.7 collective-permute-start.2
  11.9 0.0 copy-start.2
  11.9 0.0 copy-start
  11.9 0.0 collective-permute-done.2
  11.9 2.4 %collective-permute-done.3 = bf16[12,64,128]{2,1,0:T(8,128)(2,1)S(1)} collective-permute-done((bf16[12,64,128]{2,1,0:T(8,128)(2,1)S(1)}, bf16[12,64,128]{2,1,0:T(8,128)(2,1)S(1)}, u32[]{:S(2)}, u32[]{:S(2)}) %collective-permute-start.3) | collective-permute-done | bytes 196640 | tf_op jit(solution)/shard_map/ppermute | solution.py:109
  14.4 5.6 %collective-permute-start.5 = (bf16[36,64,128]{2,1,0:T(8,128)(2,1)S(1)}, bf16[36,64,128]{2,1,0:T(8,128)(2,1)S(1)}, u32[]{:S(2)}, u32[]{:S(2)}) collective-permute-start(bf16[36,64,128]{2,1,0:T(8,128)(2,1)S(1)} %constant_dynamic-update-slice_fusion.mid_ref), channel_id=1, source_target_pairs={{64,128},{192,256},{320,384},{128,64},{256,192},{384,320},{65,129}... | collective-permute-start | bytes 1769480 | tf_op jit(solution)/shard_map/ppermute | solution.py:108
  20.0 5.0 %collective-permute-start.4 = (bf16[36,64,128]{2,1,0:T(8,128)(2,1)S(1)}, bf16[36,64,128]{2,1,0:T(8,128)(2,1)S(1)}, u32[]{:S(2)}, u32[]{:S(2)}) collective-permute-start(bf16[36,64,128]{2,1,0:T(8,128)(2,1)S(1)} %constant_dynamic-update-slice_fusion.mid_ref), channel_id=1, source_target_pairs={{0,64},{128,192},{256,320},{384,448},{64,0},{192,128},{320,256},{4... | collective-permute-start | bytes 1769480 | tf_op jit(solution)/shard_map/ppermute | solution.py:109
  25.1 0.0 copy-done.1
  25.1 0.1 copy.13
  25.2 0.1 reshape.20
  25.3 2.4 %hold_weights.1 = (bf16[16,768,128]{2,1,0:T(8,128)(2,1)S(1)}, f32[16,8,128]{2,1,0:T(8,128)S(1)}) custom-call(bf16[16,768,128]{2,1,0:T(8,128)(2,1)} %bitcast.12), custom_call_target="tpu_custom_call" | custom-call | bytes 6291456 | tf_op jit(solution)/shard_map/hold_weights/pallas_call | solution.py:84
  27.7 0.0 copy-done.2
  27.7 0.1 pad_add_fusion.table_ref
  27.8 0.0 copy-done
  27.9 0.2 near_pool.2._
  28.0 0.0 collective-permute-done.5.other_ref
  28.0 0.0 collective-permute-done.4.partner_ref
  28.1 1.1 listed_rows.1
  29.2 5.6 %collective-permute-start.7 = (bf16[4,64,128]{2,1,0:T(8,128)(2,1)S(1)}, bf16[4,64,128]{2,1,0:T(8,128)(2,1)S(1)}, u32[]{:S(2)}, u32[]{:S(2)}) collective-permute-start(bf16[4,64,128]{2,1,0:T(8,128)(2,1)S(1)} %get-tuple-element.17), channel_id=1, source_target_pairs={{0,1},{2,3},{1,0},{3,2},{4,5},{6,7},{5,4},{7,6},{8,9},{10,11},{9,8... | collective-permute-start | bytes 196616 | tf_op jit(solution)/shard_map/ppermute | solution.py:109
  34.7 0.7 collective-permute-start.6
  35.4 0.0 collective-permute-done.6
  35.5 1.7 %collective-permute-done.7 = bf16[4,64,128]{2,1,0:T(8,128)(2,1)S(1)} collective-permute-done((bf16[4,64,128]{2,1,0:T(8,128)(2,1)S(1)}, bf16[4,64,128]{2,1,0:T(8,128)(2,1)S(1)}, u32[]{:S(2)}, u32[]{:S(2)}) %collective-permute-start.7) | collective-permute-done | bytes 65568 | tf_op jit(solution)/shard_map/ppermute | solution.py:109
  37.2 0.7 collective-permute-start.8
  37.9 9.4 %collective-permute-start.9 = (bf16[12,64,128]{2,1,0:T(8,128)(2,1)S(1)}, bf16[12,64,128]{2,1,0:T(8,128)(2,1)S(1)}, u32[]{:S(2)}, u32[]{:S(2)}) collective-permute-start(bf16[12,64,128]{2,1,0:T(8,128)(2,1)S(1)} %get-tuple-element.20), channel_id=1, source_target_pairs={{0,4},{8,12},{16,20},{24,28},{32,36},{40,44},{48,52},{56,60},{4,0}... | collective-permute-start | bytes 589832 | tf_op jit(solution)/shard_map/ppermute | solution.py:109
  47.3 0.0 collective-permute-done.8
  47.4 4.3 %collective-permute-done.9 = bf16[12,64,128]{2,1,0:T(8,128)(2,1)S(1)} collective-permute-done((bf16[12,64,128]{2,1,0:T(8,128)(2,1)S(1)}, bf16[12,64,128]{2,1,0:T(8,128)(2,1)S(1)}, u32[]{:S(2)}, u32[]{:S(2)}) %collective-permute-start.9) | collective-permute-done | bytes 196640 | tf_op jit(solution)/shard_map/ppermute | solution.py:109
  51.7 5.2 %collective-permute-start.11 = (bf16[36,64,128]{2,1,0:T(8,128)(2,1)S(1)}, bf16[36,64,128]{2,1,0:T(8,128)(2,1)S(1)}, u32[]{:S(2)}, u32[]{:S(2)}) collective-permute-start(bf16[36,64,128]{2,1,0:T(8,128)(2,1)S(1)} %constant_dynamic-update-slice_fusion.8.mid_ref), channel_id=1, source_target_pairs={{64,128},{192,256},{320,384},{128,64},{256,192},{384,320},{65,129}... | collective-permute-start | bytes 1769480 | tf_op jit(solution)/shard_map/ppermute | solution.py:108
  56.9 1.9 %collective-permute-start.10 = (bf16[36,64,128]{2,1,0:T(8,128)(2,1)S(1)}, bf16[36,64,128]{2,1,0:T(8,128)(2,1)S(1)}, u32[]{:S(2)}, u32[]{:S(2)}) collective-permute-start(bf16[36,64,128]{2,1,0:T(8,128)(2,1)S(1)} %constant_dynamic-update-slice_fusion.8.mid_ref), channel_id=1, source_target_pairs={{0,64},{128,192},{256,320},{384,448},{64,0},{192,128},{320,256},{4... | collective-permute-start | bytes 1769480 | tf_op jit(solution)/shard_map/ppermute | solution.py:109
  58.9 1.3 %first_step.1 = (f32[16,64,128]{2,1,0:T(8,128)S(1)}, f32[16,64,128]{2,1,0:T(8,128)S(1)}, bf16[16,64,128]{2,1,0:T(8,128)(2,1)S(1)}) custom-call(s32[100]{0:T(128)S(1)} %pad_add_fusion.table_ref, f32[64,2048]{1,0:T(8,128)S(1)} %copy-done, bf16[16,768,128]{2,1,0:T(8,128)(2,1)S(1)} %get-tuple-element.11.w_ref, f32[16,8,128]{2,1,0:T(8,128)S(1)} %get-tuple-element.12.keep_ref, ...), custom_call_target="tpu_custom_call" | custom-call | flops 201326592 | bytes 3145728 | tf_op jit(solution)/shard_map/first_step/pallas_call | solution.py:230
  60.2 0.9 first_gram.1.gram_ref
  61.1 0.2 near_pool.3._
  61.3 3.2 %collective-permute-done.11.other_ref = bf16[36,64,128]{2,1,0:T(8,128)(2,1)S(1)} collective-permute-done((bf16[36,64,128]{2,1,0:T(8,128)(2,1)S(1)}, bf16[36,64,128]{2,1,0:T(8,128)(2,1)S(1)}, u32[]{:S(2)}, u32[]{:S(2)}) %collective-permute-start.11) | collective-permute-done | bytes 589856 | tf_op jit(solution)/shard_map/ppermute | solution.py:108
  64.5 0.0 collective-permute-done.10.partner_ref
  64.5 2.1 %second_step.1 = (f32[16,64,128]{2,1,0:T(8,128)S(1)}, f32[64,128]{1,0:T(8,128)S(1)}, bf16[124,64,128]{2,1,0:T(8,128)(2,1)S(1)}) custom-call(s32[100]{0:T(128)S(1)} %pad_add_fusion.table_ref, f32[16,64,128]{2,1,0:T(8,128)S(1)} %get-tuple-element.14.base_ref, bf16[16,768,128]{2,1,0:T(8,128)(2,1)S(1)} %get-tuple-element.11.w_ref, ...), custom_call_target="tpu_custom_call", output_to_operand_aliasing={{2}: (4, {})} | custom-call | tf_op jit(solution)/shard_map/second_step/pallas_call | solution.py:288
  66.5 16.7 %all_to_all.15 = f32[32,2,128]{2,1,0:T(2,128)S(1)} all-to-all(f32[32,2,128]{2,1,0:T(2,128)S(1)} %bitcast.11), channel_id=1, replica_groups=mesh['tx'=8,'ty'=16,'tz'=4] {'tx','tz'}, dimensions={0} | all-to-all | bytes 65536 | tf_op jit(solution)/shard_map/all_to_all | solution.py:312
  83.3 25.2 %all_to_all.16 = f32[16,2,128]{2,1,0:T(2,128)S(1)} all-to-all(f32[16,2,128]{2,1,0:T(2,128)S(1)} %broadcast_in_dim.24), channel_id=1, replica_groups=mesh['tx'=8,'ty'=16,'tz'=4] {'ty'}, dimensions={0} | all-to-all | bytes 32768 | tf_op jit(solution)/shard_map/all_to_all | solution.py:314
  108.5 12.2 %all_to_all.17 = f32[32,2,128]{2,1,0:T(2,128)S(1)} all-to-all(f32[32,2,128]{2,1,0:T(2,128)S(1)} %broadcast_in_dim.25), channel_id=1, replica_groups=mesh['tx'=8,'ty'=16,'tz'=4] {'tx','tz'}, dimensions={0} | all-to-all | bytes 65536 | tf_op jit(solution)/shard_map/all_to_all | solution.py:316
  120.7 2.9 %finish.1 = (f32[64,2048]{1,0:T(8,128)}, f32[64,64]{1,0:T(8,128)}) custom-call(f32[64,128]{1,0:T(8,128)S(1)} %bitcast.10, f32[16,64,128]{2,1,0:T(8,128)S(1)} %get-tuple-element.19.mixed_ref), custom_call_target="tpu_custom_call" | custom-call | tf_op jit(solution)/shard_map/finish/pallas_call | solution.py:391
  (17 shorter events, 0.4 us)
Async XLA Ops:
  0.6 24.4 %copy-start.1 = (s32[16,6]{0,1:T(8,128)S(1)}, s32[16,6]{0,1:T(8,128)}, u32[]{:S(2)}) copy-start(s32[16,6]{0,1:T(8,128)} %param.6) | copy-start | bytes 1156
  1.7 5.7 %collective-permute-start.1 = (bf16[4,64,128]{2,1,0:T(8,128)(2,1)S(1)}, bf16[4,64,128]{2,1,0:T(8,128)(2,1)S(1)}, u32[]{:S(2)}, u32[]{:S(2)}) collective-permute-start(bf16[4,64,128]{2,1,0:T(8,128)(2,1)S(1)} %edges.1), channel_id=1, source_target_pairs={{0,1},{2,3},{1,0},{3,2},{4,5},{6,7},{5,4},{7,6},{8,9},{10,11},{9,8... | collective-permute-start | bytes 196616 | tf_op jit(solution)/shard_map/ppermute | solution.py:109
  5.8 1.6 %collective-permute-start = (bf16[4,64,128]{2,1,0:T(8,128)(2,1)S(1)}, bf16[4,64,128]{2,1,0:T(8,128)(2,1)S(1)}, u32[]{:S(2)}, u32[]{:S(2)}) collective-permute-start(bf16[4,64,128]{2,1,0:T(8,128)(2,1)S(1)} %edges.1), channel_id=1, source_target_pairs={{1,2},{2,1},{5,6},{6,5},{9,10},{10,9},{13,14},{14,13},{17,18},{18,... | collective-permute-start | bytes 196616 | tf_op jit(solution)/shard_map/ppermute | solution.py:108
  7.4 6.9 %collective-permute-start.3 = (bf16[12,64,128]{2,1,0:T(8,128)(2,1)S(1)}, bf16[12,64,128]{2,1,0:T(8,128)(2,1)S(1)}, u32[]{:S(2)}, u32[]{:S(2)}) collective-permute-start(bf16[12,64,128]{2,1,0:T(8,128)(2,1)S(1)} %pad_maximum_fusion), channel_id=1, source_target_pairs={{0,4},{8,12},{16,20},{24,28},{32,36},{40,44},{48,52},{56,60},{4,0}... | collective-permute-start | bytes 589832 | tf_op jit(solution)/shard_map/ppermute | solution.py:109
  11.2 0.7 collective-permute-start.2
  11.9 15.8 %copy-start.2 = (s32[4]{0:T(128)S(1)}, s32[4]{0:T(128)}, u32[]{:S(2)}) copy-start(s32[4]{0:T(128)} %list_ref.1) | copy-start | bytes 52
  11.9 15.9 %copy-start = (f32[64,2048]{1,0:T(8,128)S(1)}, f32[64,2048]{1,0:T(8,128)}, u32[]{:S(2)}) copy-start(f32[64,2048]{1,0:T(8,128)} %x_ref.5) | copy-start | bytes 1572868
  14.4 13.6 %collective-permute-start.5 = (bf16[36,64,128]{2,1,0:T(8,128)(2,1)S(1)}, bf16[36,64,128]{2,1,0:T(8,128)(2,1)S(1)}, u32[]{:S(2)}, u32[]{:S(2)}) collective-permute-start(bf16[36,64,128]{2,1,0:T(8,128)(2,1)S(1)} %constant_dynamic-update-slice_fusion.mid_ref), channel_id=1, source_target_pairs={{64,128},{192,256},{320,384},{128,64},{256,192},{384,320},{65,129}... | collective-permute-start | bytes 1769480 | tf_op jit(solution)/shard_map/ppermute | solution.py:108
  20.0 8.0 %collective-permute-start.4 = (bf16[36,64,128]{2,1,0:T(8,128)(2,1)S(1)}, bf16[36,64,128]{2,1,0:T(8,128)(2,1)S(1)}, u32[]{:S(2)}, u32[]{:S(2)}) collective-permute-start(bf16[36,64,128]{2,1,0:T(8,128)(2,1)S(1)} %constant_dynamic-update-slice_fusion.mid_ref), channel_id=1, source_target_pairs={{0,64},{128,192},{256,320},{384,448},{64,0},{192,128},{320,256},{4... | collective-permute-start | bytes 1769480 | tf_op jit(solution)/shard_map/ppermute | solution.py:109
  29.2 8.0 %collective-permute-start.7 = (bf16[4,64,128]{2,1,0:T(8,128)(2,1)S(1)}, bf16[4,64,128]{2,1,0:T(8,128)(2,1)S(1)}, u32[]{:S(2)}, u32[]{:S(2)}) collective-permute-start(bf16[4,64,128]{2,1,0:T(8,128)(2,1)S(1)} %get-tuple-element.17), channel_id=1, source_target_pairs={{0,1},{2,3},{1,0},{3,2},{4,5},{6,7},{5,4},{7,6},{8,9},{10,11},{9,8... | collective-permute-start | bytes 196616 | tf_op jit(solution)/shard_map/ppermute | solution.py:109
  34.7 0.7 collective-permute-start.6
  37.2 10.1 %collective-permute-start.8 = (bf16[12,64,128]{2,1,0:T(8,128)(2,1)S(1)}, bf16[12,64,128]{2,1,0:T(8,128)(2,1)S(1)}, u32[]{:S(2)}, u32[]{:S(2)}) collective-permute-start(bf16[12,64,128]{2,1,0:T(8,128)(2,1)S(1)} %get-tuple-element.20), channel_id=1, source_target_pairs={{4,8},{12,16},{20,24},{28,32},{36,40},{44,48},{52,56},{8,4},{16,12... | collective-permute-start | bytes 589832 | tf_op jit(solution)/shard_map/ppermute | solution.py:108
  37.9 13.8 %collective-permute-start.9 = (bf16[12,64,128]{2,1,0:T(8,128)(2,1)S(1)}, bf16[12,64,128]{2,1,0:T(8,128)(2,1)S(1)}, u32[]{:S(2)}, u32[]{:S(2)}) collective-permute-start(bf16[12,64,128]{2,1,0:T(8,128)(2,1)S(1)} %get-tuple-element.20), channel_id=1, source_target_pairs={{0,4},{8,12},{16,20},{24,28},{32,36},{40,44},{48,52},{56,60},{4,0}... | collective-permute-start | bytes 589832 | tf_op jit(solution)/shard_map/ppermute | solution.py:109
  51.7 12.7 %collective-permute-start.11 = (bf16[36,64,128]{2,1,0:T(8,128)(2,1)S(1)}, bf16[36,64,128]{2,1,0:T(8,128)(2,1)S(1)}, u32[]{:S(2)}, u32[]{:S(2)}) collective-permute-start(bf16[36,64,128]{2,1,0:T(8,128)(2,1)S(1)} %constant_dynamic-update-slice_fusion.8.mid_ref), channel_id=1, source_target_pairs={{64,128},{192,256},{320,384},{128,64},{256,192},{384,320},{65,129}... | collective-permute-start | bytes 1769480 | tf_op jit(solution)/shard_map/ppermute | solution.py:108
  56.9 7.6 %collective-permute-start.10 = (bf16[36,64,128]{2,1,0:T(8,128)(2,1)S(1)}, bf16[36,64,128]{2,1,0:T(8,128)(2,1)S(1)}, u32[]{:S(2)}, u32[]{:S(2)}) collective-permute-start(bf16[36,64,128]{2,1,0:T(8,128)(2,1)S(1)} %constant_dynamic-update-slice_fusion.8.mid_ref), channel_id=1, source_target_pairs={{0,64},{128,192},{256,320},{384,448},{64,0},{192,128},{320,256},{4... | collective-permute-start | bytes 1769480 | tf_op jit(solution)/shard_map/ppermute | solution.py:109

commit v6 on v5

--- a/solution.py
+++ b/solution.py
@@ -306,14 +306,14 @@
 
 def sum_over_devices(values):
     rows, lanes = values.shape
-    plane = lax.axis_size("tx") * lax.axis_size("tz")
-    line = lax.axis_size("ty")
-    piece = rows // plane
-    parts = lax.all_to_all(values.reshape(plane, piece, lanes), PLANE, 0, 0)
+    along, deep, line = (lax.axis_size(axis) for axis in ("tx", "tz", "ty"))
+    shape = (rows // along, lanes)
+    parts = jnp.broadcast_to(values.reshape(along, 1, *shape), (along, deep, *shape))
+    parts = lax.all_to_all(parts.reshape(along * deep, *shape), PLANE, 0, 0)
     mine = jnp.sum(parts, axis=0)
-    parts = lax.all_to_all(jnp.broadcast_to(mine[None], (line, piece, lanes)), "ty", 0, 0)
+    parts = lax.all_to_all(jnp.broadcast_to(mine[None], (line, *shape)), "ty", 0, 0)
     mine = jnp.sum(parts, axis=0)
-    parts = lax.all_to_all(jnp.broadcast_to(mine[None], (plane, piece, lanes)), PLANE, 0, 0)
+    parts = lax.all_to_all(jnp.broadcast_to(mine[None], (along, *shape)), "tx", 0, 0)
     return parts.reshape(rows, lanes)
 
 

time: 124 us -> 122 us (0.984)
  blocking collectives: 54 us -> 51.7 us
    all_to_all x3, blocking collectives: 54 us -> 51.7 us  [the longest x1 25.3 us: sum_over_devices(): lax.all_to_all(jnp.broadcast_to(mine[None], (line, *shape)), 'ty', 0, 0)]
where the time goes in v6:
time: 122 us; the launch traced here: 121 us
  blocking collectives  51.7 us (42%)
  starting transfers between devices  43.1 us (35%)
  waiting for transfers between devices  12.6 us (10%)
  Pallas kernels  12.2 us (10%)
    ppermute x6, starting transfers between devices, partners_along(): return (other, lax.ppermute(block, axis, pairs(0)))  29.6 us
    all_to_all x1, blocking collectives, sum_over_devices(): lax.all_to_all(jnp.broadcast_to(mine[None], (line, *shape)), 'ty', 0, 0)  25.3 us
    all_to_all x1, blocking collectives, sum_over_devices(): parts = lax.all_to_all(parts.reshape(along * deep, *shape), PLANE, 0, 0)  17.1 us
    ppermute x6, starting transfers between devices, partners_along(): other = lax.ppermute(block, axis, pairs(1))  13.5 us
    ppermute x6, waiting for transfers between devices, partners_along(): return (other, lax.ppermute(block, axis, pairs(0)))  9.43 us
    all_to_all x1, blocking collectives, sum_over_devices(): lax.all_to_all(jnp.broadcast_to(mine[None], (along, *shape)), 'tx', 0, 0)  9.31 us
    ppermute x6, waiting for transfers between devices, partners_along(): other = lax.ppermute(block, axis, pairs(1))  3.22 us
    pallas_call x1, Pallas kernels, finish(): pl.pallas_call(functools.partial(finish_kernel, root_scale), out_shape=(j...  2.95 us
  transfers between devices with their start and end apart: 12, of which 5 were waited for; matrix products, arithmetic and copies ran while one was open for 0% of the time, Pallas kernels for 4%

profile of v6, /device:TPU:1, one launch (start us, length us, event | category | flops | bytes accessed | tf_op | source)
XLA Modules:
  0.0 121.3 jit_solution(6413336852031363252)
XLA Ops:
  0.6 0.0 copy-start.1
  0.6 1.1 edges.1
  1.7 4.0 %collective-permute-start.1 = (bf16[4,64,128]{2,1,0:T(8,128)(2,1)S(1)}, bf16[4,64,128]{2,1,0:T(8,128)(2,1)S(1)}, u32[]{:S(2)}, u32[]{:S(2)}) collective-permute-start(bf16[4,64,128]{2,1,0:T(8,128)(2,1)S(1)} %edges.1), channel_id=1, source_target_pairs={{0,1},{2,3},{1,0},{3,2},{4,5},{6,7},{5,4},{7,6},{8,9},{10,11},{9,8... | collective-permute-start | bytes 196616 | tf_op jit(solution)/shard_map/ppermute | solution.py:109
  5.8 0.7 collective-permute-start
  6.5 1.0 collective-permute-done.1
  7.4 0.0 collective-permute-done
  7.4 3.7 %collective-permute-start.3 = (bf16[12,64,128]{2,1,0:T(8,128)(2,1)S(1)}, bf16[12,64,128]{2,1,0:T(8,128)(2,1)S(1)}, u32[]{:S(2)}, u32[]{:S(2)}) collective-permute-start(bf16[12,64,128]{2,1,0:T(8,128)(2,1)S(1)} %pad_maximum_fusion), channel_id=1, source_target_pairs={{0,4},{8,12},{16,20},{24,28},{32,36},{40,44},{48,52},{56,60},{4,0}... | collective-permute-start | bytes 589832 | tf_op jit(solution)/shard_map/ppermute | solution.py:109
  11.2 0.7 collective-permute-start.2
  11.9 0.0 copy-start.2
  11.9 0.0 copy-start
  11.9 0.0 collective-permute-done.2
  11.9 2.4 %collective-permute-done.3 = bf16[12,64,128]{2,1,0:T(8,128)(2,1)S(1)} collective-permute-done((bf16[12,64,128]{2,1,0:T(8,128)(2,1)S(1)}, bf16[12,64,128]{2,1,0:T(8,128)(2,1)S(1)}, u32[]{:S(2)}, u32[]{:S(2)}) %collective-permute-start.3) | collective-permute-done | bytes 196640 | tf_op jit(solution)/shard_map/ppermute | solution.py:109
  14.4 5.6 %collective-permute-start.5 = (bf16[36,64,128]{2,1,0:T(8,128)(2,1)S(1)}, bf16[36,64,128]{2,1,0:T(8,128)(2,1)S(1)}, u32[]{:S(2)}, u32[]{:S(2)}) collective-permute-start(bf16[36,64,128]{2,1,0:T(8,128)(2,1)S(1)} %constant_dynamic-update-slice_fusion.mid_ref), channel_id=1, source_target_pairs={{64,128},{192,256},{320,384},{128,64},{256,192},{384,320},{65,129}... | collective-permute-start | bytes 1769480 | tf_op jit(solution)/shard_map/ppermute | solution.py:108
  20.0 5.0 %collective-permute-start.4 = (bf16[36,64,128]{2,1,0:T(8,128)(2,1)S(1)}, bf16[36,64,128]{2,1,0:T(8,128)(2,1)S(1)}, u32[]{:S(2)}, u32[]{:S(2)}) collective-permute-start(bf16[36,64,128]{2,1,0:T(8,128)(2,1)S(1)} %constant_dynamic-update-slice_fusion.mid_ref), channel_id=1, source_target_pairs={{0,64},{128,192},{256,320},{384,448},{64,0},{192,128},{320,256},{4... | collective-permute-start | bytes 1769480 | tf_op jit(solution)/shard_map/ppermute | solution.py:109
  25.1 0.0 copy-done.1
  25.1 0.1 copy.11
  25.2 0.1 reshape.22
  25.3 2.4 %hold_weights.1 = (bf16[16,768,128]{2,1,0:T(8,128)(2,1)S(1)}, f32[16,8,128]{2,1,0:T(8,128)S(1)}) custom-call(bf16[16,768,128]{2,1,0:T(8,128)(2,1)} %bitcast.13), custom_call_target="tpu_custom_call" | custom-call | bytes 6291456 | tf_op jit(solution)/shard_map/hold_weights/pallas_call | solution.py:84
  27.7 0.0 copy-done.2
  27.7 0.1 pad_add_fusion.table_ref
  27.8 0.0 copy-done
  27.9 0.2 near_pool.2._
  28.0 0.0 collective-permute-done.5.other_ref
  28.0 0.0 collective-permute-done.4.partner_ref
  28.1 1.1 listed_rows.1
  29.2 5.6 %collective-permute-start.7 = (bf16[4,64,128]{2,1,0:T(8,128)(2,1)S(1)}, bf16[4,64,128]{2,1,0:T(8,128)(2,1)S(1)}, u32[]{:S(2)}, u32[]{:S(2)}) collective-permute-start(bf16[4,64,128]{2,1,0:T(8,128)(2,1)S(1)} %get-tuple-element.17), channel_id=1, source_target_pairs={{0,1},{2,3},{1,0},{3,2},{4,5},{6,7},{5,4},{7,6},{8,9},{10,11},{9,8... | collective-permute-start | bytes 196616 | tf_op jit(solution)/shard_map/ppermute | solution.py:109
  34.7 0.7 collective-permute-start.6
  35.4 0.0 collective-permute-done.6
  35.5 1.7 %collective-permute-done.7 = bf16[4,64,128]{2,1,0:T(8,128)(2,1)S(1)} collective-permute-done((bf16[4,64,128]{2,1,0:T(8,128)(2,1)S(1)}, bf16[4,64,128]{2,1,0:T(8,128)(2,1)S(1)}, u32[]{:S(2)}, u32[]{:S(2)}) %collective-permute-start.7) | collective-permute-done | bytes 65568 | tf_op jit(solution)/shard_map/ppermute | solution.py:109
  37.2 0.7 collective-permute-start.8
  37.9 9.4 %collective-permute-start.9 = (bf16[12,64,128]{2,1,0:T(8,128)(2,1)S(1)}, bf16[12,64,128]{2,1,0:T(8,128)(2,1)S(1)}, u32[]{:S(2)}, u32[]{:S(2)}) collective-permute-start(bf16[12,64,128]{2,1,0:T(8,128)(2,1)S(1)} %get-tuple-element.20), channel_id=1, source_target_pairs={{0,4},{8,12},{16,20},{24,28},{32,36},{40,44},{48,52},{56,60},{4,0}... | collective-permute-start | bytes 589832 | tf_op jit(solution)/shard_map/ppermute | solution.py:109
  47.3 0.0 collective-permute-done.8
  47.4 4.3 %collective-permute-done.9 = bf16[12,64,128]{2,1,0:T(8,128)(2,1)S(1)} collective-permute-done((bf16[12,64,128]{2,1,0:T(8,128)(2,1)S(1)}, bf16[12,64,128]{2,1,0:T(8,128)(2,1)S(1)}, u32[]{:S(2)}, u32[]{:S(2)}) %collective-permute-start.9) | collective-permute-done | bytes 196640 | tf_op jit(solution)/shard_map/ppermute | solution.py:109
  51.7 5.2 %collective-permute-start.11 = (bf16[36,64,128]{2,1,0:T(8,128)(2,1)S(1)}, bf16[36,64,128]{2,1,0:T(8,128)(2,1)S(1)}, u32[]{:S(2)}, u32[]{:S(2)}) collective-permute-start(bf16[36,64,128]{2,1,0:T(8,128)(2,1)S(1)} %constant_dynamic-update-slice_fusion.8.mid_ref), channel_id=1, source_target_pairs={{64,128},{192,256},{320,384},{128,64},{256,192},{384,320},{65,129}... | collective-permute-start | bytes 1769480 | tf_op jit(solution)/shard_map/ppermute | solution.py:108
  56.9 1.9 %collective-permute-start.10 = (bf16[36,64,128]{2,1,0:T(8,128)(2,1)S(1)}, bf16[36,64,128]{2,1,0:T(8,128)(2,1)S(1)}, u32[]{:S(2)}, u32[]{:S(2)}) collective-permute-start(bf16[36,64,128]{2,1,0:T(8,128)(2,1)S(1)} %constant_dynamic-update-slice_fusion.8.mid_ref), channel_id=1, source_target_pairs={{0,64},{128,192},{256,320},{384,448},{64,0},{192,128},{320,256},{4... | collective-permute-start | bytes 1769480 | tf_op jit(solution)/shard_map/ppermute | solution.py:109
  58.9 1.3 %first_step.1 = (f32[16,64,128]{2,1,0:T(8,128)S(1)}, f32[16,64,128]{2,1,0:T(8,128)S(1)}, bf16[16,64,128]{2,1,0:T(8,128)(2,1)S(1)}) custom-call(s32[100]{0:T(128)S(1)} %pad_add_fusion.table_ref, f32[64,2048]{1,0:T(8,128)S(1)} %copy-done, bf16[16,768,128]{2,1,0:T(8,128)(2,1)S(1)} %get-tuple-element.11.w_ref, f32[16,8,128]{2,1,0:T(8,128)S(1)} %get-tuple-element.12.keep_ref, ...), custom_call_target="tpu_custom_call" | custom-call | flops 201326592 | bytes 3145728 | tf_op jit(solution)/shard_map/first_step/pallas_call | solution.py:230
  60.2 0.9 first_gram.1.gram_ref
  61.1 0.2 near_pool.3._
  61.3 3.2 %collective-permute-done.11.other_ref = bf16[36,64,128]{2,1,0:T(8,128)(2,1)S(1)} collective-permute-done((bf16[36,64,128]{2,1,0:T(8,128)(2,1)S(1)}, bf16[36,64,128]{2,1,0:T(8,128)(2,1)S(1)}, u32[]{:S(2)}, u32[]{:S(2)}) %collective-permute-start.11) | collective-permute-done | bytes 589856 | tf_op jit(solution)/shard_map/ppermute | solution.py:108
  64.5 0.0 collective-permute-done.10.partner_ref
  64.5 2.1 %second_step.1 = (f32[16,64,128]{2,1,0:T(8,128)S(1)}, f32[64,128]{1,0:T(8,128)S(1)}, bf16[124,64,128]{2,1,0:T(8,128)(2,1)S(1)}) custom-call(s32[100]{0:T(128)S(1)} %pad_add_fusion.table_ref, f32[16,64,128]{2,1,0:T(8,128)S(1)} %get-tuple-element.14.base_ref, bf16[16,768,128]{2,1,0:T(8,128)(2,1)S(1)} %get-tuple-element.11.w_ref, ...), custom_call_target="tpu_custom_call", output_to_operand_aliasing={{2}: (4, {})} | custom-call | tf_op jit(solution)/shard_map/second_step/pallas_call | solution.py:288
  66.6 17.1 %all_to_all.15 = f32[32,8,128]{2,1,0:T(8,128)S(1)} all-to-all(f32[32,8,128]{2,1,0:T(8,128)S(1)} %bitcast.14), channel_id=1, replica_groups=mesh['tx'=8,'ty'=16,'tz'=4] {'tx','tz'}, dimensions={0} | all-to-all | bytes 262144 | tf_op jit(solution)/shard_map/all_to_all | solution.py:312
  83.7 25.3 %all_to_all.16 = f32[16,8,128]{2,1,0:T(8,128)S(1)} all-to-all(f32[16,8,128]{2,1,0:T(8,128)S(1)} %broadcast_in_dim.33), channel_id=1, replica_groups=mesh['tx'=8,'ty'=16,'tz'=4] {'ty'}, dimensions={0} | all-to-all | bytes 131072 | tf_op jit(solution)/shard_map/all_to_all | solution.py:314
  109.1 9.3 %all_to_all.17 = f32[8,8,128]{2,1,0:T(8,128)S(1)} all-to-all(f32[8,8,128]{2,1,0:T(8,128)S(1)} %broadcast_in_dim.34), channel_id=1, replica_groups=mesh['tx'=8,'ty'=16,'tz'=4] {'tx'}, dimensions={0} | all-to-all | bytes 65536 | tf_op jit(solution)/shard_map/all_to_all | solution.py:316
  118.4 2.9 %finish.1 = (f32[64,2048]{1,0:T(8,128)}, f32[64,64]{1,0:T(8,128)}) custom-call(f32[64,128]{1,0:T(8,128)S(1)} %bitcast.11, f32[16,64,128]{2,1,0:T(8,128)S(1)} %get-tuple-element.19.mixed_ref), custom_call_target="tpu_custom_call" | custom-call | tf_op jit(solution)/shard_map/finish/pallas_call | solution.py:391
  (18 shorter events, 0.4 us)
Async XLA Ops:
  0.6 24.4 %copy-start.1 = (s32[16,6]{0,1:T(8,128)S(1)}, s32[16,6]{0,1:T(8,128)}, u32[]{:S(2)}) copy-start(s32[16,6]{0,1:T(8,128)} %param.6) | copy-start | bytes 1156
  1.7 5.7 %collective-permute-start.1 = (bf16[4,64,128]{2,1,0:T(8,128)(2,1)S(1)}, bf16[4,64,128]{2,1,0:T(8,128)(2,1)S(1)}, u32[]{:S(2)}, u32[]{:S(2)}) collective-permute-start(bf16[4,64,128]{2,1,0:T(8,128)(2,1)S(1)} %edges.1), channel_id=1, source_target_pairs={{0,1},{2,3},{1,0},{3,2},{4,5},{6,7},{5,4},{7,6},{8,9},{10,11},{9,8... | collective-permute-start | bytes 196616 | tf_op jit(solution)/shard_map/ppermute | solution.py:109
  5.8 1.6 %collective-permute-start = (bf16[4,64,128]{2,1,0:T(8,128)(2,1)S(1)}, bf16[4,64,128]{2,1,0:T(8,128)(2,1)S(1)}, u32[]{:S(2)}, u32[]{:S(2)}) collective-permute-start(bf16[4,64,128]{2,1,0:T(8,128)(2,1)S(1)} %edges.1), channel_id=1, source_target_pairs={{1,2},{2,1},{5,6},{6,5},{9,10},{10,9},{13,14},{14,13},{17,18},{18,... | collective-permute-start | bytes 196616 | tf_op jit(solution)/shard_map/ppermute | solution.py:108
  7.4 6.9 %collective-permute-start.3 = (bf16[12,64,128]{2,1,0:T(8,128)(2,1)S(1)}, bf16[12,64,128]{2,1,0:T(8,128)(2,1)S(1)}, u32[]{:S(2)}, u32[]{:S(2)}) collective-permute-start(bf16[12,64,128]{2,1,0:T(8,128)(2,1)S(1)} %pad_maximum_fusion), channel_id=1, source_target_pairs={{0,4},{8,12},{16,20},{24,28},{32,36},{40,44},{48,52},{56,60},{4,0}... | collective-permute-start | bytes 589832 | tf_op jit(solution)/shard_map/ppermute | solution.py:109
  11.2 0.7 collective-permute-start.2
  11.9 15.8 %copy-start.2 = (s32[4]{0:T(128)S(1)}, s32[4]{0:T(128)}, u32[]{:S(2)}) copy-start(s32[4]{0:T(128)} %list_ref.1) | copy-start | bytes 52
  11.9 15.9 %copy-start = (f32[64,2048]{1,0:T(8,128)S(1)}, f32[64,2048]{1,0:T(8,128)}, u32[]{:S(2)}) copy-start(f32[64,2048]{1,0:T(8,128)} %x_ref.5) | copy-start | bytes 1572868
  14.4 13.6 %collective-permute-start.5 = (bf16[36,64,128]{2,1,0:T(8,128)(2,1)S(1)}, bf16[36,64,128]{2,1,0:T(8,128)(2,1)S(1)}, u32[]{:S(2)}, u32[]{:S(2)}) collective-permute-start(bf16[36,64,128]{2,1,0:T(8,128)(2,1)S(1)} %constant_dynamic-update-slice_fusion.mid_ref), channel_id=1, source_target_pairs={{64,128},{192,256},{320,384},{128,64},{256,192},{384,320},{65,129}... | collective-permute-start | bytes 1769480 | tf_op jit(solution)/shard_map/ppermute | solution.py:108
  20.0 8.0 %collective-permute-start.4 = (bf16[36,64,128]{2,1,0:T(8,128)(2,1)S(1)}, bf16[36,64,128]{2,1,0:T(8,128)(2,1)S(1)}, u32[]{:S(2)}, u32[]{:S(2)}) collective-permute-start(bf16[36,64,128]{2,1,0:T(8,128)(2,1)S(1)} %constant_dynamic-update-slice_fusion.mid_ref), channel_id=1, source_target_pairs={{0,64},{128,192},{256,320},{384,448},{64,0},{192,128},{320,256},{4... | collective-permute-start | bytes 1769480 | tf_op jit(solution)/shard_map/ppermute | solution.py:109
  29.2 8.0 %collective-permute-start.7 = (bf16[4,64,128]{2,1,0:T(8,128)(2,1)S(1)}, bf16[4,64,128]{2,1,0:T(8,128)(2,1)S(1)}, u32[]{:S(2)}, u32[]{:S(2)}) collective-permute-start(bf16[4,64,128]{2,1,0:T(8,128)(2,1)S(1)} %get-tuple-element.17), channel_id=1, source_target_pairs={{0,1},{2,3},{1,0},{3,2},{4,5},{6,7},{5,4},{7,6},{8,9},{10,11},{9,8... | collective-permute-start | bytes 196616 | tf_op jit(solution)/shard_map/ppermute | solution.py:109
  34.7 0.7 collective-permute-start.6
  37.2 10.1 %collective-permute-start.8 = (bf16[12,64,128]{2,1,0:T(8,128)(2,1)S(1)}, bf16[12,64,128]{2,1,0:T(8,128)(2,1)S(1)}, u32[]{:S(2)}, u32[]{:S(2)}) collective-permute-start(bf16[12,64,128]{2,1,0:T(8,128)(2,1)S(1)} %get-tuple-element.20), channel_id=1, source_target_pairs={{4,8},{12,16},{20,24},{28,32},{36,40},{44,48},{52,56},{8,4},{16,12... | collective-permute-start | bytes 589832 | tf_op jit(solution)/shard_map/ppermute | solution.py:108
  37.9 13.8 %collective-permute-start.9 = (bf16[12,64,128]{2,1,0:T(8,128)(2,1)S(1)}, bf16[12,64,128]{2,1,0:T(8,128)(2,1)S(1)}, u32[]{:S(2)}, u32[]{:S(2)}) collective-permute-start(bf16[12,64,128]{2,1,0:T(8,128)(2,1)S(1)} %get-tuple-element.20), channel_id=1, source_target_pairs={{0,4},{8,12},{16,20},{24,28},{32,36},{40,44},{48,52},{56,60},{4,0}... | collective-permute-start | bytes 589832 | tf_op jit(solution)/shard_map/ppermute | solution.py:109
  51.7 12.7 %collective-permute-start.11 = (bf16[36,64,128]{2,1,0:T(8,128)(2,1)S(1)}, bf16[36,64,128]{2,1,0:T(8,128)(2,1)S(1)}, u32[]{:S(2)}, u32[]{:S(2)}) collective-permute-start(bf16[36,64,128]{2,1,0:T(8,128)(2,1)S(1)} %constant_dynamic-update-slice_fusion.8.mid_ref), channel_id=1, source_target_pairs={{64,128},{192,256},{320,384},{128,64},{256,192},{384,320},{65,129}... | collective-permute-start | bytes 1769480 | tf_op jit(solution)/shard_map/ppermute | solution.py:108
  56.9 7.6 %collective-permute-start.10 = (bf16[36,64,128]{2,1,0:T(8,128)(2,1)S(1)}, bf16[36,64,128]{2,1,0:T(8,128)(2,1)S(1)}, u32[]{:S(2)}, u32[]{:S(2)}) collective-permute-start(bf16[36,64,128]{2,1,0:T(8,128)(2,1)S(1)} %constant_dynamic-update-slice_fusion.8.mid_ref), channel_id=1, source_target_pairs={{0,64},{128,192},{256,320},{384,448},{64,0},{192,128},{320,256},{4... | collective-permute-start | bytes 1769480 | tf_op jit(solution)/shard_map/ppermute | solution.py:109

commit v7 on v6

--- a/solution.py
+++ b/solution.py
@@ -14,6 +14,8 @@
 MIB = 1 << 20
 PANEL = 8
 SHARE = 0.875
+FIRST_ORDER = ("tx", "ty")
+SECOND_ORDER = ("tx",)
 
 
 def vmem():
@@ -137,18 +139,21 @@
     )(own, mid)
 
 
-def halo(own, edge):
+def halo(own, edge, partner_first):
     block = edge
     for axis in ("tz", "ty"):
-        block = jnp.concatenate([block, *partners_along(block, axis)], axis=0)
+        other, partner = partners_along(block, axis)
+        sides = (partner, other) if axis in partner_first else (other, partner)
+        block = jnp.concatenate([block, *sides], axis=0)
     other, partner = partners_along(block, "tx")
     return near_pool(own, block), partner, other
 
 
-def fill_far(pool_ref, far_refs, sem):
+def fill_far(pool_ref, far_refs, table_ref, table, sem):
     listed = far_refs[0].shape[0]
     base = pool_ref.shape[0] - 2 * listed
-    copies = []
+    copies = [pltpu.make_async_copy(table_ref, table, sem.at[2])]
+    copies[0].start()
     for j, ref in enumerate(far_refs):
         copies.append(
             pltpu.make_async_copy(ref, pool_ref.at[pl.ds(base + j * listed, listed)], sem.at[j])
@@ -158,14 +163,14 @@
         copy.wait()
 
 
-def pool_index(codes, blocks, listed):
+def pool_index(codes, blocks, listed, partner_first):
     place = codes - blocks
     offset = place // listed
     index = jnp.zeros_like(codes)
     for axis, step in (("tx", 9), ("ty", 3), ("tz", 1)):
         way = offset // step % 3
         even = lax.axis_index(axis) % 2 == 0
-        last = jnp.where(even, 0, 2) if axis == "tx" else jnp.where(even, 2, 0)
+        last = jnp.where(even, 0, 2) if axis in partner_first else jnp.where(even, 2, 0)
         index = index * 3 + jnp.where(way == 1, 0, jnp.where(way == last, 2, 1))
     return jnp.where(codes < blocks, codes, blocks + index * listed + place % listed)
 
@@ -185,14 +190,14 @@
 
 def listed_kernel(
     slots, table_ref, x_ref, w_ref, keep_ref, _, partner_ref, other_ref,
-    edge_ref, pool_ref, sem,
+    edge_ref, pool_ref, table, sem,
 ):
-    fill_far(pool_ref, (partner_ref, other_ref), sem)
+    fill_far(pool_ref, (partner_ref, other_ref), table_ref, table, sem)
     first = w_ref.shape[0] * slots
     for j in range(edge_ref.shape[0]):
-        i = table_ref[first + j]
+        i = table[first + j]
         lanes = pl.ds(pl.multiple_of(i * 128, 128), 128)
-        edge_ref[j] = first_row(slots, table_ref, x_ref, w_ref, keep_ref, pool_ref, i, lanes)[2]
+        edge_ref[j] = first_row(slots, table, x_ref, w_ref, keep_ref, pool_ref, i, lanes)[2]
 
 
 def listed_rows(table, count, start_block, weights, keep, far):
@@ -204,9 +209,12 @@
             jax.ShapeDtypeStruct((count, width, size), BF16),
             jax.ShapeDtypeStruct(far[0].shape, BF16),
         ),
-        in_specs=[smem()] + [vmem()] * 4 + [anywhere()] * 2,
+        in_specs=[anywhere()] + [vmem()] * 4 + [anywhere()] * 2,
         out_specs=(vmem(),) * 2,
-        scratch_shapes=[pltpu.SemaphoreType.DMA((2,))],
+        scratch_shapes=[
+            pltpu.SMEM(table.shape, jnp.int32),
+            pltpu.SemaphoreType.DMA((3,)),
+        ],
         input_output_aliases={4: 1},
         compiler_params=pltpu.CompilerParams(vmem_limit_bytes=16 * MIB),
         name="listed_rows",
@@ -273,14 +281,24 @@
 
 def second_kernel(
     slots, table_ref, base_ref, w_ref, gram_ref, _, partner_ref, other_ref,
-    out_ref, both_ref, pool_ref, wide, sem,
+    out_ref, both_ref, pool_ref, table, wide, sem,
 ):
-    fill_far(pool_ref, (partner_ref, other_ref), sem)
+    width = base_ref.shape[1]
+    fill_far(pool_ref, (partner_ref, other_ref), table_ref, table, sem)
     for i in range(w_ref.shape[0]):
-        mixed = base_ref[i] + gather_sum(table_ref, pool_ref, w_ref, slots, i) * 0.125
+        mixed = base_ref[i] + gather_sum(table, pool_ref, w_ref, slots, i) * 0.125
         out_ref[i] = mixed
-        wide[:, i * 128:(i + 1) * 128] = mixed
-    both_ref[...] = jnp.concatenate([gram_ref[...], dot_nt(wide[...], wide[...])], axis=1)
+        rest = mixed
+        for part in range(3):
+            piece = rest.astype(BF16)
+            rest = rest - piece.astype(F32)
+            wide[part * width:(part + 1) * width, i * 128:(i + 1) * 128] = piece
+    product = lax.dot_general(
+        wide[...], wide[...], (((1,), (1,)), ((), ())), preferred_element_type=F32
+    )
+    rows = product[:width] + product[width:2 * width] + product[2 * width:]
+    total = rows[:, :width] + rows[:, width:2 * width] + rows[:, 2 * width:]
+    both_ref[...] = jnp.concatenate([gram_ref[...], total], axis=1)
 
 
 def second_step(table, base, weights, gram, far):
@@ -292,11 +310,12 @@
             jax.ShapeDtypeStruct((width, 2 * width), F32),
             jax.ShapeDtypeStruct(far[0].shape, BF16),
         ),
-        in_specs=[smem()] + [vmem()] * 4 + [anywhere()] * 2,
+        in_specs=[anywhere()] + [vmem()] * 4 + [anywhere()] * 2,
         out_specs=(vmem(),) * 3,
         scratch_shapes=[
-            pltpu.VMEM((width, blocks * 128), F32),
-            pltpu.SemaphoreType.DMA((2,)),
+            pltpu.SMEM(table.shape, jnp.int32),
+            pltpu.VMEM((3 * width, blocks * 128), BF16),
+            pltpu.SemaphoreType.DMA((3,)),
         ],
         input_output_aliases={4: 2},
         compiler_params=pltpu.CompilerParams(vmem_limit_bytes=16 * MIB),
@@ -408,15 +427,17 @@
     root_scale = float(points * devices) ** 0.5
     tiles, keep = hold_weights(weights.reshape(blocks, slots * size, size))
     listed = boundary.shape[0]
-    index = pool_index(neighbours, blocks, listed)
-    table = jnp.concatenate([index.reshape(-1), boundary])
+    tables = []
+    for partner_first in (FIRST_ORDER, SECOND_ORDER):
+        index = pool_index(neighbours, blocks, listed, partner_first)
+        tables.append(jnp.concatenate([index.reshape(-1), boundary]))
     own = jnp.swapaxes(start_block.reshape(-1, blocks, size), 0, 1).astype(BF16)
-    far = halo(own, take_edges(boundary, start_block))
-    edge, pool = listed_rows(table, listed, start_block, tiles, keep, far)
-    mixed, base, step = first_step(table, start_block, tiles, keep, pool)
-    far = halo(step, edge)
+    far = halo(own, take_edges(boundary, start_block), FIRST_ORDER)
+    edge, pool = listed_rows(tables[0], listed, start_block, tiles, keep, far)
+    mixed, base, step = first_step(tables[0], start_block, tiles, keep, pool)
+    far = halo(step, edge, SECOND_ORDER)
     gram = local_gram(mixed)
-    mixed, both = second_step(table, base, tiles, gram, far)
+    mixed, both = second_step(tables[1], base, tiles, gram, far)
     return finish(sum_over_devices(both), mixed, root_scale)
 
 

time: 122 us -> 122 us (level)
  waiting for transfers between devices: 12.6 us -> 15 us
  starting transfers between devices: 43.1 us -> 41.7 us
    ppermute x6, waiting for transfers between devices: 3.22 us -> 5.65 us  [partners_along(): other = lax.ppermute(block, axis, pairs(1))]
    ppermute x6, starting transfers between devices: 29.6 us -> 28 us  [partners_along(): return (other, lax.ppermute(block, axis, pairs(0)))]
  transfers between devices with their start and end apart: 12 -> 12, of which waited for: 5 -> 6; matrix products, arithmetic and copies ran while one was open for 0% -> 1% of each run, Pallas kernels for 4% -> 4%
where the time goes in v7:
time: 122 us; the launch traced here: 121 us
  blocking collectives  51.1 us (42%)
  starting transfers between devices  41.7 us (34%)
  waiting for transfers between devices  15 us (12%)
  Pallas kernels  11.6 us (10%)
    ppermute x6, starting transfers between devices, partners_along(): return (other, lax.ppermute(block, axis, pairs(0)))  28 us
    all_to_all x1, blocking collectives, sum_over_devices(): lax.all_to_all(jnp.broadcast_to(mine[None], (line, *shape)), 'ty', 0, 0)  24.7 us
    all_to_all x1, blocking collectives, sum_over_devices(): parts = lax.all_to_all(parts.reshape(along * deep, *shape), PLANE, 0, 0)  17.1 us
    ppermute x6, starting transfers between devices, partners_along(): other = lax.ppermute(block, axis, pairs(1))  13.7 us
    ppermute x6, waiting for transfers between devices, partners_along(): return (other, lax.ppermute(block, axis, pairs(0)))  9.36 us
    all_to_all x1, blocking collectives, sum_over_devices(): lax.all_to_all(jnp.broadcast_to(mine[None], (along, *shape)), 'tx', 0, 0)  9.31 us
    ppermute x6, waiting for transfers between devices, partners_along(): other = lax.ppermute(block, axis, pairs(1))  5.65 us
    pallas_call x1, Pallas kernels, finish(): pl.pallas_call(functools.partial(finish_kernel, root_scale), out_shape=(j...  2.95 us
  transfers between devices with their start and end apart: 12, of which 6 were waited for; matrix products, arithmetic and copies ran while one was open for 1% of the time, Pallas kernels for 4%

profile of v7, /device:TPU:1, one launch (start us, length us, event | category | flops | bytes accessed | tf_op | source)
XLA Modules:
  0.0 121.2 jit_solution(14072133475481365232)
XLA Ops:
  0.6 0.0 copy-start.1
  0.6 1.1 edges.1
  1.7 4.0 %collective-permute-start.1 = (bf16[4,64,128]{2,1,0:T(8,128)(2,1)S(1)}, bf16[4,64,128]{2,1,0:T(8,128)(2,1)S(1)}, u32[]{:S(2)}, u32[]{:S(2)}) collective-permute-start(bf16[4,64,128]{2,1,0:T(8,128)(2,1)S(1)} %edges.1), channel_id=1, source_target_pairs={{0,1},{2,3},{1,0},{3,2},{4,5},{6,7},{5,4},{7,6},{8,9},{10,11},{9,8... | collective-permute-start | bytes 196616 | tf_op jit(solution)/shard_map/ppermute | solution.py:111
  5.8 0.7 collective-permute-start
  6.5 1.0 collective-permute-done.1
  7.4 0.0 collective-permute-done
  7.4 0.7 collective-permute-start.3
  8.1 6.6 %collective-permute-start.2 = (bf16[12,64,128]{2,1,0:T(8,128)(2,1)S(1)}, bf16[12,64,128]{2,1,0:T(8,128)(2,1)S(1)}, u32[]{:S(2)}, u32[]{:S(2)}) collective-permute-start(bf16[12,64,128]{2,1,0:T(8,128)(2,1)S(1)} %pad_maximum_fusion), channel_id=1, source_target_pairs={{0,4},{8,12},{16,20},{24,28},{32,36},{40,44},{48,52},{56,60},{4,0}... | collective-permute-start | bytes 589832 | tf_op jit(solution)/shard_map/ppermute | solution.py:111
  14.7 0.0 copy-start.2
  14.8 0.0 copy-start
  14.8 3.0 %collective-permute-done.2 = bf16[12,64,128]{2,1,0:T(8,128)(2,1)S(1)} collective-permute-done((bf16[12,64,128]{2,1,0:T(8,128)(2,1)S(1)}, bf16[12,64,128]{2,1,0:T(8,128)(2,1)S(1)}, u32[]{:S(2)}, u32[]{:S(2)}) %collective-permute-start.2) | collective-permute-done | bytes 196640 | tf_op jit(solution)/shard_map/ppermute | solution.py:111
  17.8 0.0 collective-permute-done.3
  17.8 6.0 %collective-permute-start.5 = (bf16[36,64,128]{2,1,0:T(8,128)(2,1)S(1)}, bf16[36,64,128]{2,1,0:T(8,128)(2,1)S(1)}, u32[]{:S(2)}, u32[]{:S(2)}) collective-permute-start(bf16[36,64,128]{2,1,0:T(8,128)(2,1)S(1)} %constant_dynamic-update-slice_fusion.mid_ref), channel_id=1, source_target_pairs={{64,128},{192,256},{320,384},{128,64},{256,192},{384,320},{65,129}... | collective-permute-start | bytes 1769480 | tf_op jit(solution)/shard_map/ppermute | solution.py:110
  23.8 1.9 %collective-permute-start.4 = (bf16[36,64,128]{2,1,0:T(8,128)(2,1)S(1)}, bf16[36,64,128]{2,1,0:T(8,128)(2,1)S(1)}, u32[]{:S(2)}, u32[]{:S(2)}) collective-permute-start(bf16[36,64,128]{2,1,0:T(8,128)(2,1)S(1)} %constant_dynamic-update-slice_fusion.mid_ref), channel_id=1, source_target_pairs={{0,64},{128,192},{256,320},{384,448},{64,0},{192,128},{320,256},{4... | collective-permute-start | bytes 1769480 | tf_op jit(solution)/shard_map/ppermute | solution.py:111
  25.8 0.0 copy-done.1
  25.8 0.1 copy.14
  25.9 0.1 reshape.26
  26.0 0.1 copy.13
  26.1 0.1 reshape.25
  26.2 2.4 %hold_weights.1 = (bf16[16,768,128]{2,1,0:T(8,128)(2,1)S(1)}, f32[16,8,128]{2,1,0:T(8,128)S(1)}) custom-call(bf16[16,768,128]{2,1,0:T(8,128)(2,1)} %bitcast.13), custom_call_target="tpu_custom_call" | custom-call | bytes 6291456 | tf_op jit(solution)/shard_map/hold_weights/pallas_call | solution.py:86
  28.6 0.0 copy-done.2
  28.6 0.1 pad_add_fusion.1
  28.7 0.0 copy-done
  28.8 0.2 near_pool.2._
  28.9 2.4 %collective-permute-done.5.other_ref = bf16[36,64,128]{2,1,0:T(8,128)(2,1)S(1)} collective-permute-done((bf16[36,64,128]{2,1,0:T(8,128)(2,1)S(1)}, bf16[36,64,128]{2,1,0:T(8,128)(2,1)S(1)}, u32[]{:S(2)}, u32[]{:S(2)}) %collective-permute-start.5) | collective-permute-done | bytes 589856 | tf_op jit(solution)/shard_map/ppermute | solution.py:110
  31.4 0.0 collective-permute-done.4.partner_ref
  31.4 0.9 listed_rows.1
  32.2 6.0 %collective-permute-start.7 = (bf16[4,64,128]{2,1,0:T(8,128)(2,1)S(1)}, bf16[4,64,128]{2,1,0:T(8,128)(2,1)S(1)}, u32[]{:S(2)}, u32[]{:S(2)}) collective-permute-start(bf16[4,64,128]{2,1,0:T(8,128)(2,1)S(1)} %get-tuple-element.17), channel_id=1, source_target_pairs={{0,1},{2,3},{1,0},{3,2},{4,5},{6,7},{5,4},{7,6},{8,9},{10,11},{9,8... | collective-permute-start | bytes 196616 | tf_op jit(solution)/shard_map/ppermute | solution.py:111
  38.2 0.7 collective-permute-start.6
  38.9 0.0 collective-permute-done.6
  39.0 0.9 collective-permute-done.7
  39.9 0.7 collective-permute-start.8
  40.6 7.6 %collective-permute-start.9 = (bf16[12,64,128]{2,1,0:T(8,128)(2,1)S(1)}, bf16[12,64,128]{2,1,0:T(8,128)(2,1)S(1)}, u32[]{:S(2)}, u32[]{:S(2)}) collective-permute-start(bf16[12,64,128]{2,1,0:T(8,128)(2,1)S(1)} %get-tuple-element.20), channel_id=1, source_target_pairs={{0,4},{8,12},{16,20},{24,28},{32,36},{40,44},{48,52},{56,60},{4,0}... | collective-permute-start | bytes 589832 | tf_op jit(solution)/shard_map/ppermute | solution.py:111
  48.2 0.0 collective-permute-done.8
  48.2 4.5 %collective-permute-done.9 = bf16[12,64,128]{2,1,0:T(8,128)(2,1)S(1)} collective-permute-done((bf16[12,64,128]{2,1,0:T(8,128)(2,1)S(1)}, bf16[12,64,128]{2,1,0:T(8,128)(2,1)S(1)}, u32[]{:S(2)}, u32[]{:S(2)}) %collective-permute-start.9) | collective-permute-done | bytes 196640 | tf_op jit(solution)/shard_map/ppermute | solution.py:111
  52.8 5.0 %collective-permute-start.11 = (bf16[36,64,128]{2,1,0:T(8,128)(2,1)S(1)}, bf16[36,64,128]{2,1,0:T(8,128)(2,1)S(1)}, u32[]{:S(2)}, u32[]{:S(2)}) collective-permute-start(bf16[36,64,128]{2,1,0:T(8,128)(2,1)S(1)} %constant_dynamic-update-slice_fusion.8.mid_ref), channel_id=1, source_target_pairs={{64,128},{192,256},{320,384},{128,64},{256,192},{384,320},{65,129}... | collective-permute-start | bytes 1769480 | tf_op jit(solution)/shard_map/ppermute | solution.py:110
  57.8 1.9 %collective-permute-start.10 = (bf16[36,64,128]{2,1,0:T(8,128)(2,1)S(1)}, bf16[36,64,128]{2,1,0:T(8,128)(2,1)S(1)}, u32[]{:S(2)}, u32[]{:S(2)}) collective-permute-start(bf16[36,64,128]{2,1,0:T(8,128)(2,1)S(1)} %constant_dynamic-update-slice_fusion.8.mid_ref), channel_id=1, source_target_pairs={{0,64},{128,192},{256,320},{384,448},{64,0},{192,128},{320,256},{4... | collective-permute-start | bytes 1769480 | tf_op jit(solution)/shard_map/ppermute | solution.py:111
  59.7 1.3 %first_step.1 = (f32[16,64,128]{2,1,0:T(8,128)S(1)}, f32[16,64,128]{2,1,0:T(8,128)S(1)}, bf16[16,64,128]{2,1,0:T(8,128)(2,1)S(1)}) custom-call(s32[100]{0:T(128)S(1)} %get-tuple-element.28.table_ref, f32[64,2048]{1,0:T(8,128)S(1)} %copy-done, bf16[16,768,128]{2,1,0:T(8,128)(2,1)S(1)} %get-tuple-element.11.w_ref, ...), custom_call_target="tpu_custom_call" | custom-call | flops 201326592 | bytes 3145728 | tf_op jit(solution)/shard_map/first_step/pallas_call | solution.py:238
  61.0 0.9 first_gram.1.gram_ref
  62.0 0.2 near_pool.3._
  62.1 3.2 %collective-permute-done.11.other_ref = bf16[36,64,128]{2,1,0:T(8,128)(2,1)S(1)} collective-permute-done((bf16[36,64,128]{2,1,0:T(8,128)(2,1)S(1)}, bf16[36,64,128]{2,1,0:T(8,128)(2,1)S(1)}, u32[]{:S(2)}, u32[]{:S(2)}) %collective-permute-start.11) | collective-permute-done | bytes 589856 | tf_op jit(solution)/shard_map/ppermute | solution.py:110
  65.4 0.0 collective-permute-done.10.partner_ref
  65.4 1.7 %second_step.1 = (f32[16,64,128]{2,1,0:T(8,128)S(1)}, f32[64,128]{1,0:T(8,128)S(1)}, bf16[124,64,128]{2,1,0:T(8,128)(2,1)S(1)}) custom-call(s32[100]{0:T(128)S(1)} %get-tuple-element.29.table_ref, f32[16,64,128]{2,1,0:T(8,128)S(1)} %get-tuple-element.14.base_ref, bf16[16,768,128]{2,1,0:T(8,128)(2,1)S(1)} %get-tuple-element.11.w_ref, ...), custom_call_target="tpu_custom_call", output_to_operand_aliasing={{2}: (4, {})} | custom-call | tf_op jit(solution)/shard_map/second_step/pallas_call | solution.py:306
  67.1 17.1 %all_to_all.15 = f32[32,8,128]{2,1,0:T(8,128)S(1)} all-to-all(f32[32,8,128]{2,1,0:T(8,128)S(1)} %bitcast.14), channel_id=1, replica_groups=mesh['tx'=8,'ty'=16,'tz'=4] {'tx','tz'}, dimensions={0} | all-to-all | bytes 262144 | tf_op jit(solution)/shard_map/all_to_all | solution.py:331
  84.3 24.7 %all_to_all.16 = f32[16,8,128]{2,1,0:T(8,128)S(1)} all-to-all(f32[16,8,128]{2,1,0:T(8,128)S(1)} %broadcast_in_dim.42), channel_id=1, replica_groups=mesh['tx'=8,'ty'=16,'tz'=4] {'ty'}, dimensions={0} | all-to-all | bytes 131072 | tf_op jit(solution)/shard_map/all_to_all | solution.py:333
  109.0 9.3 %all_to_all.17 = f32[8,8,128]{2,1,0:T(8,128)S(1)} all-to-all(f32[8,8,128]{2,1,0:T(8,128)S(1)} %broadcast_in_dim.43), channel_id=1, replica_groups=mesh['tx'=8,'ty'=16,'tz'=4] {'tx'}, dimensions={0} | all-to-all | bytes 65536 | tf_op jit(solution)/shard_map/all_to_all | solution.py:335
  118.3 2.9 %finish.1 = (f32[64,2048]{1,0:T(8,128)}, f32[64,64]{1,0:T(8,128)}) custom-call(f32[64,128]{1,0:T(8,128)S(1)} %bitcast.11, f32[16,64,128]{2,1,0:T(8,128)S(1)} %get-tuple-element.19.mixed_ref), custom_call_target="tpu_custom_call" | custom-call | tf_op jit(solution)/shard_map/finish/pallas_call | solution.py:410
  (18 shorter events, 0.4 us)
Async XLA Ops:
  0.6 25.2 %copy-start.1 = (s32[16,6]{0,1:T(8,128)S(1)}, s32[16,6]{0,1:T(8,128)}, u32[]{:S(2)}) copy-start(s32[16,6]{0,1:T(8,128)} %param.6) | copy-start | bytes 1156
  1.7 5.7 %collective-permute-start.1 = (bf16[4,64,128]{2,1,0:T(8,128)(2,1)S(1)}, bf16[4,64,128]{2,1,0:T(8,128)(2,1)S(1)}, u32[]{:S(2)}, u32[]{:S(2)}) collective-permute-start(bf16[4,64,128]{2,1,0:T(8,128)(2,1)S(1)} %edges.1), channel_id=1, source_target_pairs={{0,1},{2,3},{1,0},{3,2},{4,5},{6,7},{5,4},{7,6},{8,9},{10,11},{9,8... | collective-permute-start | bytes 196616 | tf_op jit(solution)/shard_map/ppermute | solution.py:111
  5.8 1.6 %collective-permute-start = (bf16[4,64,128]{2,1,0:T(8,128)(2,1)S(1)}, bf16[4,64,128]{2,1,0:T(8,128)(2,1)S(1)}, u32[]{:S(2)}, u32[]{:S(2)}) collective-permute-start(bf16[4,64,128]{2,1,0:T(8,128)(2,1)S(1)} %edges.1), channel_id=1, source_target_pairs={{1,2},{2,1},{5,6},{6,5},{9,10},{10,9},{13,14},{14,13},{17,18},{18,... | collective-permute-start | bytes 196616 | tf_op jit(solution)/shard_map/ppermute | solution.py:110
  7.4 10.3 %collective-permute-start.3 = (bf16[12,64,128]{2,1,0:T(8,128)(2,1)S(1)}, bf16[12,64,128]{2,1,0:T(8,128)(2,1)S(1)}, u32[]{:S(2)}, u32[]{:S(2)}) collective-permute-start(bf16[12,64,128]{2,1,0:T(8,128)(2,1)S(1)} %pad_maximum_fusion), channel_id=1, source_target_pairs={{4,8},{12,16},{20,24},{28,32},{36,40},{44,48},{52,56},{8,4},{16,12... | collective-permute-start | bytes 589832 | tf_op jit(solution)/shard_map/ppermute | solution.py:110
  8.1 9.6 %collective-permute-start.2 = (bf16[12,64,128]{2,1,0:T(8,128)(2,1)S(1)}, bf16[12,64,128]{2,1,0:T(8,128)(2,1)S(1)}, u32[]{:S(2)}, u32[]{:S(2)}) collective-permute-start(bf16[12,64,128]{2,1,0:T(8,128)(2,1)S(1)} %pad_maximum_fusion), channel_id=1, source_target_pairs={{0,4},{8,12},{16,20},{24,28},{32,36},{40,44},{48,52},{56,60},{4,0}... | collective-permute-start | bytes 589832 | tf_op jit(solution)/shard_map/ppermute | solution.py:111
  14.7 13.9 %copy-start.2 = (s32[4]{0:T(128)S(1)}, s32[4]{0:T(128)}, u32[]{:S(2)}) copy-start(s32[4]{0:T(128)} %list_ref.1) | copy-start | bytes 52
  14.8 14.0 %copy-start = (f32[64,2048]{1,0:T(8,128)S(1)}, f32[64,2048]{1,0:T(8,128)}, u32[]{:S(2)}) copy-start(f32[64,2048]{1,0:T(8,128)} %x_ref.5) | copy-start | bytes 1572868
  17.8 13.5 %collective-permute-start.5 = (bf16[36,64,128]{2,1,0:T(8,128)(2,1)S(1)}, bf16[36,64,128]{2,1,0:T(8,128)(2,1)S(1)}, u32[]{:S(2)}, u32[]{:S(2)}) collective-permute-start(bf16[36,64,128]{2,1,0:T(8,128)(2,1)S(1)} %constant_dynamic-update-slice_fusion.mid_ref), channel_id=1, source_target_pairs={{64,128},{192,256},{320,384},{128,64},{256,192},{384,320},{65,129}... | collective-permute-start | bytes 1769480 | tf_op jit(solution)/shard_map/ppermute | solution.py:110
  23.8 7.6 %collective-permute-start.4 = (bf16[36,64,128]{2,1,0:T(8,128)(2,1)S(1)}, bf16[36,64,128]{2,1,0:T(8,128)(2,1)S(1)}, u32[]{:S(2)}, u32[]{:S(2)}) collective-permute-start(bf16[36,64,128]{2,1,0:T(8,128)(2,1)S(1)} %constant_dynamic-update-slice_fusion.mid_ref), channel_id=1, source_target_pairs={{0,64},{128,192},{256,320},{384,448},{64,0},{192,128},{320,256},{4... | collective-permute-start | bytes 1769480 | tf_op jit(solution)/shard_map/ppermute | solution.py:111
  32.2 7.6 %collective-permute-start.7 = (bf16[4,64,128]{2,1,0:T(8,128)(2,1)S(1)}, bf16[4,64,128]{2,1,0:T(8,128)(2,1)S(1)}, u32[]{:S(2)}, u32[]{:S(2)}) collective-permute-start(bf16[4,64,128]{2,1,0:T(8,128)(2,1)S(1)} %get-tuple-element.17), channel_id=1, source_target_pairs={{0,1},{2,3},{1,0},{3,2},{4,5},{6,7},{5,4},{7,6},{8,9},{10,11},{9,8... | collective-permute-start | bytes 196616 | tf_op jit(solution)/shard_map/ppermute | solution.py:111
  38.2 0.7 collective-permute-start.6
  39.9 8.3 %collective-permute-start.8 = (bf16[12,64,128]{2,1,0:T(8,128)(2,1)S(1)}, bf16[12,64,128]{2,1,0:T(8,128)(2,1)S(1)}, u32[]{:S(2)}, u32[]{:S(2)}) collective-permute-start(bf16[12,64,128]{2,1,0:T(8,128)(2,1)S(1)} %get-tuple-element.20), channel_id=1, source_target_pairs={{4,8},{12,16},{20,24},{28,32},{36,40},{44,48},{52,56},{8,4},{16,12... | collective-permute-start | bytes 589832 | tf_op jit(solution)/shard_map/ppermute | solution.py:110
  40.6 12.2 %collective-permute-start.9 = (bf16[12,64,128]{2,1,0:T(8,128)(2,1)S(1)}, bf16[12,64,128]{2,1,0:T(8,128)(2,1)S(1)}, u32[]{:S(2)}, u32[]{:S(2)}) collective-permute-start(bf16[12,64,128]{2,1,0:T(8,128)(2,1)S(1)} %get-tuple-element.20), channel_id=1, source_target_pairs={{0,4},{8,12},{16,20},{24,28},{32,36},{40,44},{48,52},{56,60},{4,0}... | collective-permute-start | bytes 589832 | tf_op jit(solution)/shard_map/ppermute | solution.py:111
  52.8 12.6 %collective-permute-start.11 = (bf16[36,64,128]{2,1,0:T(8,128)(2,1)S(1)}, bf16[36,64,128]{2,1,0:T(8,128)(2,1)S(1)}, u32[]{:S(2)}, u32[]{:S(2)}) collective-permute-start(bf16[36,64,128]{2,1,0:T(8,128)(2,1)S(1)} %constant_dynamic-update-slice_fusion.8.mid_ref), channel_id=1, source_target_pairs={{64,128},{192,256},{320,384},{128,64},{256,192},{384,320},{65,129}... | collective-permute-start | bytes 1769480 | tf_op jit(solution)/shard_map/ppermute | solution.py:110
  57.8 7.6 %collective-permute-start.10 = (bf16[36,64,128]{2,1,0:T(8,128)(2,1)S(1)}, bf16[36,64,128]{2,1,0:T(8,128)(2,1)S(1)}, u32[]{:S(2)}, u32[]{:S(2)}) collective-permute-start(bf16[36,64,128]{2,1,0:T(8,128)(2,1)S(1)} %constant_dynamic-update-slice_fusion.8.mid_ref), channel_id=1, source_target_pairs={{0,64},{128,192},{256,320},{384,448},{64,0},{192,128},{320,256},{4... | collective-permute-start | bytes 1769480 | tf_op jit(solution)/shard_map/ppermute | solution.py:111

commit v8 on v7

--- a/solution.py
+++ b/solution.py
@@ -14,8 +14,6 @@
 MIB = 1 << 20
 PANEL = 8
 SHARE = 0.875
-FIRST_ORDER = ("tx", "ty")
-SECOND_ORDER = ("tx",)
 
 
 def vmem():
@@ -139,12 +137,10 @@
     )(own, mid)
 
 
-def halo(own, edge, partner_first):
+def halo(own, edge):
     block = edge
     for axis in ("tz", "ty"):
-        other, partner = partners_along(block, axis)
-        sides = (partner, other) if axis in partner_first else (other, partner)
-        block = jnp.concatenate([block, *sides], axis=0)
+        block = jnp.concatenate([block, *partners_along(block, axis)], axis=0)
     other, partner = partners_along(block, "tx")
     return near_pool(own, block), partner, other
 
@@ -163,14 +159,14 @@
         copy.wait()
 
 
-def pool_index(codes, blocks, listed, partner_first):
+def pool_index(codes, blocks, listed):
     place = codes - blocks
     offset = place // listed
     index = jnp.zeros_like(codes)
     for axis, step in (("tx", 9), ("ty", 3), ("tz", 1)):
         way = offset // step % 3
         even = lax.axis_index(axis) % 2 == 0
-        last = jnp.where(even, 0, 2) if axis in partner_first else jnp.where(even, 2, 0)
+        last = jnp.where(even, 0, 2) if axis == "tx" else jnp.where(even, 2, 0)
         index = index * 3 + jnp.where(way == 1, 0, jnp.where(way == last, 2, 1))
     return jnp.where(codes < blocks, codes, blocks + index * listed + place % listed)
 
@@ -427,17 +423,15 @@
     root_scale = float(points * devices) ** 0.5
     tiles, keep = hold_weights(weights.reshape(blocks, slots * size, size))
     listed = boundary.shape[0]
-    tables = []
-    for partner_first in (FIRST_ORDER, SECOND_ORDER):
-        index = pool_index(neighbours, blocks, listed, partner_first)
-        tables.append(jnp.concatenate([index.reshape(-1), boundary]))
+    index = pool_index(neighbours, blocks, listed)
+    table = jnp.concatenate([index.reshape(-1), boundary])
     own = jnp.swapaxes(start_block.reshape(-1, blocks, size), 0, 1).astype(BF16)
-    far = halo(own, take_edges(boundary, start_block), FIRST_ORDER)
-    edge, pool = listed_rows(tables[0], listed, start_block, tiles, keep, far)
-    mixed, base, step = first_step(tables[0], start_block, tiles, keep, pool)
-    far = halo(step, edge, SECOND_ORDER)
+    far = halo(own, take_edges(boundary, start_block))
+    edge, pool = listed_rows(table, listed, start_block, tiles, keep, far)
+    mixed, base, step = first_step(table, start_block, tiles, keep, pool)
+    far = halo(step, edge)
     gram = local_gram(mixed)
-    mixed, both = second_step(tables[1], base, tiles, gram, far)
+    mixed, both = second_step(table, base, tiles, gram, far)
     return finish(sum_over_devices(both), mixed, root_scale)
 
 

time: 122 us -> 121 us (level)
  waiting for transfers between devices: 15 us -> 12.7 us
  starting transfers between devices: 41.7 us -> 43.1 us
    ppermute x6, waiting for transfers between devices: 5.65 us -> 3.23 us  [partners_along(): other = lax.ppermute(block, axis, pairs(1))]
    ppermute x6, starting transfers between devices: 28 us -> 29.6 us  [partners_along(): return (other, lax.ppermute(block, axis, pairs(0)))]
  transfers between devices with their start and end apart: 12 -> 12, of which waited for: 6 -> 5; matrix products, arithmetic and copies ran while one was open for 1% -> 0% of each run, Pallas kernels for 4% -> 4%
where the time goes in v8:
time: 121 us
  blocking collectives  51.7 us (43%)
  starting transfers between devices  43.1 us (36%)
  waiting for transfers between devices  12.7 us (10%)
  Pallas kernels  11.6 us (10%)
    ppermute x6, starting transfers between devices, partners_along(): return (other, lax.ppermute(block, axis, pairs(0)))  29.6 us
    all_to_all x1, blocking collectives, sum_over_devices(): lax.all_to_all(jnp.broadcast_to(mine[None], (line, *shape)), 'ty', 0, 0)  25.3 us
    all_to_all x1, blocking collectives, sum_over_devices(): parts = lax.all_to_all(parts.reshape(along * deep, *shape), PLANE, 0, 0)  17.1 us
    ppermute x6, starting transfers between devices, partners_along(): other = lax.ppermute(block, axis, pairs(1))  13.5 us
    ppermute x6, waiting for transfers between devices, partners_along(): return (other, lax.ppermute(block, axis, pairs(0)))  9.42 us
    all_to_all x1, blocking collectives, sum_over_devices(): lax.all_to_all(jnp.broadcast_to(mine[None], (along, *shape)), 'tx', 0, 0)  9.31 us
    ppermute x6, waiting for transfers between devices, partners_along(): other = lax.ppermute(block, axis, pairs(1))  3.23 us
    pallas_call x1, Pallas kernels, finish(): pl.pallas_call(functools.partial(finish_kernel, root_scale), out_shape=(j...  2.95 us
  transfers between devices with their start and end apart: 12, of which 5 were waited for; matrix products, arithmetic and copies ran while one was open for 0% of the time, Pallas kernels for 4%

profile of v8, /device:TPU:1, one launch (start us, length us, event | category | flops | bytes accessed | tf_op | source)
XLA Modules:
  0.0 120.8 jit_solution(11663307792102005906)
XLA Ops:
  0.6 0.0 copy-start.1
  0.6 1.1 edges.1
  1.7 4.0 %collective-permute-start.1 = (bf16[4,64,128]{2,1,0:T(8,128)(2,1)S(1)}, bf16[4,64,128]{2,1,0:T(8,128)(2,1)S(1)}, u32[]{:S(2)}, u32[]{:S(2)}) collective-permute-start(bf16[4,64,128]{2,1,0:T(8,128)(2,1)S(1)} %edges.1), channel_id=1, source_target_pairs={{0,1},{2,3},{1,0},{3,2},{4,5},{6,7},{5,4},{7,6},{8,9},{10,11},{9,8... | collective-permute-start | bytes 196616 | tf_op jit(solution)/shard_map/ppermute | solution.py:109
  5.8 0.7 collective-permute-start
  6.5 1.0 collective-permute-done.1
  7.4 0.0 collective-permute-done
  7.4 3.7 %collective-permute-start.3 = (bf16[12,64,128]{2,1,0:T(8,128)(2,1)S(1)}, bf16[12,64,128]{2,1,0:T(8,128)(2,1)S(1)}, u32[]{:S(2)}, u32[]{:S(2)}) collective-permute-start(bf16[12,64,128]{2,1,0:T(8,128)(2,1)S(1)} %pad_maximum_fusion), channel_id=1, source_target_pairs={{0,4},{8,12},{16,20},{24,28},{32,36},{40,44},{48,52},{56,60},{4,0}... | collective-permute-start | bytes 589832 | tf_op jit(solution)/shard_map/ppermute | solution.py:109
  11.2 0.7 collective-permute-start.2
  11.9 0.0 copy-start.2
  11.9 0.0 copy-start
  11.9 0.0 collective-permute-done.2
  11.9 2.4 %collective-permute-done.3 = bf16[12,64,128]{2,1,0:T(8,128)(2,1)S(1)} collective-permute-done((bf16[12,64,128]{2,1,0:T(8,128)(2,1)S(1)}, bf16[12,64,128]{2,1,0:T(8,128)(2,1)S(1)}, u32[]{:S(2)}, u32[]{:S(2)}) %collective-permute-start.3) | collective-permute-done | bytes 196640 | tf_op jit(solution)/shard_map/ppermute | solution.py:109
  14.4 5.6 %collective-permute-start.5 = (bf16[36,64,128]{2,1,0:T(8,128)(2,1)S(1)}, bf16[36,64,128]{2,1,0:T(8,128)(2,1)S(1)}, u32[]{:S(2)}, u32[]{:S(2)}) collective-permute-start(bf16[36,64,128]{2,1,0:T(8,128)(2,1)S(1)} %constant_dynamic-update-slice_fusion.mid_ref), channel_id=1, source_target_pairs={{64,128},{192,256},{320,384},{128,64},{256,192},{384,320},{65,129}... | collective-permute-start | bytes 1769480 | tf_op jit(solution)/shard_map/ppermute | solution.py:108
  20.0 5.0 %collective-permute-start.4 = (bf16[36,64,128]{2,1,0:T(8,128)(2,1)S(1)}, bf16[36,64,128]{2,1,0:T(8,128)(2,1)S(1)}, u32[]{:S(2)}, u32[]{:S(2)}) collective-permute-start(bf16[36,64,128]{2,1,0:T(8,128)(2,1)S(1)} %constant_dynamic-update-slice_fusion.mid_ref), channel_id=1, source_target_pairs={{0,64},{128,192},{256,320},{384,448},{64,0},{192,128},{320,256},{4... | collective-permute-start | bytes 1769480 | tf_op jit(solution)/shard_map/ppermute | solution.py:109
  25.1 0.0 copy-done.1
  25.1 0.1 copy.11
  25.2 0.1 reshape.22
  25.3 2.4 %hold_weights.1 = (bf16[16,768,128]{2,1,0:T(8,128)(2,1)S(1)}, f32[16,8,128]{2,1,0:T(8,128)S(1)}) custom-call(bf16[16,768,128]{2,1,0:T(8,128)(2,1)} %bitcast.13), custom_call_target="tpu_custom_call" | custom-call | bytes 6291456 | tf_op jit(solution)/shard_map/hold_weights/pallas_call | solution.py:84
  27.7 0.0 copy-done.2
  27.7 0.1 pad_add_fusion.table_ref
  27.8 0.0 copy-done
  27.9 0.2 near_pool.2._
  28.0 0.0 collective-permute-done.5.other_ref
  28.0 0.0 collective-permute-done.4.partner_ref
  28.1 0.9 listed_rows.1
  28.9 5.6 %collective-permute-start.7 = (bf16[4,64,128]{2,1,0:T(8,128)(2,1)S(1)}, bf16[4,64,128]{2,1,0:T(8,128)(2,1)S(1)}, u32[]{:S(2)}, u32[]{:S(2)}) collective-permute-start(bf16[4,64,128]{2,1,0:T(8,128)(2,1)S(1)} %get-tuple-element.17), channel_id=1, source_target_pairs={{0,1},{2,3},{1,0},{3,2},{4,5},{6,7},{5,4},{7,6},{8,9},{10,11},{9,8... | collective-permute-start | bytes 196616 | tf_op jit(solution)/shard_map/ppermute | solution.py:109
  34.5 0.7 collective-permute-start.6
  35.2 0.0 collective-permute-done.6
  35.2 1.7 %collective-permute-done.7 = bf16[4,64,128]{2,1,0:T(8,128)(2,1)S(1)} collective-permute-done((bf16[4,64,128]{2,1,0:T(8,128)(2,1)S(1)}, bf16[4,64,128]{2,1,0:T(8,128)(2,1)S(1)}, u32[]{:S(2)}, u32[]{:S(2)}) %collective-permute-start.7) | collective-permute-done | bytes 65568 | tf_op jit(solution)/shard_map/ppermute | solution.py:109
  37.0 0.7 collective-permute-start.8
  37.6 9.4 %collective-permute-start.9 = (bf16[12,64,128]{2,1,0:T(8,128)(2,1)S(1)}, bf16[12,64,128]{2,1,0:T(8,128)(2,1)S(1)}, u32[]{:S(2)}, u32[]{:S(2)}) collective-permute-start(bf16[12,64,128]{2,1,0:T(8,128)(2,1)S(1)} %get-tuple-element.20), channel_id=1, source_target_pairs={{0,4},{8,12},{16,20},{24,28},{32,36},{40,44},{48,52},{56,60},{4,0}... | collective-permute-start | bytes 589832 | tf_op jit(solution)/shard_map/ppermute | solution.py:109
  47.1 0.0 collective-permute-done.8
  47.1 4.3 %collective-permute-done.9 = bf16[12,64,128]{2,1,0:T(8,128)(2,1)S(1)} collective-permute-done((bf16[12,64,128]{2,1,0:T(8,128)(2,1)S(1)}, bf16[12,64,128]{2,1,0:T(8,128)(2,1)S(1)}, u32[]{:S(2)}, u32[]{:S(2)}) %collective-permute-start.9) | collective-permute-done | bytes 196640 | tf_op jit(solution)/shard_map/ppermute | solution.py:109
  51.5 5.2 %collective-permute-start.11 = (bf16[36,64,128]{2,1,0:T(8,128)(2,1)S(1)}, bf16[36,64,128]{2,1,0:T(8,128)(2,1)S(1)}, u32[]{:S(2)}, u32[]{:S(2)}) collective-permute-start(bf16[36,64,128]{2,1,0:T(8,128)(2,1)S(1)} %constant_dynamic-update-slice_fusion.8.mid_ref), channel_id=1, source_target_pairs={{64,128},{192,256},{320,384},{128,64},{256,192},{384,320},{65,129}... | collective-permute-start | bytes 1769480 | tf_op jit(solution)/shard_map/ppermute | solution.py:108
  56.7 1.9 %collective-permute-start.10 = (bf16[36,64,128]{2,1,0:T(8,128)(2,1)S(1)}, bf16[36,64,128]{2,1,0:T(8,128)(2,1)S(1)}, u32[]{:S(2)}, u32[]{:S(2)}) collective-permute-start(bf16[36,64,128]{2,1,0:T(8,128)(2,1)S(1)} %constant_dynamic-update-slice_fusion.8.mid_ref), channel_id=1, source_target_pairs={{0,64},{128,192},{256,320},{384,448},{64,0},{192,128},{320,256},{4... | collective-permute-start | bytes 1769480 | tf_op jit(solution)/shard_map/ppermute | solution.py:109
  58.6 1.3 %first_step.1 = (f32[16,64,128]{2,1,0:T(8,128)S(1)}, f32[16,64,128]{2,1,0:T(8,128)S(1)}, bf16[16,64,128]{2,1,0:T(8,128)(2,1)S(1)}) custom-call(s32[100]{0:T(128)S(1)} %pad_add_fusion.table_ref, f32[64,2048]{1,0:T(8,128)S(1)} %copy-done, bf16[16,768,128]{2,1,0:T(8,128)(2,1)S(1)} %get-tuple-element.11.w_ref, f32[16,8,128]{2,1,0:T(8,128)S(1)} %get-tuple-element.12.keep_ref, ...), custom_call_target="tpu_custom_call" | custom-call | flops 201326592 | bytes 3145728 | tf_op jit(solution)/shard_map/first_step/pallas_call | solution.py:234
  59.9 0.9 first_gram.1.gram_ref
  60.9 0.2 near_pool.3._
  61.0 3.2 %collective-permute-done.11.other_ref = bf16[36,64,128]{2,1,0:T(8,128)(2,1)S(1)} collective-permute-done((bf16[36,64,128]{2,1,0:T(8,128)(2,1)S(1)}, bf16[36,64,128]{2,1,0:T(8,128)(2,1)S(1)}, u32[]{:S(2)}, u32[]{:S(2)}) %collective-permute-start.11) | collective-permute-done | bytes 589856 | tf_op jit(solution)/shard_map/ppermute | solution.py:108
  64.2 0.0 collective-permute-done.10.partner_ref
  64.2 1.7 %second_step.1 = (f32[16,64,128]{2,1,0:T(8,128)S(1)}, f32[64,128]{1,0:T(8,128)S(1)}, bf16[124,64,128]{2,1,0:T(8,128)(2,1)S(1)}) custom-call(s32[100]{0:T(128)S(1)} %pad_add_fusion.table_ref, f32[16,64,128]{2,1,0:T(8,128)S(1)} %get-tuple-element.14.base_ref, bf16[16,768,128]{2,1,0:T(8,128)(2,1)S(1)} %get-tuple-element.11.w_ref, ...), custom_call_target="tpu_custom_call", output_to_operand_aliasing={{2}: (4, {})} | custom-call | tf_op jit(solution)/shard_map/second_step/pallas_call | solution.py:302
  66.0 17.1 %all_to_all.15 = f32[32,8,128]{2,1,0:T(8,128)S(1)} all-to-all(f32[32,8,128]{2,1,0:T(8,128)S(1)} %bitcast.14), channel_id=1, replica_groups=mesh['tx'=8,'ty'=16,'tz'=4] {'tx','tz'}, dimensions={0} | all-to-all | bytes 262144 | tf_op jit(solution)/shard_map/all_to_all | solution.py:327
  83.1 25.3 %all_to_all.16 = f32[16,8,128]{2,1,0:T(8,128)S(1)} all-to-all(f32[16,8,128]{2,1,0:T(8,128)S(1)} %broadcast_in_dim.33), channel_id=1, replica_groups=mesh['tx'=8,'ty'=16,'tz'=4] {'ty'}, dimensions={0} | all-to-all | bytes 131072 | tf_op jit(solution)/shard_map/all_to_all | solution.py:329
  108.5 9.3 %all_to_all.17 = f32[8,8,128]{2,1,0:T(8,128)S(1)} all-to-all(f32[8,8,128]{2,1,0:T(8,128)S(1)} %broadcast_in_dim.34), channel_id=1, replica_groups=mesh['tx'=8,'ty'=16,'tz'=4] {'tx'}, dimensions={0} | all-to-all | bytes 65536 | tf_op jit(solution)/shard_map/all_to_all | solution.py:331
  117.8 2.9 %finish.1 = (f32[64,2048]{1,0:T(8,128)}, f32[64,64]{1,0:T(8,128)}) custom-call(f32[64,128]{1,0:T(8,128)S(1)} %bitcast.11, f32[16,64,128]{2,1,0:T(8,128)S(1)} %get-tuple-element.19.mixed_ref), custom_call_target="tpu_custom_call" | custom-call | tf_op jit(solution)/shard_map/finish/pallas_call | solution.py:406
  (18 shorter events, 0.4 us)
Async XLA Ops:
  0.6 24.4 %copy-start.1 = (s32[16,6]{0,1:T(8,128)S(1)}, s32[16,6]{0,1:T(8,128)}, u32[]{:S(2)}) copy-start(s32[16,6]{0,1:T(8,128)} %param.6) | copy-start | bytes 1156
  1.7 5.7 %collective-permute-start.1 = (bf16[4,64,128]{2,1,0:T(8,128)(2,1)S(1)}, bf16[4,64,128]{2,1,0:T(8,128)(2,1)S(1)}, u32[]{:S(2)}, u32[]{:S(2)}) collective-permute-start(bf16[4,64,128]{2,1,0:T(8,128)(2,1)S(1)} %edges.1), channel_id=1, source_target_pairs={{0,1},{2,3},{1,0},{3,2},{4,5},{6,7},{5,4},{7,6},{8,9},{10,11},{9,8... | collective-permute-start | bytes 196616 | tf_op jit(solution)/shard_map/ppermute | solution.py:109
  5.8 1.6 %collective-permute-start = (bf16[4,64,128]{2,1,0:T(8,128)(2,1)S(1)}, bf16[4,64,128]{2,1,0:T(8,128)(2,1)S(1)}, u32[]{:S(2)}, u32[]{:S(2)}) collective-permute-start(bf16[4,64,128]{2,1,0:T(8,128)(2,1)S(1)} %edges.1), channel_id=1, source_target_pairs={{1,2},{2,1},{5,6},{6,5},{9,10},{10,9},{13,14},{14,13},{17,18},{18,... | collective-permute-start | bytes 196616 | tf_op jit(solution)/shard_map/ppermute | solution.py:108
  7.4 6.9 %collective-permute-start.3 = (bf16[12,64,128]{2,1,0:T(8,128)(2,1)S(1)}, bf16[12,64,128]{2,1,0:T(8,128)(2,1)S(1)}, u32[]{:S(2)}, u32[]{:S(2)}) collective-permute-start(bf16[12,64,128]{2,1,0:T(8,128)(2,1)S(1)} %pad_maximum_fusion), channel_id=1, source_target_pairs={{0,4},{8,12},{16,20},{24,28},{32,36},{40,44},{48,52},{56,60},{4,0}... | collective-permute-start | bytes 589832 | tf_op jit(solution)/shard_map/ppermute | solution.py:109
  11.2 0.7 collective-permute-start.2
  11.9 15.8 %copy-start.2 = (s32[4]{0:T(128)S(1)}, s32[4]{0:T(128)}, u32[]{:S(2)}) copy-start(s32[4]{0:T(128)} %list_ref.1) | copy-start | bytes 52
  11.9 15.9 %copy-start = (f32[64,2048]{1,0:T(8,128)S(1)}, f32[64,2048]{1,0:T(8,128)}, u32[]{:S(2)}) copy-start(f32[64,2048]{1,0:T(8,128)} %x_ref.5) | copy-start | bytes 1572868
  14.4 13.6 %collective-permute-start.5 = (bf16[36,64,128]{2,1,0:T(8,128)(2,1)S(1)}, bf16[36,64,128]{2,1,0:T(8,128)(2,1)S(1)}, u32[]{:S(2)}, u32[]{:S(2)}) collective-permute-start(bf16[36,64,128]{2,1,0:T(8,128)(2,1)S(1)} %constant_dynamic-update-slice_fusion.mid_ref), channel_id=1, source_target_pairs={{64,128},{192,256},{320,384},{128,64},{256,192},{384,320},{65,129}... | collective-permute-start | bytes 1769480 | tf_op jit(solution)/shard_map/ppermute | solution.py:108
  20.0 8.0 %collective-permute-start.4 = (bf16[36,64,128]{2,1,0:T(8,128)(2,1)S(1)}, bf16[36,64,128]{2,1,0:T(8,128)(2,1)S(1)}, u32[]{:S(2)}, u32[]{:S(2)}) collective-permute-start(bf16[36,64,128]{2,1,0:T(8,128)(2,1)S(1)} %constant_dynamic-update-slice_fusion.mid_ref), channel_id=1, source_target_pairs={{0,64},{128,192},{256,320},{384,448},{64,0},{192,128},{320,256},{4... | collective-permute-start | bytes 1769480 | tf_op jit(solution)/shard_map/ppermute | solution.py:109
  28.9 8.0 %collective-permute-start.7 = (bf16[4,64,128]{2,1,0:T(8,128)(2,1)S(1)}, bf16[4,64,128]{2,1,0:T(8,128)(2,1)S(1)}, u32[]{:S(2)}, u32[]{:S(2)}) collective-permute-start(bf16[4,64,128]{2,1,0:T(8,128)(2,1)S(1)} %get-tuple-element.17), channel_id=1, source_target_pairs={{0,1},{2,3},{1,0},{3,2},{4,5},{6,7},{5,4},{7,6},{8,9},{10,11},{9,8... | collective-permute-start | bytes 196616 | tf_op jit(solution)/shard_map/ppermute | solution.py:109
  34.5 0.7 collective-permute-start.6
  37.0 10.1 %collective-permute-start.8 = (bf16[12,64,128]{2,1,0:T(8,128)(2,1)S(1)}, bf16[12,64,128]{2,1,0:T(8,128)(2,1)S(1)}, u32[]{:S(2)}, u32[]{:S(2)}) collective-permute-start(bf16[12,64,128]{2,1,0:T(8,128)(2,1)S(1)} %get-tuple-element.20), channel_id=1, source_target_pairs={{4,8},{12,16},{20,24},{28,32},{36,40},{44,48},{52,56},{8,4},{16,12... | collective-permute-start | bytes 589832 | tf_op jit(solution)/shard_map/ppermute | solution.py:108
  37.6 13.8 %collective-permute-start.9 = (bf16[12,64,128]{2,1,0:T(8,128)(2,1)S(1)}, bf16[12,64,128]{2,1,0:T(8,128)(2,1)S(1)}, u32[]{:S(2)}, u32[]{:S(2)}) collective-permute-start(bf16[12,64,128]{2,1,0:T(8,128)(2,1)S(1)} %get-tuple-element.20), channel_id=1, source_target_pairs={{0,4},{8,12},{16,20},{24,28},{32,36},{40,44},{48,52},{56,60},{4,0}... | collective-permute-start | bytes 589832 | tf_op jit(solution)/shard_map/ppermute | solution.py:109
  51.5 12.7 %collective-permute-start.11 = (bf16[36,64,128]{2,1,0:T(8,128)(2,1)S(1)}, bf16[36,64,128]{2,1,0:T(8,128)(2,1)S(1)}, u32[]{:S(2)}, u32[]{:S(2)}) collective-permute-start(bf16[36,64,128]{2,1,0:T(8,128)(2,1)S(1)} %constant_dynamic-update-slice_fusion.8.mid_ref), channel_id=1, source_target_pairs={{64,128},{192,256},{320,384},{128,64},{256,192},{384,320},{65,129}... | collective-permute-start | bytes 1769480 | tf_op jit(solution)/shard_map/ppermute | solution.py:108
  56.7 7.6 %collective-permute-start.10 = (bf16[36,64,128]{2,1,0:T(8,128)(2,1)S(1)}, bf16[36,64,128]{2,1,0:T(8,128)(2,1)S(1)}, u32[]{:S(2)}, u32[]{:S(2)}) collective-permute-start(bf16[36,64,128]{2,1,0:T(8,128)(2,1)S(1)} %constant_dynamic-update-slice_fusion.8.mid_ref), channel_id=1, source_target_pairs={{0,64},{128,192},{256,320},{384,448},{64,0},{192,128},{320,256},{4... | collective-permute-start | bytes 1769480 | tf_op jit(solution)/shard_map/ppermute | solution.py:109

commit v9 on v8

--- a/solution.py
+++ b/solution.py
@@ -139,7 +139,7 @@
 
 def halo(own, edge):
     block = edge
-    for axis in ("tz", "ty"):
+    for axis in ("ty", "tz"):
         block = jnp.concatenate([block, *partners_along(block, axis)], axis=0)
     other, partner = partners_along(block, "tx")
     return near_pool(own, block), partner, other
@@ -163,7 +163,7 @@
     place = codes - blocks
     offset = place // listed
     index = jnp.zeros_like(codes)
-    for axis, step in (("tx", 9), ("ty", 3), ("tz", 1)):
+    for axis, step in (("tx", 9), ("tz", 1), ("ty", 3)):
         way = offset // step % 3
         even = lax.axis_index(axis) % 2 == 0
         last = jnp.where(even, 0, 2) if axis == "tx" else jnp.where(even, 2, 0)

time: 121 us -> 122 us (level)
    all_to_all x1, blocking collectives: 25.3 us -> 29.8 us  [sum_over_devices(): lax.all_to_all(jnp.broadcast_to(mine[None], (line, *shape)), 'ty', 0, 0)]
    all_to_all x1, blocking collectives: 17.1 us -> 13.2 us  [sum_over_devices(): parts = lax.all_to_all(parts.reshape(along * deep, *shape), PLANE, 0, 0)]
where the time goes in v9:
time: 122 us; the launch traced here: 121 us
  blocking collectives  52.4 us (43%)
  starting transfers between devices  43.7 us (36%)
  waiting for transfers between devices  12 us (10%)
  Pallas kernels  11.6 us (10%)
    ppermute x6, starting transfers between devices, partners_along(): return (other, lax.ppermute(block, axis, pairs(0)))  30.3 us
    all_to_all x1, blocking collectives, sum_over_devices(): lax.all_to_all(jnp.broadcast_to(mine[None], (line, *shape)), 'ty', 0, 0)  29.8 us
    ppermute x6, starting transfers between devices, partners_along(): other = lax.ppermute(block, axis, pairs(1))  13.5 us
    all_to_all x1, blocking collectives, sum_over_devices(): parts = lax.all_to_all(parts.reshape(along * deep, *shape), PLANE, 0, 0)  13.2 us
    all_to_all x1, blocking collectives, sum_over_devices(): lax.all_to_all(jnp.broadcast_to(mine[None], (along, *shape)), 'tx', 0, 0)  9.31 us
    ppermute x6, waiting for transfers between devices, partners_along(): return (other, lax.ppermute(block, axis, pairs(0)))  8.78 us
    ppermute x6, waiting for transfers between devices, partners_along(): other = lax.ppermute(block, axis, pairs(1))  3.23 us
    pallas_call x1, Pallas kernels, finish(): pl.pallas_call(functools.partial(finish_kernel, root_scale), out_shape=(j...  2.95 us
  transfers between devices with their start and end apart: 12, of which 5 were waited for; matrix products, arithmetic and copies ran while one was open for 0% of the time, Pallas kernels for 4%

profile of v9, /device:TPU:1, one launch (start us, length us, event | category | flops | bytes accessed | tf_op | source)
XLA Modules:
  0.0 121.4 jit_solution(3960655929322074213)
XLA Ops:
  0.6 0.0 copy-start.1
  0.6 1.1 edges.1
  1.7 4.4 %collective-permute-start.1 = (bf16[4,64,128]{2,1,0:T(8,128)(2,1)S(1)}, bf16[4,64,128]{2,1,0:T(8,128)(2,1)S(1)}, u32[]{:S(2)}, u32[]{:S(2)}) collective-permute-start(bf16[4,64,128]{2,1,0:T(8,128)(2,1)S(1)} %edges.1), channel_id=1, source_target_pairs={{0,4},{8,12},{16,20},{24,28},{32,36},{40,44},{48,52},{56,60},{4,0}... | collective-permute-start | bytes 196616 | tf_op jit(solution)/shard_map/ppermute | solution.py:109
  6.1 0.7 collective-permute-start
  6.8 1.0 collective-permute-done.1
  7.8 0.0 collective-permute-done
  7.8 3.2 %collective-permute-start.3 = (bf16[12,64,128]{2,1,0:T(8,128)(2,1)S(1)}, bf16[12,64,128]{2,1,0:T(8,128)(2,1)S(1)}, u32[]{:S(2)}, u32[]{:S(2)}) collective-permute-start(bf16[12,64,128]{2,1,0:T(8,128)(2,1)S(1)} %pad_maximum_fusion), channel_id=1, source_target_pairs={{0,1},{2,3},{1,0},{3,2},{4,5},{6,7},{5,4},{7,6},{8,9},{10,11},{9,8... | collective-permute-start | bytes 589832 | tf_op jit(solution)/shard_map/ppermute | solution.py:109
  11.0 0.7 collective-permute-start.2
  11.7 0.0 copy-start.2
  11.7 0.0 copy-start
  11.7 0.0 collective-permute-done.2
  11.8 2.6 %collective-permute-done.3 = bf16[12,64,128]{2,1,0:T(8,128)(2,1)S(1)} collective-permute-done((bf16[12,64,128]{2,1,0:T(8,128)(2,1)S(1)}, bf16[12,64,128]{2,1,0:T(8,128)(2,1)S(1)}, u32[]{:S(2)}, u32[]{:S(2)}) %collective-permute-start.3) | collective-permute-done | bytes 196640 | tf_op jit(solution)/shard_map/ppermute | solution.py:109
  14.4 5.6 %collective-permute-start.5 = (bf16[36,64,128]{2,1,0:T(8,128)(2,1)S(1)}, bf16[36,64,128]{2,1,0:T(8,128)(2,1)S(1)}, u32[]{:S(2)}, u32[]{:S(2)}) collective-permute-start(bf16[36,64,128]{2,1,0:T(8,128)(2,1)S(1)} %constant_dynamic-update-slice_fusion.mid_ref), channel_id=1, source_target_pairs={{64,128},{192,256},{320,384},{128,64},{256,192},{384,320},{65,129}... | collective-permute-start | bytes 1769480 | tf_op jit(solution)/shard_map/ppermute | solution.py:108
  20.0 5.0 %collective-permute-start.4 = (bf16[36,64,128]{2,1,0:T(8,128)(2,1)S(1)}, bf16[36,64,128]{2,1,0:T(8,128)(2,1)S(1)}, u32[]{:S(2)}, u32[]{:S(2)}) collective-permute-start(bf16[36,64,128]{2,1,0:T(8,128)(2,1)S(1)} %constant_dynamic-update-slice_fusion.mid_ref), channel_id=1, source_target_pairs={{0,64},{128,192},{256,320},{384,448},{64,0},{192,128},{320,256},{4... | collective-permute-start | bytes 1769480 | tf_op jit(solution)/shard_map/ppermute | solution.py:109
  25.1 0.0 copy-done.1
  25.1 0.1 copy.11
  25.2 0.1 reshape.22
  25.3 2.4 %hold_weights.1 = (bf16[16,768,128]{2,1,0:T(8,128)(2,1)S(1)}, f32[16,8,128]{2,1,0:T(8,128)S(1)}) custom-call(bf16[16,768,128]{2,1,0:T(8,128)(2,1)} %bitcast.13), custom_call_target="tpu_custom_call" | custom-call | bytes 6291456 | tf_op jit(solution)/shard_map/hold_weights/pallas_call | solution.py:84
  27.7 0.0 copy-done.2
  27.7 0.1 pad_add_fusion.table_ref
  27.8 0.0 copy-done
  27.9 0.2 near_pool.2._
  28.0 0.0 collective-permute-done.5.other_ref
  28.0 0.0 collective-permute-done.4.partner_ref
  28.1 0.9 listed_rows.1
  28.9 6.8 %collective-permute-start.7 = (bf16[4,64,128]{2,1,0:T(8,128)(2,1)S(1)}, bf16[4,64,128]{2,1,0:T(8,128)(2,1)S(1)}, u32[]{:S(2)}, u32[]{:S(2)}) collective-permute-start(bf16[4,64,128]{2,1,0:T(8,128)(2,1)S(1)} %get-tuple-element.17), channel_id=1, source_target_pairs={{0,4},{8,12},{16,20},{24,28},{32,36},{40,44},{48,52},{56,60},{4,0}... | collective-permute-start | bytes 196616 | tf_op jit(solution)/shard_map/ppermute | solution.py:109
  35.7 0.7 collective-permute-start.6
  36.4 0.0 collective-permute-done.6
  36.5 0.9 collective-permute-done.7
  37.4 0.7 collective-permute-start.8
  38.1 9.0 %collective-permute-start.9 = (bf16[12,64,128]{2,1,0:T(8,128)(2,1)S(1)}, bf16[12,64,128]{2,1,0:T(8,128)(2,1)S(1)}, u32[]{:S(2)}, u32[]{:S(2)}) collective-permute-start(bf16[12,64,128]{2,1,0:T(8,128)(2,1)S(1)} %get-tuple-element.20), channel_id=1, source_target_pairs={{0,1},{2,3},{1,0},{3,2},{4,5},{6,7},{5,4},{7,6},{8,9},{10,11},{9,8... | collective-permute-start | bytes 589832 | tf_op jit(solution)/shard_map/ppermute | solution.py:109
  47.1 0.0 collective-permute-done.8
  47.1 4.3 %collective-permute-done.9 = bf16[12,64,128]{2,1,0:T(8,128)(2,1)S(1)} collective-permute-done((bf16[12,64,128]{2,1,0:T(8,128)(2,1)S(1)}, bf16[12,64,128]{2,1,0:T(8,128)(2,1)S(1)}, u32[]{:S(2)}, u32[]{:S(2)}) %collective-permute-start.9) | collective-permute-done | bytes 196640 | tf_op jit(solution)/shard_map/ppermute | solution.py:109
  51.5 5.2 %collective-permute-start.11 = (bf16[36,64,128]{2,1,0:T(8,128)(2,1)S(1)}, bf16[36,64,128]{2,1,0:T(8,128)(2,1)S(1)}, u32[]{:S(2)}, u32[]{:S(2)}) collective-permute-start(bf16[36,64,128]{2,1,0:T(8,128)(2,1)S(1)} %constant_dynamic-update-slice_fusion.8.mid_ref), channel_id=1, source_target_pairs={{64,128},{192,256},{320,384},{128,64},{256,192},{384,320},{65,129}... | collective-permute-start | bytes 1769480 | tf_op jit(solution)/shard_map/ppermute | solution.py:108
  56.7 1.9 %collective-permute-start.10 = (bf16[36,64,128]{2,1,0:T(8,128)(2,1)S(1)}, bf16[36,64,128]{2,1,0:T(8,128)(2,1)S(1)}, u32[]{:S(2)}, u32[]{:S(2)}) collective-permute-start(bf16[36,64,128]{2,1,0:T(8,128)(2,1)S(1)} %constant_dynamic-update-slice_fusion.8.mid_ref), channel_id=1, source_target_pairs={{0,64},{128,192},{256,320},{384,448},{64,0},{192,128},{320,256},{4... | collective-permute-start | bytes 1769480 | tf_op jit(solution)/shard_map/ppermute | solution.py:109
  58.6 1.3 %first_step.1 = (f32[16,64,128]{2,1,0:T(8,128)S(1)}, f32[16,64,128]{2,1,0:T(8,128)S(1)}, bf16[16,64,128]{2,1,0:T(8,128)(2,1)S(1)}) custom-call(s32[100]{0:T(128)S(1)} %pad_add_fusion.table_ref, f32[64,2048]{1,0:T(8,128)S(1)} %copy-done, bf16[16,768,128]{2,1,0:T(8,128)(2,1)S(1)} %get-tuple-element.11.w_ref, f32[16,8,128]{2,1,0:T(8,128)S(1)} %get-tuple-element.12.keep_ref, ...), custom_call_target="tpu_custom_call" | custom-call | flops 201326592 | bytes 3145728 | tf_op jit(solution)/shard_map/first_step/pallas_call | solution.py:234
  59.9 0.9 first_gram.1.gram_ref
  60.9 0.2 near_pool.3._
  61.0 3.2 %collective-permute-done.11.other_ref = bf16[36,64,128]{2,1,0:T(8,128)(2,1)S(1)} collective-permute-done((bf16[36,64,128]{2,1,0:T(8,128)(2,1)S(1)}, bf16[36,64,128]{2,1,0:T(8,128)(2,1)S(1)}, u32[]{:S(2)}, u32[]{:S(2)}) %collective-permute-start.11) | collective-permute-done | bytes 589856 | tf_op jit(solution)/shard_map/ppermute | solution.py:108
  64.2 0.0 collective-permute-done.10.partner_ref
  64.2 1.7 %second_step.1 = (f32[16,64,128]{2,1,0:T(8,128)S(1)}, f32[64,128]{1,0:T(8,128)S(1)}, bf16[124,64,128]{2,1,0:T(8,128)(2,1)S(1)}) custom-call(s32[100]{0:T(128)S(1)} %pad_add_fusion.table_ref, f32[16,64,128]{2,1,0:T(8,128)S(1)} %get-tuple-element.14.base_ref, bf16[16,768,128]{2,1,0:T(8,128)(2,1)S(1)} %get-tuple-element.11.w_ref, ...), custom_call_target="tpu_custom_call", output_to_operand_aliasing={{2}: (4, {})} | custom-call | tf_op jit(solution)/shard_map/second_step/pallas_call | solution.py:302
  66.0 13.2 %all_to_all.15 = f32[32,8,128]{2,1,0:T(8,128)S(1)} all-to-all(f32[32,8,128]{2,1,0:T(8,128)S(1)} %bitcast.14), channel_id=1, replica_groups=mesh['tx'=8,'ty'=16,'tz'=4] {'tx','tz'}, dimensions={0} | all-to-all | bytes 262144 | tf_op jit(solution)/shard_map/all_to_all | solution.py:327
  79.3 29.8 %all_to_all.16 = f32[16,8,128]{2,1,0:T(8,128)S(1)} all-to-all(f32[16,8,128]{2,1,0:T(8,128)S(1)} %broadcast_in_dim.33), channel_id=1, replica_groups=mesh['tx'=8,'ty'=16,'tz'=4] {'ty'}, dimensions={0} | all-to-all | bytes 131072 | tf_op jit(solution)/shard_map/all_to_all | solution.py:329
  109.2 9.3 %all_to_all.17 = f32[8,8,128]{2,1,0:T(8,128)S(1)} all-to-all(f32[8,8,128]{2,1,0:T(8,128)S(1)} %broadcast_in_dim.34), channel_id=1, replica_groups=mesh['tx'=8,'ty'=16,'tz'=4] {'tx'}, dimensions={0} | all-to-all | bytes 65536 | tf_op jit(solution)/shard_map/all_to_all | solution.py:331
  118.5 2.9 %finish.1 = (f32[64,2048]{1,0:T(8,128)}, f32[64,64]{1,0:T(8,128)}) custom-call(f32[64,128]{1,0:T(8,128)S(1)} %bitcast.11, f32[16,64,128]{2,1,0:T(8,128)S(1)} %get-tuple-element.19.mixed_ref), custom_call_target="tpu_custom_call" | custom-call | tf_op jit(solution)/shard_map/finish/pallas_call | solution.py:406
  (18 shorter events, 0.4 us)
Async XLA Ops:
  0.6 24.4 %copy-start.1 = (s32[16,6]{0,1:T(8,128)S(1)}, s32[16,6]{0,1:T(8,128)}, u32[]{:S(2)}) copy-start(s32[16,6]{0,1:T(8,128)} %param.6) | copy-start | bytes 1156
  1.7 6.0 %collective-permute-start.1 = (bf16[4,64,128]{2,1,0:T(8,128)(2,1)S(1)}, bf16[4,64,128]{2,1,0:T(8,128)(2,1)S(1)}, u32[]{:S(2)}, u32[]{:S(2)}) collective-permute-start(bf16[4,64,128]{2,1,0:T(8,128)(2,1)S(1)} %edges.1), channel_id=1, source_target_pairs={{0,4},{8,12},{16,20},{24,28},{32,36},{40,44},{48,52},{56,60},{4,0}... | collective-permute-start | bytes 196616 | tf_op jit(solution)/shard_map/ppermute | solution.py:109
  6.1 1.6 %collective-permute-start = (bf16[4,64,128]{2,1,0:T(8,128)(2,1)S(1)}, bf16[4,64,128]{2,1,0:T(8,128)(2,1)S(1)}, u32[]{:S(2)}, u32[]{:S(2)}) collective-permute-start(bf16[4,64,128]{2,1,0:T(8,128)(2,1)S(1)} %edges.1), channel_id=1, source_target_pairs={{4,8},{12,16},{20,24},{28,32},{36,40},{44,48},{52,56},{8,4},{16,12... | collective-permute-start | bytes 196616 | tf_op jit(solution)/shard_map/ppermute | solution.py:108
  7.8 6.6 %collective-permute-start.3 = (bf16[12,64,128]{2,1,0:T(8,128)(2,1)S(1)}, bf16[12,64,128]{2,1,0:T(8,128)(2,1)S(1)}, u32[]{:S(2)}, u32[]{:S(2)}) collective-permute-start(bf16[12,64,128]{2,1,0:T(8,128)(2,1)S(1)} %pad_maximum_fusion), channel_id=1, source_target_pairs={{0,1},{2,3},{1,0},{3,2},{4,5},{6,7},{5,4},{7,6},{8,9},{10,11},{9,8... | collective-permute-start | bytes 589832 | tf_op jit(solution)/shard_map/ppermute | solution.py:109
  11.0 0.7 collective-permute-start.2
  11.7 16.0 %copy-start.2 = (s32[4]{0:T(128)S(1)}, s32[4]{0:T(128)}, u32[]{:S(2)}) copy-start(s32[4]{0:T(128)} %list_ref.1) | copy-start | bytes 52
  11.7 16.1 %copy-start = (f32[64,2048]{1,0:T(8,128)S(1)}, f32[64,2048]{1,0:T(8,128)}, u32[]{:S(2)}) copy-start(f32[64,2048]{1,0:T(8,128)} %x_ref.5) | copy-start | bytes 1572868
  14.4 13.6 %collective-permute-start.5 = (bf16[36,64,128]{2,1,0:T(8,128)(2,1)S(1)}, bf16[36,64,128]{2,1,0:T(8,128)(2,1)S(1)}, u32[]{:S(2)}, u32[]{:S(2)}) collective-permute-start(bf16[36,64,128]{2,1,0:T(8,128)(2,1)S(1)} %constant_dynamic-update-slice_fusion.mid_ref), channel_id=1, source_target_pairs={{64,128},{192,256},{320,384},{128,64},{256,192},{384,320},{65,129}... | collective-permute-start | bytes 1769480 | tf_op jit(solution)/shard_map/ppermute | solution.py:108
  20.0 8.0 %collective-permute-start.4 = (bf16[36,64,128]{2,1,0:T(8,128)(2,1)S(1)}, bf16[36,64,128]{2,1,0:T(8,128)(2,1)S(1)}, u32[]{:S(2)}, u32[]{:S(2)}) collective-permute-start(bf16[36,64,128]{2,1,0:T(8,128)(2,1)S(1)} %constant_dynamic-update-slice_fusion.mid_ref), channel_id=1, source_target_pairs={{0,64},{128,192},{256,320},{384,448},{64,0},{192,128},{320,256},{4... | collective-permute-start | bytes 1769480 | tf_op jit(solution)/shard_map/ppermute | solution.py:109
  28.9 8.5 %collective-permute-start.7 = (bf16[4,64,128]{2,1,0:T(8,128)(2,1)S(1)}, bf16[4,64,128]{2,1,0:T(8,128)(2,1)S(1)}, u32[]{:S(2)}, u32[]{:S(2)}) collective-permute-start(bf16[4,64,128]{2,1,0:T(8,128)(2,1)S(1)} %get-tuple-element.17), channel_id=1, source_target_pairs={{0,4},{8,12},{16,20},{24,28},{32,36},{40,44},{48,52},{56,60},{4,0}... | collective-permute-start | bytes 196616 | tf_op jit(solution)/shard_map/ppermute | solution.py:109
  35.7 0.7 collective-permute-start.6
  37.4 9.7 %collective-permute-start.8 = (bf16[12,64,128]{2,1,0:T(8,128)(2,1)S(1)}, bf16[12,64,128]{2,1,0:T(8,128)(2,1)S(1)}, u32[]{:S(2)}, u32[]{:S(2)}) collective-permute-start(bf16[12,64,128]{2,1,0:T(8,128)(2,1)S(1)} %get-tuple-element.20), channel_id=1, source_target_pairs={{1,2},{2,1},{5,6},{6,5},{9,10},{10,9},{13,14},{14,13},{17,18},{18,... | collective-permute-start | bytes 589832 | tf_op jit(solution)/shard_map/ppermute | solution.py:108
  38.1 13.4 %collective-permute-start.9 = (bf16[12,64,128]{2,1,0:T(8,128)(2,1)S(1)}, bf16[12,64,128]{2,1,0:T(8,128)(2,1)S(1)}, u32[]{:S(2)}, u32[]{:S(2)}) collective-permute-start(bf16[12,64,128]{2,1,0:T(8,128)(2,1)S(1)} %get-tuple-element.20), channel_id=1, source_target_pairs={{0,1},{2,3},{1,0},{3,2},{4,5},{6,7},{5,4},{7,6},{8,9},{10,11},{9,8... | collective-permute-start | bytes 589832 | tf_op jit(solution)/shard_map/ppermute | solution.py:109
  51.5 12.7 %collective-permute-start.11 = (bf16[36,64,128]{2,1,0:T(8,128)(2,1)S(1)}, bf16[36,64,128]{2,1,0:T(8,128)(2,1)S(1)}, u32[]{:S(2)}, u32[]{:S(2)}) collective-permute-start(bf16[36,64,128]{2,1,0:T(8,128)(2,1)S(1)} %constant_dynamic-update-slice_fusion.8.mid_ref), channel_id=1, source_target_pairs={{64,128},{192,256},{320,384},{128,64},{256,192},{384,320},{65,129}... | collective-permute-start | bytes 1769480 | tf_op jit(solution)/shard_map/ppermute | solution.py:108
  56.7 7.6 %collective-permute-start.10 = (bf16[36,64,128]{2,1,0:T(8,128)(2,1)S(1)}, bf16[36,64,128]{2,1,0:T(8,128)(2,1)S(1)}, u32[]{:S(2)}, u32[]{:S(2)}) collective-permute-start(bf16[36,64,128]{2,1,0:T(8,128)(2,1)S(1)} %constant_dynamic-update-slice_fusion.8.mid_ref), channel_id=1, source_target_pairs={{0,64},{128,192},{256,320},{384,448},{64,0},{192,128},{320,256},{4... | collective-permute-start | bytes 1769480 | tf_op jit(solution)/shard_map/ppermute | solution.py:109

commit v10 on v8

--- a/solution.py
+++ b/solution.py
@@ -140,7 +140,9 @@
 def halo(own, edge):
     block = edge
     for axis in ("tz", "ty"):
-        block = jnp.concatenate([block, *partners_along(block, axis)], axis=0)
+        other, partner = partners_along(block, axis)
+        sides = (other, partner) if axis == "tz" else (partner, other)
+        block = jnp.concatenate([block, *sides], axis=0)
     other, partner = partners_along(block, "tx")
     return near_pool(own, block), partner, other
 
@@ -166,7 +168,7 @@
     for axis, step in (("tx", 9), ("ty", 3), ("tz", 1)):
         way = offset // step % 3
         even = lax.axis_index(axis) % 2 == 0
-        last = jnp.where(even, 0, 2) if axis == "tx" else jnp.where(even, 2, 0)
+        last = jnp.where(even, 0, 2) if axis != "tz" else jnp.where(even, 2, 0)
         index = index * 3 + jnp.where(way == 1, 0, jnp.where(way == last, 2, 1))
     return jnp.where(codes < blocks, codes, blocks + index * listed + place % listed)
 

time: 121 us -> 122 us (level)
  starting transfers between devices: 43.1 us -> 38.2 us
  blocking collectives: 51.7 us -> 55.7 us
  waiting for transfers between devices: 12.7 us -> 14.1 us
    ppermute x6, starting transfers between devices: 29.6 us -> 24.1 us  [partners_along(): return (other, lax.ppermute(block, axis, pairs(0)))]
    all_to_all x1, blocking collectives: 25.3 us -> 29.4 us  [sum_over_devices(): lax.all_to_all(jnp.broadcast_to(mine[None], (line, *shape)), 'ty', 0, 0)]
    ppermute x6, waiting for transfers between devices: 3.23 us -> 5.83 us  [partners_along(): other = lax.ppermute(block, axis, pairs(1))]
  transfers between devices with their start and end apart: 12 -> 12, of which waited for: 5 -> 6; matrix products, arithmetic and copies ran while one was open for 0% -> 0% of each run, Pallas kernels for 4% -> 4%
where the time goes in v10:
time: 122 us; the launch traced here: 121 us
  blocking collectives  55.7 us (46%)
  starting transfers between devices  38.2 us (31%)
  waiting for transfers between devices  14.1 us (12%)
  Pallas kernels  11.6 us (10%)
    all_to_all x1, blocking collectives, sum_over_devices(): lax.all_to_all(jnp.broadcast_to(mine[None], (line, *shape)), 'ty', 0, 0)  29.4 us
    ppermute x6, starting transfers between devices, partners_along(): return (other, lax.ppermute(block, axis, pairs(0)))  24.1 us
    all_to_all x1, blocking collectives, sum_over_devices(): parts = lax.all_to_all(parts.reshape(along * deep, *shape), PLANE, 0, 0)  16.9 us
    ppermute x6, starting transfers between devices, partners_along(): other = lax.ppermute(block, axis, pairs(1))  14.1 us
    all_to_all x1, blocking collectives, sum_over_devices(): lax.all_to_all(jnp.broadcast_to(mine[None], (along, *shape)), 'tx', 0, 0)  9.31 us
    ppermute x6, waiting for transfers between devices, partners_along(): return (other, lax.ppermute(block, axis, pairs(0)))  8.26 us
    ppermute x6, waiting for transfers between devices, partners_along(): other = lax.ppermute(block, axis, pairs(1))  5.83 us
    pallas_call x1, Pallas kernels, finish(): pl.pallas_call(functools.partial(finish_kernel, root_scale), out_shape=(j...  2.95 us
  transfers between devices with their start and end apart: 12, of which 6 were waited for; matrix products, arithmetic and copies ran while one was open for 0% of the time, Pallas kernels for 4%

profile of v10, /device:TPU:1, one launch (start us, length us, event | category | flops | bytes accessed | tf_op | source)
XLA Modules:
  0.0 121.2 jit_solution(829605373221086726)
XLA Ops:
  0.6 0.0 copy-start.1
  0.6 1.1 edges.1
  1.7 4.0 %collective-permute-start.1 = (bf16[4,64,128]{2,1,0:T(8,128)(2,1)S(1)}, bf16[4,64,128]{2,1,0:T(8,128)(2,1)S(1)}, u32[]{:S(2)}, u32[]{:S(2)}) collective-permute-start(bf16[4,64,128]{2,1,0:T(8,128)(2,1)S(1)} %edges.1), channel_id=1, source_target_pairs={{0,1},{2,3},{1,0},{3,2},{4,5},{6,7},{5,4},{7,6},{8,9},{10,11},{9,8... | collective-permute-start | bytes 196616 | tf_op jit(solution)/shard_map/ppermute | solution.py:109
  5.8 0.7 collective-permute-start
  6.5 1.0 collective-permute-done.1
  7.4 0.0 collective-permute-done
  7.4 0.7 collective-permute-start.3
  8.1 6.6 %collective-permute-start.2 = (bf16[12,64,128]{2,1,0:T(8,128)(2,1)S(1)}, bf16[12,64,128]{2,1,0:T(8,128)(2,1)S(1)}, u32[]{:S(2)}, u32[]{:S(2)}) collective-permute-start(bf16[12,64,128]{2,1,0:T(8,128)(2,1)S(1)} %pad_maximum_fusion), channel_id=1, source_target_pairs={{0,4},{8,12},{16,20},{24,28},{32,36},{40,44},{48,52},{56,60},{4,0}... | collective-permute-start | bytes 589832 | tf_op jit(solution)/shard_map/ppermute | solution.py:109
  14.7 0.0 copy-start.2
  14.8 0.0 copy-start
  14.8 3.0 %collective-permute-done.2 = bf16[12,64,128]{2,1,0:T(8,128)(2,1)S(1)} collective-permute-done((bf16[12,64,128]{2,1,0:T(8,128)(2,1)S(1)}, bf16[12,64,128]{2,1,0:T(8,128)(2,1)S(1)}, u32[]{:S(2)}, u32[]{:S(2)}) %collective-permute-start.2) | collective-permute-done | bytes 196640 | tf_op jit(solution)/shard_map/ppermute | solution.py:109
  17.8 0.0 collective-permute-done.3
  17.8 6.0 %collective-permute-start.5 = (bf16[36,64,128]{2,1,0:T(8,128)(2,1)S(1)}, bf16[36,64,128]{2,1,0:T(8,128)(2,1)S(1)}, u32[]{:S(2)}, u32[]{:S(2)}) collective-permute-start(bf16[36,64,128]{2,1,0:T(8,128)(2,1)S(1)} %constant_dynamic-update-slice_fusion.mid_ref), channel_id=1, source_target_pairs={{64,128},{192,256},{320,384},{128,64},{256,192},{384,320},{65,129}... | collective-permute-start | bytes 1769480 | tf_op jit(solution)/shard_map/ppermute | solution.py:108
  23.8 1.9 %collective-permute-start.4 = (bf16[36,64,128]{2,1,0:T(8,128)(2,1)S(1)}, bf16[36,64,128]{2,1,0:T(8,128)(2,1)S(1)}, u32[]{:S(2)}, u32[]{:S(2)}) collective-permute-start(bf16[36,64,128]{2,1,0:T(8,128)(2,1)S(1)} %constant_dynamic-update-slice_fusion.mid_ref), channel_id=1, source_target_pairs={{0,64},{128,192},{256,320},{384,448},{64,0},{192,128},{320,256},{4... | collective-permute-start | bytes 1769480 | tf_op jit(solution)/shard_map/ppermute | solution.py:109
  25.8 0.0 copy-done.1
  25.8 0.1 copy.11
  25.9 0.1 reshape.22
  26.0 2.4 %hold_weights.1 = (bf16[16,768,128]{2,1,0:T(8,128)(2,1)S(1)}, f32[16,8,128]{2,1,0:T(8,128)S(1)}) custom-call(bf16[16,768,128]{2,1,0:T(8,128)(2,1)} %bitcast.13), custom_call_target="tpu_custom_call" | custom-call | bytes 6291456 | tf_op jit(solution)/shard_map/hold_weights/pallas_call | solution.py:84
  28.5 0.0 copy-done.2
  28.5 0.1 pad_add_fusion.table_ref
  28.5 0.0 copy-done
  28.6 0.2 near_pool.2._
  28.8 2.6 %collective-permute-done.5.other_ref = bf16[36,64,128]{2,1,0:T(8,128)(2,1)S(1)} collective-permute-done((bf16[36,64,128]{2,1,0:T(8,128)(2,1)S(1)}, bf16[36,64,128]{2,1,0:T(8,128)(2,1)S(1)}, u32[]{:S(2)}, u32[]{:S(2)}) %collective-permute-start.5) | collective-permute-done | bytes 589856 | tf_op jit(solution)/shard_map/ppermute | solution.py:108
  31.4 0.0 collective-permute-done.4.partner_ref
  31.4 0.9 listed_rows.1
  32.2 6.0 %collective-permute-start.7 = (bf16[4,64,128]{2,1,0:T(8,128)(2,1)S(1)}, bf16[4,64,128]{2,1,0:T(8,128)(2,1)S(1)}, u32[]{:S(2)}, u32[]{:S(2)}) collective-permute-start(bf16[4,64,128]{2,1,0:T(8,128)(2,1)S(1)} %get-tuple-element.17), channel_id=1, source_target_pairs={{0,1},{2,3},{1,0},{3,2},{4,5},{6,7},{5,4},{7,6},{8,9},{10,11},{9,8... | collective-permute-start | bytes 196616 | tf_op jit(solution)/shard_map/ppermute | solution.py:109
  38.2 0.7 collective-permute-start.6
  38.9 0.0 collective-permute-done.6
  39.0 0.9 collective-permute-done.7
  39.9 3.6 %collective-permute-start.8 = (bf16[12,64,128]{2,1,0:T(8,128)(2,1)S(1)}, bf16[12,64,128]{2,1,0:T(8,128)(2,1)S(1)}, u32[]{:S(2)}, u32[]{:S(2)}) collective-permute-start(bf16[12,64,128]{2,1,0:T(8,128)(2,1)S(1)} %get-tuple-element.20), channel_id=1, source_target_pairs={{0,4},{8,12},{16,20},{24,28},{32,36},{40,44},{48,52},{56,60},{4,0}... | collective-permute-start | bytes 589832 | tf_op jit(solution)/shard_map/ppermute | solution.py:109
  43.5 0.7 collective-permute-start.9
  44.2 3.4 %collective-permute-done.8 = bf16[12,64,128]{2,1,0:T(8,128)(2,1)S(1)} collective-permute-done((bf16[12,64,128]{2,1,0:T(8,128)(2,1)S(1)}, bf16[12,64,128]{2,1,0:T(8,128)(2,1)S(1)}, u32[]{:S(2)}, u32[]{:S(2)}) %collective-permute-start.8) | collective-permute-done | bytes 196640 | tf_op jit(solution)/shard_map/ppermute | solution.py:109
  47.7 0.0 collective-permute-done.9
  47.7 5.5 %collective-permute-start.11 = (bf16[36,64,128]{2,1,0:T(8,128)(2,1)S(1)}, bf16[36,64,128]{2,1,0:T(8,128)(2,1)S(1)}, u32[]{:S(2)}, u32[]{:S(2)}) collective-permute-start(bf16[36,64,128]{2,1,0:T(8,128)(2,1)S(1)} %constant_dynamic-update-slice_fusion.8.mid_ref), channel_id=1, source_target_pairs={{64,128},{192,256},{320,384},{128,64},{256,192},{384,320},{65,129}... | collective-permute-start | bytes 1769480 | tf_op jit(solution)/shard_map/ppermute | solution.py:108
  53.2 1.9 %collective-permute-start.10 = (bf16[36,64,128]{2,1,0:T(8,128)(2,1)S(1)}, bf16[36,64,128]{2,1,0:T(8,128)(2,1)S(1)}, u32[]{:S(2)}, u32[]{:S(2)}) collective-permute-start(bf16[36,64,128]{2,1,0:T(8,128)(2,1)S(1)} %constant_dynamic-update-slice_fusion.8.mid_ref), channel_id=1, source_target_pairs={{0,64},{128,192},{256,320},{384,448},{64,0},{192,128},{320,256},{4... | collective-permute-start | bytes 1769480 | tf_op jit(solution)/shard_map/ppermute | solution.py:109
  55.1 1.3 %first_step.1 = (f32[16,64,128]{2,1,0:T(8,128)S(1)}, f32[16,64,128]{2,1,0:T(8,128)S(1)}, bf16[16,64,128]{2,1,0:T(8,128)(2,1)S(1)}) custom-call(s32[100]{0:T(128)S(1)} %pad_add_fusion.table_ref, f32[64,2048]{1,0:T(8,128)S(1)} %copy-done, bf16[16,768,128]{2,1,0:T(8,128)(2,1)S(1)} %get-tuple-element.11.w_ref, f32[16,8,128]{2,1,0:T(8,128)S(1)} %get-tuple-element.12.keep_ref, ...), custom_call_target="tpu_custom_call" | custom-call | flops 201326592 | bytes 3145728 | tf_op jit(solution)/shard_map/first_step/pallas_call | solution.py:236
  56.4 0.9 first_gram.1.gram_ref
  57.4 0.2 near_pool.3._
  57.5 3.2 %collective-permute-done.11.other_ref = bf16[36,64,128]{2,1,0:T(8,128)(2,1)S(1)} collective-permute-done((bf16[36,64,128]{2,1,0:T(8,128)(2,1)S(1)}, bf16[36,64,128]{2,1,0:T(8,128)(2,1)S(1)}, u32[]{:S(2)}, u32[]{:S(2)}) %collective-permute-start.11) | collective-permute-done | bytes 589856 | tf_op jit(solution)/shard_map/ppermute | solution.py:108
  60.7 0.0 collective-permute-done.10.partner_ref
  60.7 1.7 %second_step.1 = (f32[16,64,128]{2,1,0:T(8,128)S(1)}, f32[64,128]{1,0:T(8,128)S(1)}, bf16[124,64,128]{2,1,0:T(8,128)(2,1)S(1)}) custom-call(s32[100]{0:T(128)S(1)} %pad_add_fusion.table_ref, f32[16,64,128]{2,1,0:T(8,128)S(1)} %get-tuple-element.14.base_ref, bf16[16,768,128]{2,1,0:T(8,128)(2,1)S(1)} %get-tuple-element.11.w_ref, ...), custom_call_target="tpu_custom_call", output_to_operand_aliasing={{2}: (4, {})} | custom-call | tf_op jit(solution)/shard_map/second_step/pallas_call | solution.py:304
  62.5 16.9 %all_to_all.15 = f32[32,8,128]{2,1,0:T(8,128)S(1)} all-to-all(f32[32,8,128]{2,1,0:T(8,128)S(1)} %bitcast.14), channel_id=1, replica_groups=mesh['tx'=8,'ty'=16,'tz'=4] {'tx','tz'}, dimensions={0} | all-to-all | bytes 262144 | tf_op jit(solution)/shard_map/all_to_all | solution.py:329
  79.5 29.4 %all_to_all.16 = f32[16,8,128]{2,1,0:T(8,128)S(1)} all-to-all(f32[16,8,128]{2,1,0:T(8,128)S(1)} %broadcast_in_dim.33), channel_id=1, replica_groups=mesh['tx'=8,'ty'=16,'tz'=4] {'ty'}, dimensions={0} | all-to-all | bytes 131072 | tf_op jit(solution)/shard_map/all_to_all | solution.py:331
  109.0 9.3 %all_to_all.17 = f32[8,8,128]{2,1,0:T(8,128)S(1)} all-to-all(f32[8,8,128]{2,1,0:T(8,128)S(1)} %broadcast_in_dim.34), channel_id=1, replica_groups=mesh['tx'=8,'ty'=16,'tz'=4] {'tx'}, dimensions={0} | all-to-all | bytes 65536 | tf_op jit(solution)/shard_map/all_to_all | solution.py:333
  118.3 2.9 %finish.1 = (f32[64,2048]{1,0:T(8,128)}, f32[64,64]{1,0:T(8,128)}) custom-call(f32[64,128]{1,0:T(8,128)S(1)} %bitcast.11, f32[16,64,128]{2,1,0:T(8,128)S(1)} %get-tuple-element.19.mixed_ref), custom_call_target="tpu_custom_call" | custom-call | tf_op jit(solution)/shard_map/finish/pallas_call | solution.py:408
  (18 shorter events, 0.4 us)
Async XLA Ops:
  0.6 25.2 %copy-start.1 = (s32[16,6]{0,1:T(8,128)S(1)}, s32[16,6]{0,1:T(8,128)}, u32[]{:S(2)}) copy-start(s32[16,6]{0,1:T(8,128)} %param.6) | copy-start | bytes 1156
  1.7 5.7 %collective-permute-start.1 = (bf16[4,64,128]{2,1,0:T(8,128)(2,1)S(1)}, bf16[4,64,128]{2,1,0:T(8,128)(2,1)S(1)}, u32[]{:S(2)}, u32[]{:S(2)}) collective-permute-start(bf16[4,64,128]{2,1,0:T(8,128)(2,1)S(1)} %edges.1), channel_id=1, source_target_pairs={{0,1},{2,3},{1,0},{3,2},{4,5},{6,7},{5,4},{7,6},{8,9},{10,11},{9,8... | collective-permute-start | bytes 196616 | tf_op jit(solution)/shard_map/ppermute | solution.py:109
  5.8 1.6 %collective-permute-start = (bf16[4,64,128]{2,1,0:T(8,128)(2,1)S(1)}, bf16[4,64,128]{2,1,0:T(8,128)(2,1)S(1)}, u32[]{:S(2)}, u32[]{:S(2)}) collective-permute-start(bf16[4,64,128]{2,1,0:T(8,128)(2,1)S(1)} %edges.1), channel_id=1, source_target_pairs={{1,2},{2,1},{5,6},{6,5},{9,10},{10,9},{13,14},{14,13},{17,18},{18,... | collective-permute-start | bytes 196616 | tf_op jit(solution)/shard_map/ppermute | solution.py:108
  7.4 10.3 %collective-permute-start.3 = (bf16[12,64,128]{2,1,0:T(8,128)(2,1)S(1)}, bf16[12,64,128]{2,1,0:T(8,128)(2,1)S(1)}, u32[]{:S(2)}, u32[]{:S(2)}) collective-permute-start(bf16[12,64,128]{2,1,0:T(8,128)(2,1)S(1)} %pad_maximum_fusion), channel_id=1, source_target_pairs={{4,8},{12,16},{20,24},{28,32},{36,40},{44,48},{52,56},{8,4},{16,12... | collective-permute-start | bytes 589832 | tf_op jit(solution)/shard_map/ppermute | solution.py:108
  8.1 9.6 %collective-permute-start.2 = (bf16[12,64,128]{2,1,0:T(8,128)(2,1)S(1)}, bf16[12,64,128]{2,1,0:T(8,128)(2,1)S(1)}, u32[]{:S(2)}, u32[]{:S(2)}) collective-permute-start(bf16[12,64,128]{2,1,0:T(8,128)(2,1)S(1)} %pad_maximum_fusion), channel_id=1, source_target_pairs={{0,4},{8,12},{16,20},{24,28},{32,36},{40,44},{48,52},{56,60},{4,0}... | collective-permute-start | bytes 589832 | tf_op jit(solution)/shard_map/ppermute | solution.py:109
  14.7 13.7 %copy-start.2 = (s32[4]{0:T(128)S(1)}, s32[4]{0:T(128)}, u32[]{:S(2)}) copy-start(s32[4]{0:T(128)} %list_ref.1) | copy-start | bytes 52
  14.8 13.8 %copy-start = (f32[64,2048]{1,0:T(8,128)S(1)}, f32[64,2048]{1,0:T(8,128)}, u32[]{:S(2)}) copy-start(f32[64,2048]{1,0:T(8,128)} %x_ref.5) | copy-start | bytes 1572868
  17.8 13.5 %collective-permute-start.5 = (bf16[36,64,128]{2,1,0:T(8,128)(2,1)S(1)}, bf16[36,64,128]{2,1,0:T(8,128)(2,1)S(1)}, u32[]{:S(2)}, u32[]{:S(2)}) collective-permute-start(bf16[36,64,128]{2,1,0:T(8,128)(2,1)S(1)} %constant_dynamic-update-slice_fusion.mid_ref), channel_id=1, source_target_pairs={{64,128},{192,256},{320,384},{128,64},{256,192},{384,320},{65,129}... | collective-permute-start | bytes 1769480 | tf_op jit(solution)/shard_map/ppermute | solution.py:108
  23.8 7.6 %collective-permute-start.4 = (bf16[36,64,128]{2,1,0:T(8,128)(2,1)S(1)}, bf16[36,64,128]{2,1,0:T(8,128)(2,1)S(1)}, u32[]{:S(2)}, u32[]{:S(2)}) collective-permute-start(bf16[36,64,128]{2,1,0:T(8,128)(2,1)S(1)} %constant_dynamic-update-slice_fusion.mid_ref), channel_id=1, source_target_pairs={{0,64},{128,192},{256,320},{384,448},{64,0},{192,128},{320,256},{4... | collective-permute-start | bytes 1769480 | tf_op jit(solution)/shard_map/ppermute | solution.py:109
  32.2 7.6 %collective-permute-start.7 = (bf16[4,64,128]{2,1,0:T(8,128)(2,1)S(1)}, bf16[4,64,128]{2,1,0:T(8,128)(2,1)S(1)}, u32[]{:S(2)}, u32[]{:S(2)}) collective-permute-start(bf16[4,64,128]{2,1,0:T(8,128)(2,1)S(1)} %get-tuple-element.17), channel_id=1, source_target_pairs={{0,1},{2,3},{1,0},{3,2},{4,5},{6,7},{5,4},{7,6},{8,9},{10,11},{9,8... | collective-permute-start | bytes 196616 | tf_op jit(solution)/shard_map/ppermute | solution.py:109
  38.2 0.7 collective-permute-start.6
  39.9 7.8 %collective-permute-start.8 = (bf16[12,64,128]{2,1,0:T(8,128)(2,1)S(1)}, bf16[12,64,128]{2,1,0:T(8,128)(2,1)S(1)}, u32[]{:S(2)}, u32[]{:S(2)}) collective-permute-start(bf16[12,64,128]{2,1,0:T(8,128)(2,1)S(1)} %get-tuple-element.20), channel_id=1, source_target_pairs={{0,4},{8,12},{16,20},{24,28},{32,36},{40,44},{48,52},{56,60},{4,0}... | collective-permute-start | bytes 589832 | tf_op jit(solution)/shard_map/ppermute | solution.py:109
  43.5 4.1 %collective-permute-start.9 = (bf16[12,64,128]{2,1,0:T(8,128)(2,1)S(1)}, bf16[12,64,128]{2,1,0:T(8,128)(2,1)S(1)}, u32[]{:S(2)}, u32[]{:S(2)}) collective-permute-start(bf16[12,64,128]{2,1,0:T(8,128)(2,1)S(1)} %get-tuple-element.20), channel_id=1, source_target_pairs={{4,8},{12,16},{20,24},{28,32},{36,40},{44,48},{52,56},{8,4},{16,12... | collective-permute-start | bytes 589832 | tf_op jit(solution)/shard_map/ppermute | solution.py:108
  47.7 13.0 %collective-permute-start.11 = (bf16[36,64,128]{2,1,0:T(8,128)(2,1)S(1)}, bf16[36,64,128]{2,1,0:T(8,128)(2,1)S(1)}, u32[]{:S(2)}, u32[]{:S(2)}) collective-permute-start(bf16[36,64,128]{2,1,0:T(8,128)(2,1)S(1)} %constant_dynamic-update-slice_fusion.8.mid_ref), channel_id=1, source_target_pairs={{64,128},{192,256},{320,384},{128,64},{256,192},{384,320},{65,129}... | collective-permute-start | bytes 1769480 | tf_op jit(solution)/shard_map/ppermute | solution.py:108
  53.2 7.6 %collective-permute-start.10 = (bf16[36,64,128]{2,1,0:T(8,128)(2,1)S(1)}, bf16[36,64,128]{2,1,0:T(8,128)(2,1)S(1)}, u32[]{:S(2)}, u32[]{:S(2)}) collective-permute-start(bf16[36,64,128]{2,1,0:T(8,128)(2,1)S(1)} %constant_dynamic-update-slice_fusion.8.mid_ref), channel_id=1, source_target_pairs={{0,64},{128,192},{256,320},{384,448},{64,0},{192,128},{320,256},{4... | collective-permute-start | bytes 1769480 | tf_op jit(solution)/shard_map/ppermute | solution.py:109
